TPU v7x, 512 devices: a whole 4x8x8 slice. The times are simulated.
512 devices in a mesh: ctx: 64 (over x, y, core), head: 8 (over z).
Axes of the slice: x: 4, y: 8, z: 8, core: 2. Of those that a mesh axis runs over, the one named last changes fastest.
Arguments:
- queries: bfloat16 [98304, 4096], P(('ctx', 'head')), may hold values from -8 to 8
- keys: bfloat16 [98304, 1024], P(('ctx', 'head')), may hold values from -4 to 4
- values: bfloat16 [98304, 1024], P(('ctx', 'head')), may hold values from -6 to 6
- doc_start: int32 [256], replicated, may hold values from 0 to 768, as said below
- doc_blocks: int32 [256], replicated, may hold values from 0 to 12, as said below
- doc_rank: int32 [256], replicated, may hold values from 0 to 63, as said below
- doc_slot: int32 [256], replicated, may hold values from 0 to 12, as said below
Outputs:
- attended: bfloat16 [98304, 4096], P(('ctx', 'head'))
Inputs may be any that keep to these rules, and one draw needn't show every extreme that they name: Entries are listed in packing order: doc_start is the sum of doc_blocks over the earlier entries, so the entries cover the 98304 tokens block by block. `doc_blocks`: an entry may hold 0 blocks. `doc_rank`: each ctx rank is named by exactly 4 entries. The entries that name one rank cover its 12 blocks without gaps or repeats; doc_slot is the first block of each.
All inputs are finite; a program needn't handle non-finite values.
Results may differ from a plain program's by a relative error of at most 0.0036.
Values may be sent and summed in bfloat16 or wider, within the bound.
No kernel may reach another device: no remote copies, remote signals or barrier semaphores. Data moves between devices by JAX's collectives and lax.ppermute only.
A program may use at most 64 MiB of HBM per device.

v0:
```python
import math

import jax
import jax.numpy as jnp
from jax import lax
from jax.sharding import PartitionSpec as P

HEAD_WIDTH = 128
BLOCK = 128


def locate(owner, local_rows, doc_start, doc_blocks, doc_rank, doc_slot):
    block_ids = local_rows // BLOCK
    matches = (
        (doc_rank[None, :] == owner[:, None])
        & (doc_slot[None, :] <= block_ids[:, None])
        & (block_ids[:, None] < (doc_slot + doc_blocks)[None, :])
    ).astype(jnp.int32)
    entry_list = jnp.arange(doc_start.shape[0], dtype=jnp.int32)
    entry_ids = jnp.sum(matches * entry_list[None, :], axis=1)
    offset_rows = jnp.sum(matches * (doc_start - doc_slot)[None, :], axis=1) * BLOCK
    slot_start = jnp.sum(matches * doc_slot[None, :], axis=1)
    return (entry_ids, offset_rows, slot_start)


def by_peer(array, ctx_count):
    return array.reshape(array.shape[0] // ctx_count, ctx_count, array.shape[1])


def finish(totals, weighted):
    return (weighted / jnp.transpose(totals, (2, 0, 1))[..., None]).astype(jnp.bfloat16)


def on_device(queries, keys, values, doc_start, doc_blocks, doc_rank, doc_slot):
    ctx_count = lax.axis_size("ctx")
    head_count = lax.axis_size("head")
    rank_index = lax.axis_index("ctx")
    rows_per_rank = queries.shape[0] * head_count
    per_peer = rows_per_rank // ctx_count
    scaling = 1.0 / math.sqrt(HEAD_WIDTH)
    lanes = (
        lax.all_to_all(queries, "head", split_axis=1, concat_axis=0, tiled=True),
        lax.all_to_all(keys, "head", split_axis=1, concat_axis=0, tiled=True),
        lax.all_to_all(values, "head", split_axis=1, concat_axis=0, tiled=True),
    )
    handed = (
        lax.all_to_all(
            by_peer(lanes[0], ctx_count), "ctx", split_axis=1, concat_axis=1, tiled=True
        ),
        lax.all_to_all(
            by_peer(lanes[1], ctx_count), "ctx", split_axis=1, concat_axis=1, tiled=True
        ),
        lax.all_to_all(
            by_peer(lanes[2], ctx_count), "ctx", split_axis=1, concat_axis=1, tiled=True
        ),
    )
    flat_slots = jnp.arange(rows_per_rank, dtype=jnp.int32)
    owner = flat_slots % ctx_count
    local_new = flat_slots // ctx_count * ctx_count + rank_index
    unused_entries, offset_rows, unused_slots = locate(
        owner, local_new, doc_start, doc_blocks, doc_rank, doc_slot
    )
    anchor_point = local_new + offset_rows
    picked = anchor_point % rows_per_rank // ctx_count * ctx_count + anchor_point // rows_per_rank
    moved = [
        jnp.take(array.reshape(rows_per_rank, array.shape[2]), picked, axis=0).reshape(
            per_peer, ctx_count, array.shape[2]
        )
        for array in handed
    ]
    placed = (
        lax.all_to_all(moved[0], "ctx", split_axis=1, concat_axis=1, tiled=True),
        lax.all_to_all(moved[1], "ctx", split_axis=1, concat_axis=1, tiled=True),
        lax.all_to_all(moved[2], "ctx", split_axis=1, concat_axis=1, tiled=True),
    )
    query_new = placed[0].reshape(rows_per_rank, placed[0].shape[2])
    key_new = placed[1].reshape(rows_per_rank, placed[1].shape[2])
    value_new = placed[2].reshape(rows_per_rank, placed[2].shape[2])
    row_ids = jnp.arange(rows_per_rank, dtype=jnp.int32)
    entry_rows, unused_offsets, slot_rows = locate(
        jnp.full((rows_per_rank,), rank_index, jnp.int32),
        row_ids,
        doc_start,
        doc_blocks,
        doc_rank,
        doc_slot,
    )
    key_heads = key_new.shape[1] // HEAD_WIDTH
    repeat_factor = query_new.shape[1] // HEAD_WIDTH // key_heads
    query_heads = query_new.reshape(rows_per_rank, key_heads, repeat_factor, HEAD_WIDTH)
    key_matrix = key_new.reshape(rows_per_rank, key_heads, HEAD_WIDTH)
    value_matrix = value_new.reshape(rows_per_rank, key_heads, HEAD_WIDTH)
    block_list = jnp.arange(rows_per_rank // BLOCK, dtype=jnp.int32)

    def whole_block(block_index):
        first_row = block_index * BLOCK
        query_tile = lax.dynamic_slice_in_dim(query_heads, first_row, BLOCK, 0)
        scores = (
            jnp.einsum("pgrd,qgd->grpq", query_tile, key_matrix, preferred_element_type=jnp.float32)
            * scaling
        )
        tile_rows = first_row + jnp.arange(BLOCK, dtype=jnp.int32)
        tile_entries = lax.dynamic_slice_in_dim(entry_rows, first_row, BLOCK, 0)
        allowed = (tile_entries[:, None] == entry_rows[None, :]) & (
            row_ids[None, :] <= tile_rows[:, None]
        )
        row_top = jnp.max(jnp.where(allowed, scores, -jnp.inf), axis=-1, keepdims=True)
        weights = jnp.where(allowed, jnp.exp(scores - row_top), 0.0)
        totals = jnp.sum(weights, axis=-1)
        weighted = jnp.einsum(
            "grpq,qgd->pgrd",
            weights.astype(jnp.bfloat16),
            value_matrix,
            preferred_element_type=jnp.float32,
        )
        return finish(totals, weighted)

    outputs = lax.map(whole_block, block_list)
    attended = outputs.reshape(rows_per_rank, key_heads * repeat_factor * HEAD_WIDTH)
    return lax.all_to_all(attended, "head", split_axis=0, concat_axis=1, tiled=True)


def solution(mesh):
    return jax.shard_map(
        on_device,
        mesh=mesh,
        in_specs=(
            P(("ctx", "head"), None),
            P(("ctx", "head"), None),
            P(("ctx", "head"), None),
            P(),
            P(),
            P(),
            P(),
        ),
        out_specs=P(("ctx", "head"), None),
        check_vma=False,
    )
```

profile of v0, /device:TPU:1, one launch (start us, length us, event | category | flops | bytes accessed | tf_op | source)
XLA Modules:
  0.0 379.0 jit_solution(9094983809029167196)
XLA Ops:
  1.8 10.9 %all-to-all-start.3 = ((bf16[192,8,128]{2,0,1:T(8,128)(2,1)}), bf16[192,8,128]{2,0,1:T(8,128)(2,1)S(1)}, u32[]{:S(2)}, u32[]{:S(2)}) async-start(bf16[192,8,128]{2,0,1:T(8,128)(2,1)} %copy_bitcast_fusion.4), calls=%async_computation.3 | async-start | bytes 786432 | tf_op jit(solution)/shard_map/all_to_all | solution.py:43
  13.5 13.4 %all-to-all-done.3 = bf16[192,8,128]{2,0,1:T(8,128)(2,1)S(1)} async-done(((bf16[192,8,128]{2,0,1:T(8,128)(2,1)}), bf16[192,8,128]{2,0,1:T(8,128)(2,1)S(1)}, u32[]{:S(2)}, u32[]{:S(2)}) %all-to-all-start.3) | async-done | bytes 393248 | tf_op jit(solution)/shard_map/all_to_all | solution.py:43
  26.9 3.5 all-to-all-start.6
  31.3 11.7 %all-to-all-done.6 = bf16[192,8,128]{2,0,1:T(8,128)(2,1)S(1)} async-done(((bf16[192,8,128]{2,0,1:T(8,128)(2,1)}), bf16[192,8,128]{2,0,1:T(8,128)(2,1)S(1)}, u32[]{:S(2)}, u32[]{:S(2)}) %all-to-all-start.6) | async-done | bytes 393248 | tf_op jit(solution)/shard_map/all_to_all | solution.py:44
  43.1 12.9 %all-to-all-start.4 = ((bf16[24,64,128]{2,0,1:T(8,128)(2,1)}), bf16[24,64,128]{2,0,1:T(8,128)(2,1)S(1)}, u32[]{:S(2)}, u32[]{:S(2)}) async-start(bf16[24,64,128]{2,0,1:T(8,128)(2,1)} %copy.61), calls=%async_computation.4 | async-start | bytes 786432 | tf_op jit(solution)/shard_map/all_to_all | solution.py:50
  57.0 13.6 %all-to-all-done.4 = bf16[24,64,128]{2,0,1:T(8,128)(2,1)S(1)} async-done(((bf16[24,64,128]{2,0,1:T(8,128)(2,1)}), bf16[24,64,128]{2,0,1:T(8,128)(2,1)S(1)}, u32[]{:S(2)}, u32[]{:S(2)}) %all-to-all-start.4) | async-done | bytes 393248 | tf_op jit(solution)/shard_map/all_to_all | solution.py:50
  70.6 6.2 %all-to-all-start.7 = ((bf16[24,64,128]{2,0,1:T(8,128)(2,1)}), bf16[24,64,128]{2,0,1:T(8,128)(2,1)S(1)}, u32[]{:S(2)}, u32[]{:S(2)}) async-start(bf16[24,64,128]{2,0,1:T(8,128)(2,1)} %copy.66), calls=%async_computation.7 | async-start | bytes 786432 | tf_op jit(solution)/shard_map/all_to_all | solution.py:53
  76.9 1.3 copy.89
  78.1 13.3 %all-to-all-done.7 = bf16[24,64,128]{2,0,1:T(8,128)(2,1)S(1)} async-done(((bf16[24,64,128]{2,0,1:T(8,128)(2,1)}), bf16[24,64,128]{2,0,1:T(8,128)(2,1)S(1)}, u32[]{:S(2)}, u32[]{:S(2)}) %all-to-all-start.7) | async-done | bytes 393248 | tf_op jit(solution)/shard_map/all_to_all | solution.py:53
  91.5 3.7 all-to-all-start
  95.3 1.7 select_reduce_fusion.1
  97.7 3.2 gather_fusion.1
  101.0 3.2 gather_fusion.2
  106.2 27.2 %all-to-all-done = bf16[192,8,512]{2,0,1:T(8,128)(2,1)S(1)} async-done(((bf16[192,8,512]{2,0,1:T(8,128)(2,1)}), bf16[192,8,512]{2,0,1:T(8,128)(2,1)S(1)}, u32[]{:S(2)}, u32[]{:S(2)}) %all-to-all-start) | async-done | bytes 1572896 | tf_op jit(solution)/shard_map/all_to_all | solution.py:42
  133.4 8.3 %all-to-all-start.8 = ((bf16[24,64,128]{2,0,1:T(8,128)(2,1)}), bf16[24,64,128]{2,0,1:T(8,128)(2,1)S(1)}, u32[]{:S(2)}, u32[]{:S(2)}) async-start(bf16[24,64,128]{2,0,1:T(8,128)(2,1)} %copy.68), calls=%async_computation.8 | async-start | bytes 786432 | tf_op jit(solution)/shard_map/all_to_all | solution.py:74
  141.6 2.0 copy.56
  143.6 12.6 %all-to-all-done.8 = bf16[24,64,128]{2,0,1:T(8,128)(2,1)S(1)} async-done(((bf16[24,64,128]{2,0,1:T(8,128)(2,1)}), bf16[24,64,128]{2,0,1:T(8,128)(2,1)S(1)}, u32[]{:S(2)}, u32[]{:S(2)}) %all-to-all-start.8) | async-done | bytes 393248 | tf_op jit(solution)/shard_map/all_to_all | solution.py:74
  157.0 6.2 %all-to-all-start.1 = ((bf16[24,64,512]{2,0,1:T(8,128)(2,1)}), bf16[24,64,512]{2,0,1:T(8,128)(2,1)S(1)}, u32[]{:S(2)}, u32[]{:S(2)}) async-start(bf16[24,64,512]{2,0,1:T(8,128)(2,1)} %copy.56), calls=%async_computation.1 | async-start | bytes 3145728 | tf_op jit(solution)/shard_map/all_to_all | solution.py:47
  164.2 38.8 %all-to-all-done.1 = bf16[24,64,512]{2,0,1:T(8,128)(2,1)S(1)} async-done(((bf16[24,64,512]{2,0,1:T(8,128)(2,1)}), bf16[24,64,512]{2,0,1:T(8,128)(2,1)S(1)}, u32[]{:S(2)}, u32[]{:S(2)}) %all-to-all-start.1) | async-done | bytes 1572896 | tf_op jit(solution)/shard_map/all_to_all | solution.py:47
  203.0 6.3 %all-to-all-start.5 = ((bf16[24,64,128]{2,0,1:T(8,128)(2,1)}), bf16[24,64,128]{2,0,1:T(8,128)(2,1)}, u32[]{:S(2)}, u32[]{:S(2)}) async-start(bf16[24,64,128]{2,0,1:T(8,128)(2,1)} %copy.63), calls=%async_computation.5 | async-start | bytes 786432 | tf_op jit(solution)/shard_map/all_to_all | solution.py:73
  210.8 4.9 %gather_fusion = bf16[1536,512]{1,0:T(8,128)(2,1)S(1)} fusion(bf16[1536,512]{1,0:T(8,128)(2,1)S(1)} %bitcast.104, s32[2048]{0:T(1024)} %pad_clamp_fusion.1), kind=kCustom, calls=%fused_computation.2 | custom fusion | bytes 3151872 | tf_op jit(solution)/shard_map/jit(_take)/gather | solution.py:66
  215.7 2.2 copy_select_fusion
  217.9 5.9 %all-to-all-done.5 = bf16[24,64,128]{2,0,1:T(8,128)(2,1)} async-done(((bf16[24,64,128]{2,0,1:T(8,128)(2,1)}), bf16[24,64,128]{2,0,1:T(8,128)(2,1)}, u32[]{:S(2)}, u32[]{:S(2)}) %all-to-all-start.5) | async-done | bytes 393248 | tf_op jit(solution)/shard_map/all_to_all | solution.py:73
  223.9 6.2 %all-to-all-start.2 = ((bf16[24,64,512]{2,0,1:T(8,128)(2,1)}), bf16[24,64,512]{2,0,1:T(8,128)(2,1)S(1)}, u32[]{:S(2)}, u32[]{:S(2)}) async-start(bf16[24,64,512]{2,0,1:T(8,128)(2,1)} %copy_select_fusion), calls=%async_computation.2 | async-start | bytes 3145728 | tf_op jit(solution)/shard_map/all_to_all | solution.py:72
  230.2 1.1 copy.64
  231.3 38.6 %all-to-all-done.2 = bf16[24,64,512]{2,0,1:T(8,128)(2,1)S(1)} async-done(((bf16[24,64,512]{2,0,1:T(8,128)(2,1)}), bf16[24,64,512]{2,0,1:T(8,128)(2,1)S(1)}, u32[]{:S(2)}, u32[]{:S(2)}) %all-to-all-start.2) | async-done | bytes 1572896 | tf_op jit(solution)/shard_map/all_to_all | solution.py:72
  269.9 1.7 copy.59
  271.5 2.4 reshape_reshape.9
  273.9 58.4 %while.11 = (s32[]{:T(128)}, bf16[12,128,1,4,128]{4,3,1,0,2:T(4,128)(2,1)}, s32[12]{0:T(128)S(1)}, s32[1536]{0:T(1024)S(1)}, bf16[1536,1,4,128]{3,2,0,1:T(4,128)...) while((s32[]{:T(128)}, ...), condition=%wide.region_5.7_spmd.clone, body=%wide.region_2.6_spmd.clone.sunk | while | flops 410451072 | bytes 11816115 | solution.py:118
  332.3 2.5 all_to_all.83
  334.8 42.9 %all_to_all.97 = bf16[8,192,512]{2,1,0:T(8,128)(2,1)S(1)} all-to-all(bf16[8,192,512]{2,1,0:T(8,128)(2,1)S(1)} %all_to_all.83), channel_id=1, replica_groups=mesh['ctx'=64,'head'=8] {'head'}, dimensions={0} | all-to-all | bytes 3145728 | tf_op jit(solution)/shard_map/all_to_all | solution.py:120
  377.7 1.3 copy.79
  (151 shorter events, 60.4 us)
Async XLA Ops:
  0.0 1.0 copy-start
  0.0 12.7 %copy-start.4 = (bf16[192,1024]{1,0:T(8,128)(2,1)S(1)}, bf16[192,1024]{1,0:T(8,128)(2,1)}, u32[]{:S(2)}) copy-start(bf16[192,1024]{1,0:T(8,128)(2,1)} %param.13) | copy-start | bytes 1179652
  1.8 25.1 %all-to-all-start.3 = ((bf16[192,8,128]{2,0,1:T(8,128)(2,1)}), bf16[192,8,128]{2,0,1:T(8,128)(2,1)S(1)}, u32[]{:S(2)}, u32[]{:S(2)}) async-start(bf16[192,8,128]{2,0,1:T(8,128)(2,1)} %copy_bitcast_fusion.4), calls=%async_computation.3 | async-start | bytes 786432 | tf_op jit(solution)/shard_map/all_to_all | solution.py:43
  26.9 16.2 %all-to-all-start.6 = ((bf16[192,8,128]{2,0,1:T(8,128)(2,1)}), bf16[192,8,128]{2,0,1:T(8,128)(2,1)S(1)}, u32[]{:S(2)}, u32[]{:S(2)}) async-start(bf16[192,8,128]{2,0,1:T(8,128)(2,1)} %copy_bitcast_fusion.3), calls=%async_computation.6 | async-start | bytes 786432 | tf_op jit(solution)/shard_map/all_to_all | solution.py:44
  30.3 46.5 %copy-start.1 = (bf16[192,4096]{1,0:T(8,128)(2,1)S(1)}, bf16[192,4096]{1,0:T(8,128)(2,1)}, u32[]{:S(2)}) copy-start(bf16[192,4096]{1,0:T(8,128)(2,1)} %param.11) | copy-start | bytes 4718596
  43.1 27.5 %all-to-all-start.4 = ((bf16[24,64,128]{2,0,1:T(8,128)(2,1)}), bf16[24,64,128]{2,0,1:T(8,128)(2,1)S(1)}, u32[]{:S(2)}, u32[]{:S(2)}) async-start(bf16[24,64,128]{2,0,1:T(8,128)(2,1)} %copy.61), calls=%async_computation.4 | async-start | bytes 786432 | tf_op jit(solution)/shard_map/all_to_all | solution.py:50
  70.6 20.8 %all-to-all-start.7 = ((bf16[24,64,128]{2,0,1:T(8,128)(2,1)}), bf16[24,64,128]{2,0,1:T(8,128)(2,1)S(1)}, u32[]{:S(2)}, u32[]{:S(2)}) async-start(bf16[24,64,128]{2,0,1:T(8,128)(2,1)} %copy.66), calls=%async_computation.7 | async-start | bytes 786432 | tf_op jit(solution)/shard_map/all_to_all | solution.py:53
  91.5 3.8 copy-start.6
  91.5 3.8 %copy-start.5 = (s32[256]{0:T(256)S(1)}, s32[256]{0:T(256)}, u32[]{:S(2)}) copy-start(s32[256]{0:T(256)} %param.17) | copy-start | bytes 3076
  91.5 3.8 %copy-start.7 = (s32[256]{0:T(256)S(1)}, s32[256]{0:T(256)}, u32[]{:S(2)}) copy-start(s32[256]{0:T(256)} %param.15) | copy-start | bytes 3076
  91.5 3.8 %copy-start.8 = (s32[256]{0:T(256)S(1)}, s32[256]{0:T(256)}, u32[]{:S(2)}) copy-start(s32[256]{0:T(256)} %param.14) | copy-start | bytes 3076
  91.5 41.9 %all-to-all-start = ((bf16[192,8,512]{2,0,1:T(8,128)(2,1)}), bf16[192,8,512]{2,0,1:T(8,128)(2,1)S(1)}, u32[]{:S(2)}, u32[]{:S(2)}) async-start(bf16[192,8,512]{2,0,1:T(8,128)(2,1)} %bitcast.87), calls=%async_computation | async-start | bytes 3145728 | tf_op jit(solution)/shard_map/all_to_all | solution.py:42
  133.4 22.9 %all-to-all-start.8 = ((bf16[24,64,128]{2,0,1:T(8,128)(2,1)}), bf16[24,64,128]{2,0,1:T(8,128)(2,1)S(1)}, u32[]{:S(2)}, u32[]{:S(2)}) async-start(bf16[24,64,128]{2,0,1:T(8,128)(2,1)} %copy.68), calls=%async_computation.8 | async-start | bytes 786432 | tf_op jit(solution)/shard_map/all_to_all | solution.py:74
  156.3 0.8 copy-start.2
  157.0 46.0 %all-to-all-start.1 = ((bf16[24,64,512]{2,0,1:T(8,128)(2,1)}), bf16[24,64,512]{2,0,1:T(8,128)(2,1)S(1)}, u32[]{:S(2)}, u32[]{:S(2)}) async-start(bf16[24,64,512]{2,0,1:T(8,128)(2,1)} %copy.56), calls=%async_computation.1 | async-start | bytes 3145728 | tf_op jit(solution)/shard_map/all_to_all | solution.py:47
  203.0 20.8 %all-to-all-start.5 = ((bf16[24,64,128]{2,0,1:T(8,128)(2,1)}), bf16[24,64,128]{2,0,1:T(8,128)(2,1)}, u32[]{:S(2)}, u32[]{:S(2)}) async-start(bf16[24,64,128]{2,0,1:T(8,128)(2,1)} %copy.63), calls=%async_computation.5 | async-start | bytes 786432 | tf_op jit(solution)/shard_map/all_to_all | solution.py:73
  217.9 12.2 %copy-start.3 = (bf16[24,64,128]{2,0,1:T(8,128)(2,1)S(1)}, bf16[24,64,128]{2,0,1:T(8,128)(2,1)}, u32[]{:S(2)}) copy-start(bf16[24,64,128]{2,0,1:T(8,128)(2,1)} %copy-done.2) | copy-start | bytes 1179652
  223.9 46.0 %all-to-all-start.2 = ((bf16[24,64,512]{2,0,1:T(8,128)(2,1)}), bf16[24,64,512]{2,0,1:T(8,128)(2,1)S(1)}, u32[]{:S(2)}, u32[]{:S(2)}) async-start(bf16[24,64,512]{2,0,1:T(8,128)(2,1)} %copy_select_fusion), calls=%async_computation.2 | async-start | bytes 3145728 | tf_op jit(solution)/shard_map/all_to_all | solution.py:72
where the time goes:
time: 380 us; the launch traced here: 379 us
  waiting for transfers between devices  175 us (46%)
  starting transfers between devices  64.2 us (17%)
  local copies, waits for them, and re-layouts  50.6 us (13%)
  blocking collectives  42.9 us (11%)
  other arithmetic  19.5 us (5%)
  matrix products  17.7 us (5%)
  loops' own time  8.71 us (2%)
    all_to_all x1, blocking collectives, on_device(): lax.all_to_all(attended, 'head', split_axis=0, concat_axis=1, tiled=True)  42.9 us
    all_to_all x1, waiting for transfers between devices, on_device(): lax.all_to_all(by_peer(lanes[0], ctx_count), 'ctx', split_axis=1, concat_...  38.8 us
    all_to_all x1, waiting for transfers between devices, on_device(): lax.all_to_all(moved[0], 'ctx', split_axis=1, concat_axis=1, tiled=True)  38.6 us
    all_to_all x1, waiting for transfers between devices, on_device(): lax.all_to_all(queries, 'head', split_axis=1, concat_axis=0, tiled=True)  27.2 us
    all_to_all x1, waiting for transfers between devices, on_device(): lax.all_to_all(by_peer(lanes[1], ctx_count), 'ctx', split_axis=1, concat_...  13.6 us
    all_to_all x1, waiting for transfers between devices, on_device(): lax.all_to_all(keys, 'head', split_axis=1, concat_axis=0, tiled=True)  13.4 us
    all_to_all x1, waiting for transfers between devices, on_device(): lax.all_to_all(by_peer(lanes[2], ctx_count), 'ctx', split_axis=1, concat_...  13.3 us
    all_to_all x1, starting transfers between devices, on_device(): lax.all_to_all(by_peer(lanes[1], ctx_count), 'ctx', split_axis=1, concat_...  12.9 us
  transfers between devices with their start and end apart: 9, of which 9 were waited for; matrix products, arithmetic and copies ran while one was open for 7% of the time, Pallas kernels for 0%

commit v1 on v0

v1 whole, which is shorter than its diff:
```python
import math

import jax
import jax.numpy as jnp
from jax import lax
from jax.experimental import pallas as pl
from jax.experimental.pallas import tpu as pltpu
from jax.sharding import PartitionSpec as P

HEAD_WIDTH = 128
BLOCK = 128
HALF = 64
QUAD = 4
MASKED = -1e30
EXP2_SCALE = math.log2(math.e) / math.sqrt(HEAD_WIDTH)


def attend_kernel(
    lengths, q_ref, kv_hbm, halo_hbm, out_ref, kv_ref, score_ref, top_ref, sum_ref, acc_ref, sems
):
    block = pl.program_id(0)
    heads = q_ref.shape[1] // HEAD_WIDTH
    halo_rows = halo_hbm.shape[0]
    rows = heads * BLOCK

    @pl.when(block == 0)
    def _():
        own = pltpu.make_async_copy(
            kv_hbm, kv_ref.at[pl.ds(halo_rows, kv_hbm.shape[0])], sems.at[0]
        )
        before = pltpu.make_async_copy(halo_hbm, kv_ref.at[pl.ds(0, halo_rows)], sems.at[1])
        own.start()
        before.start()
        own.wait()
        before.wait()

    length = lengths[block]
    chunks = (length + 1) // 2
    last_row = halo_rows + block * BLOCK
    q = jnp.concatenate(
        [q_ref[:, h * HEAD_WIDTH : (h + 1) * HEAD_WIDTH] for h in range(heads)], axis=0
    )

    def scores_of(chunk):
        first = pl.multiple_of(last_row - BLOCK - chunk * 2 * BLOCK, BLOCK)
        keys = kv_ref[pl.ds(first, 2 * BLOCK), :HEAD_WIDTH]
        s = lax.dot_general(q, keys, (((1,), (1,)), ((), ())), preferred_element_type=jnp.float32)
        older = jnp.where(2 * chunk + 2 <= length, s[:, :BLOCK], MASKED)
        return older, s[:, BLOCK:]

    older, newer = scores_of(0)
    row_ids = lax.broadcasted_iota(jnp.int32, (rows, BLOCK), 0) % BLOCK
    col_ids = lax.broadcasted_iota(jnp.int32, (rows, BLOCK), 1)
    newer = jnp.where(col_ids <= row_ids, newer, MASKED)
    score_ref[0, :, :BLOCK] = older
    score_ref[0, :, BLOCK:] = newer
    top_ref[...] = jnp.maximum(older, newer)

    def first_pass(chunk, carry):
        older, newer = scores_of(chunk)
        score_ref[chunk, :, :BLOCK] = older
        score_ref[chunk, :, BLOCK:] = newer
        top_ref[...] = jnp.maximum(top_ref[...], jnp.maximum(older, newer))
        return carry

    lax.fori_loop(1, chunks, first_pass, 0)
    top = jnp.max(top_ref[...], axis=1, keepdims=True) * EXP2_SCALE
    top_ref[...] = jnp.broadcast_to(top, (rows, BLOCK))
    sum_ref[...] = jnp.zeros_like(sum_ref)
    acc_ref[...] = jnp.zeros_like(acc_ref)

    def second_pass(chunk, carry):
        first = pl.multiple_of(last_row - BLOCK - chunk * 2 * BLOCK, BLOCK)
        vals = kv_ref[pl.ds(first, 2 * BLOCK), HEAD_WIDTH:]
        shift = top_ref[...]
        older = jnp.exp2(score_ref[chunk, :, :BLOCK] * EXP2_SCALE - shift)
        newer = jnp.exp2(score_ref[chunk, :, BLOCK:] * EXP2_SCALE - shift)
        sum_ref[...] += older + newer
        weights = jnp.concatenate(
            [older.astype(jnp.bfloat16), newer.astype(jnp.bfloat16)], axis=1
        )
        acc_ref[...] += jnp.dot(weights, vals, preferred_element_type=jnp.float32)
        return carry

    lax.fori_loop(0, chunks, second_pass, 0)
    totals = jnp.sum(sum_ref[...], axis=1, keepdims=True)
    out = acc_ref[...] / totals
    low = lax.broadcasted_iota(jnp.int32, (HALF, HEAD_WIDTH), 0) % (2 * QUAD) < QUAD
    for h in range(heads):
        upper = out[h * BLOCK : h * BLOCK + HALF]
        lower = out[h * BLOCK + HALF : (h + 1) * BLOCK]
        even = jnp.where(low, upper, pltpu.roll(lower, QUAD, 0))
        odd = jnp.where(low, pltpu.roll(upper, HALF - QUAD, 0), lower)
        for k in range(HALF // (2 * QUAD)):
            tile = slice(2 * QUAD * k, 2 * QUAD * (k + 1))
            out_ref[2 * k * heads + h, 0] = even[tile].astype(jnp.bfloat16)
            out_ref[(2 * k + 1) * heads + h, 0] = odd[tile].astype(jnp.bfloat16)


def attend(lengths, q, kv, halo):
    blocks = q.shape[0] // BLOCK
    heads = q.shape[1] // HEAD_WIDTH
    units = HALF // QUAD * heads
    chunks = (blocks + 1) // 2
    rows = heads * BLOCK
    return pl.pallas_call(
        attend_kernel,
        out_shape=jax.ShapeDtypeStruct((units, blocks, 2 * QUAD, HEAD_WIDTH), jnp.bfloat16),
        grid_spec=pltpu.PrefetchScalarGridSpec(
            num_scalar_prefetch=1,
            grid=(blocks,),
            in_specs=[
                pl.BlockSpec((BLOCK, q.shape[1]), lambda b, lengths: (b, 0)),
                pl.BlockSpec(memory_space=pl.ANY),
                pl.BlockSpec(memory_space=pl.ANY),
            ],
            out_specs=pl.BlockSpec(
                (units, 1, 2 * QUAD, HEAD_WIDTH), lambda b, lengths: (0, b, 0, 0)
            ),
            scratch_shapes=[
                pltpu.VMEM((kv.shape[0] + halo.shape[0], kv.shape[1]), jnp.bfloat16),
                pltpu.VMEM((chunks, rows, 2 * BLOCK), jnp.float32),
                pltpu.VMEM((rows, BLOCK), jnp.float32),
                pltpu.VMEM((rows, BLOCK), jnp.float32),
                pltpu.VMEM((rows, HEAD_WIDTH), jnp.float32),
                pltpu.SemaphoreType.DMA((2,)),
            ],
        ),
        compiler_params=pltpu.CompilerParams(
            dimension_semantics=("arbitrary",), vmem_limit_bytes=32 << 20
        ),
        name="attend",
    )(lengths, q, kv, halo)


def route_kernel(index, x_ref, y_ref):
    def step(n, carry):
        for u in range(16):
            y_ref[n * 16 + u] = x_ref[index[n * 16 + u]]
        return carry

    lax.fori_loop(0, y_ref.shape[0] // 16, step, 0)


def route(index, x):
    return pl.pallas_call(
        route_kernel,
        out_shape=jax.ShapeDtypeStruct(x.shape, x.dtype),
        grid_spec=pltpu.PrefetchScalarGridSpec(
            num_scalar_prefetch=1,
            grid=(1,),
            in_specs=[pl.BlockSpec(x.shape, lambda i, index: (0, 0, 0))],
            out_specs=pl.BlockSpec(x.shape, lambda i, index: (0, 0, 0)),
        ),
        compiler_params=pltpu.CompilerParams(vmem_limit_bytes=32 << 20),
        name="route",
    )(index, x)


def on_device(queries, keys, values, doc_start, doc_blocks, doc_rank, doc_slot):
    ctx_count = lax.axis_size("ctx")
    head_count = lax.axis_size("head")
    rank_index = lax.axis_index("ctx")
    tokens = queries.shape[0]
    rows_per_rank = tokens * head_count
    blocks = rows_per_rank // BLOCK
    key_width = keys.shape[1] // head_count
    query_width = queries.shape[1] // head_count
    heads = query_width // HEAD_WIDTH

    kv = jnp.concatenate(
        [
            keys.reshape(tokens, head_count, key_width),
            values.reshape(tokens, head_count, key_width),
        ],
        axis=2,
    ).transpose(1, 0, 2)
    kv = lax.all_to_all(kv, "head", split_axis=0, concat_axis=0, tiled=True)
    kv = kv.reshape(rows_per_rank, 2 * key_width)
    halo = lax.ppermute(
        kv[BLOCK:], "ctx", [(i, (i + 1) % ctx_count) for i in range(ctx_count)]
    )
    q = queries.reshape(tokens, head_count, query_width).transpose(1, 0, 2)
    q = lax.all_to_all(q, "head", split_axis=0, concat_axis=0, tiled=True)
    q = q.reshape(rows_per_rank, query_width)

    own_blocks = rank_index * blocks + jnp.arange(blocks, dtype=jnp.int32)
    holds = (doc_start[None, :] <= own_blocks[:, None]) & (
        own_blocks[:, None] < (doc_start + doc_blocks)[None, :]
    )
    lengths = own_blocks + 1 - jnp.sum(jnp.where(holds, doc_start[None, :], 0), axis=1)

    new_blocks = jnp.arange(ctx_count * blocks, dtype=jnp.int32)
    first_new = doc_rank * blocks + doc_slot
    lands = (first_new[None, :] <= new_blocks[:, None]) & (
        new_blocks[:, None] < (first_new + doc_blocks)[None, :]
    )
    sources = new_blocks + jnp.sum(
        jnp.where(lands, (doc_start - first_new)[None, :], 0), axis=1
    )

    dealt = attend(lengths, q, kv, halo)
    dealt = lax.all_to_all(dealt, "ctx", split_axis=0, concat_axis=0, tiled=True)
    dealt = dealt.reshape(ctx_count * blocks, 2 * QUAD, HEAD_WIDTH)
    moved = route(sources, dealt)
    parts = tokens // HALF
    moved = moved.reshape(ctx_count * head_count, parts, QUAD, HEAD_WIDTH)
    placed = lax.all_to_all(moved, ("ctx", "head"), split_axis=0, concat_axis=0, tiled=True)
    placed = placed.reshape(HALF // QUAD, heads, head_count, parts, QUAD, HEAD_WIDTH)
    return placed.transpose(3, 0, 4, 2, 1, 5).reshape(tokens, queries.shape[1])


def solution(mesh):
    return jax.shard_map(
        on_device,
        mesh=mesh,
        in_specs=(
            P(("ctx", "head"), None),
            P(("ctx", "head"), None),
            P(("ctx", "head"), None),
            P(),
            P(),
            P(),
            P(),
        ),
        out_specs=P(("ctx", "head"), None),
        check_vma=False,
    )
```

time: 380 us -> 212 us (0.56)
  waiting for transfers between devices: 175 us -> 95.2 us
  local copies, waits for them, and re-layouts: 50.6 us -> 8.74 us
  starting transfers between devices: 64.2 us -> 32.1 us
  Pallas kernels: 0 us -> 20.3 us
  other arithmetic: 19.5 us -> 1.39 us
  matrix products: 17.7 us -> 0 us
  blocking collectives: 42.9 us -> 53.3 us
  loops' own time: 8.71 us -> 0 us
    all_to_all x9 -> x3, waiting for transfers between devices: 175 us -> 87 us  [the longest x1 39.6 us: on_device(): lax.all_to_all(dealt, 'ctx', split_axis=0, concat_axis=0, tiled=True)]
    all_to_all x9 -> x3, starting transfers between devices: 64.2 us -> 28.5 us  [the longest x1 13.9 us: on_device(): lax.all_to_all(dealt, 'ctx', split_axis=0, concat_axis=0, tiled=True)]
    pallas_call x0 -> x2, Pallas kernels: none -> 20.3 us  [the longest x1 18.6 us: attend(): pl.pallas_call(attend_kernel, out_shape=jax.ShapeDtypeStruct((units, bloc...]
    dot_general x24 -> x0, matrix products: 17.7 us -> none  [the longest x12 9.29 us: whole_block(): jnp.einsum('pgrd,qgd->grpq', query_tile, key_matrix, preferred_element_ty...]
    gather x3 -> x0, local copies, waits for them, and re-layouts: 11.4 us -> none  [on_device(): jnp.take(array.reshape(rows_per_rank, array.shape[2]), picked, axis=0)]
    reduce_sum x13 -> x2, other arithmetic: 11.1 us -> 0.39 us  [the longest x1 0.21 us: on_device(): jnp.sum(jnp.where(lands, (doc_start - first_new)[None, :], 0), axis=1)]
    all_to_all x1, blocking collectives: 42.9 us -> 53.3 us  [on_device(): lax.all_to_all(moved, ('ctx', 'head'), split_axis=0, concat_axis=0, tiled...]
    all_to_all x11 -> x0, local copies, waits for them, and re-layouts: 10.2 us -> none  [the longest x2 3.81 us: on_device(): lax.all_to_all(attended, 'head', split_axis=0, concat_axis=1, tiled=True)]
  transfers between devices with their start and end apart: 9 -> 4, of which waited for: 9 -> 4; matrix products, arithmetic and copies ran while one was open for 7% -> 1% of each run, Pallas kernels for 0% -> 0%
where the time goes in v1:
time: 212 us; the launch traced here: 211 us
  waiting for transfers between devices  95.2 us (45%)
  blocking collectives  53.3 us (25%)
  starting transfers between devices  32.1 us (15%)
  Pallas kernels  20.3 us (10%)
  local copies, waits for them, and re-layouts  8.74 us (4%)
    all_to_all x1, blocking collectives, on_device(): lax.all_to_all(moved, ('ctx', 'head'), split_axis=0, concat_axis=0, tiled...  53.3 us
    all_to_all x1, waiting for transfers between devices, on_device(): lax.all_to_all(dealt, 'ctx', split_axis=0, concat_axis=0, tiled=True)  39.6 us
    all_to_all x1, waiting for transfers between devices, on_device(): q = lax.all_to_all(q, 'head', split_axis=0, concat_axis=0, tiled=True)  25.1 us
    all_to_all x1, waiting for transfers between devices, on_device(): kv = lax.all_to_all(kv, 'head', split_axis=0, concat_axis=0, tiled=True)  22.3 us
    pallas_call x1, Pallas kernels, attend(): pl.pallas_call(attend_kernel, out_shape=jax.ShapeDtypeStruct((units, bloc...  18.6 us
    all_to_all x1, starting transfers between devices, on_device(): lax.all_to_all(dealt, 'ctx', split_axis=0, concat_axis=0, tiled=True)  13.9 us
    all_to_all x1, starting transfers between devices, on_device(): kv = lax.all_to_all(kv, 'head', split_axis=0, concat_axis=0, tiled=True)  10.9 us
    ppermute x1, waiting for transfers between devices, on_device(): lax.ppermute(kv[BLOCK:], 'ctx', [(i, (i + 1) % ctx_count) for i in range(...  8.26 us
  transfers between devices with their start and end apart: 4, of which 4 were waited for; matrix products, arithmetic and copies ran while one was open for 1% of the time, Pallas kernels for 0%

profile of v1, /device:TPU:1, one launch (start us, length us, event | category | flops | bytes accessed | tf_op | source)
XLA Modules:
  0.0 211.2 jit_solution(17040088775955714907)
XLA Ops:
  0.0 0.0 copy-start
  0.0 1.0 copy-done
  1.0 1.2 copy_bitcast_fusion.1
  2.2 0.0 copy-start.2
  2.2 1.0 maximum_bitcast_fusion
  3.2 10.9 %all-to-all-start.1 = ((bf16[8,192,256]{2,1,0:T(8,128)(2,1)}), bf16[8,192,256]{2,1,0:T(8,128)(2,1)S(1)}, u32[]{:S(2)}, u32[]{:S(2)}) async-start(bf16[8,192,256]{2,1,0:T(8,128)(2,1)} %maximum_bitcast_fusion), calls=%async_computation.1 | async-start | bytes 1572864 | tf_op jit(solution)/shard_map/all_to_all | solution.py:178
  14.0 0.0 copy-done.2
  14.0 1.3 copy.23
  15.3 22.3 %all-to-all-done.1 = bf16[8,192,256]{2,1,0:T(8,128)(2,1)S(1)} async-done(((bf16[8,192,256]{2,1,0:T(8,128)(2,1)}), bf16[8,192,256]{2,1,0:T(8,128)(2,1)S(1)}, u32[]{:S(2)}, u32[]{:S(2)}) %all-to-all-start.1) | async-done | bytes 786464 | tf_op jit(solution)/shard_map/all_to_all | solution.py:178
  37.6 0.0 copy-start.3
  37.6 0.0 copy-start.4
  37.6 0.0 copy-start.5
  37.6 3.7 %all-to-all-start = ((bf16[8,192,512]{2,1,0:T(8,128)(2,1)}), bf16[8,192,512]{2,1,0:T(8,128)(2,1)S(1)}, u32[]{:S(2)}, u32[]{:S(2)}) async-start(bf16[8,192,512]{2,1,0:T(8,128)(2,1)} %bitcast.32), calls=%async_computation | async-start | bytes 3145728 | tf_op jit(solution)/shard_map/all_to_all | solution.py:184
  41.4 0.9 slice.4
  42.3 3.6 %collective-permute-start = (bf16[1408,256]{1,0:T(8,128)(2,1)}, bf16[1408,256]{1,0:T(8,128)(2,1)S(1)}, u32[]{:S(2)}, u32[]{:S(2)}) collective-permute-start(bf16[1408,256]{1,0:T(8,128)(2,1)} %slice.4), channel_id=1, source_target_pairs={{0,8},{8,16},{16,24},{24,32},{32,40},{40,48},{48,56},{56,64},{64,7... | collective-permute-start | bytes 2162696 | tf_op jit(solution)/shard_map/ppermute | solution.py:180
  45.9 0.0 copy-done.3
  45.9 0.0 copy-done.4
  45.9 0.0 copy-done.5
  45.9 0.0 copy-done.6
  45.9 0.2 select_reduce_fusion.1
  46.1 8.3 %collective-permute-done.halo_hbm = bf16[1408,256]{1,0:T(8,128)(2,1)S(1)} collective-permute-done((bf16[1408,256]{1,0:T(8,128)(2,1)}, bf16[1408,256]{1,0:T(8,128)(2,1)S(1)}, u32[]{:S(2)}, u32[]{:S(2)}) %collective-permute-start) | collective-permute-done | bytes 720928 | tf_op jit(solution)/shard_map/ppermute | solution.py:180
  54.4 25.1 %all-to-all-done = bf16[8,192,512]{2,1,0:T(8,128)(2,1)S(1)} async-done(((bf16[8,192,512]{2,1,0:T(8,128)(2,1)}), bf16[8,192,512]{2,1,0:T(8,128)(2,1)S(1)}, u32[]{:S(2)}, u32[]{:S(2)}) %all-to-all-start) | async-done | bytes 1572896 | tf_op jit(solution)/shard_map/all_to_all | solution.py:184
  79.5 18.6 %attend.1 = bf16[64,12,8,128]{3,2,1,0:T(8,128)(2,1)S(1)} custom-call(s32[12]{0:T(128)S(1)} %add_subtract_fusion.lengths, bf16[1536,512]{1,0:T(8,128)(2,1)S(1)} %bitcast.31, bf16[1536,256]{1,0:T(8,128)(2,1)S(1)} %bitcast.28, bf16[1408,256]{1,0:T(8,128)(2,1)S(1)} %collective-permute-done.halo_hbm), custom_call_target="tpu_custom_call" | custom-call | tf_op jit(solution)/shard_map/attend/pallas_call | solution.py:106
  98.2 0.0 copy-start.1
  98.2 1.1 copy-done.1
  99.3 13.9 %all-to-all-start.2 = ((bf16[64,12,8,128]{3,2,1,0:T(8,128)(2,1)}), bf16[64,12,8,128]{3,2,1,0:T(8,128)(2,1)S(1)}, u32[]{:S(2)}, u32[]{:S(2)}) async-start(bf16[64,12,8,128]{3,2,1,0:T(8,128)(2,1)} %copy-done.1), calls=%async_computation.2 | async-start | bytes 3145728 | tf_op jit(solution)/shard_map/all_to_all | solution.py:203
  113.3 0.2 select_reduce_fusion
  113.5 39.6 %all-to-all-done.2 = bf16[64,12,8,128]{3,2,1,0:T(8,128)(2,1)S(1)} async-done(((bf16[64,12,8,128]{3,2,1,0:T(8,128)(2,1)}), bf16[64,12,8,128]{3,2,1,0:T(8,128)(2,1)S(1)}, u32[]{:S(2)}, u32[]{:S(2)}) %all-to-all-start.2) | async-done | bytes 1572896 | tf_op jit(solution)/shard_map/all_to_all | solution.py:203
  153.1 1.6 route.1
  154.7 53.3 %all_to_all.20 = bf16[512,3,4,128]{3,2,1,0:T(4,128)(2,1)S(1)} all-to-all(bf16[512,3,4,128]{3,2,1,0:T(4,128)(2,1)S(1)} %bitcast.30), channel_id=1, replica_groups=mesh['ctx'=64,'head'=8] {'ctx','head'}, dimensions={0} | all-to-all | bytes 3145728 | tf_op jit(solution)/shard_map/all_to_all | solution.py:208
  208.0 0.8 copy.24
  208.8 2.4 %reshape.44 = bf16[192,4096]{1,0:T(8,128)(2,1)} reshape(bf16[3,16,4,8,4,128]{5,4,3,2,1,0:T(4,128)(2,1)S(1)} %bitcast.34) | data formatting | bytes 3145728 | tf_op jit(solution)/shard_map/reshape | solution.py:210
  (6 shorter events, 0.0 us)
Async XLA Ops:
  0.0 1.0 copy-start
  2.2 11.9 %copy-start.2 = (bf16[192,4096]{1,0:T(8,128)(2,1)S(1)}, bf16[192,4096]{1,0:T(8,128)(2,1)}, u32[]{:S(2)}) copy-start(bf16[192,4096]{1,0:T(8,128)(2,1)} %param.7) | copy-start | bytes 4718596
  3.2 34.4 %all-to-all-start.1 = ((bf16[8,192,256]{2,1,0:T(8,128)(2,1)}), bf16[8,192,256]{2,1,0:T(8,128)(2,1)S(1)}, u32[]{:S(2)}, u32[]{:S(2)}) async-start(bf16[8,192,256]{2,1,0:T(8,128)(2,1)} %maximum_bitcast_fusion), calls=%async_computation.1 | async-start | bytes 1572864 | tf_op jit(solution)/shard_map/all_to_all | solution.py:178
  37.6 8.3 %copy-start.3 = (s32[256]{0:T(256)S(1)}, s32[256]{0:T(256)}, u32[]{:S(2)}) copy-start(s32[256]{0:T(256)} %param.10) | copy-start | bytes 3076
  37.6 8.3 %copy-start.4 = (s32[256]{0:T(256)S(1)}, s32[256]{0:T(256)}, u32[]{:S(2)}) copy-start(s32[256]{0:T(256)} %param.11) | copy-start | bytes 3076
  37.6 8.3 %copy-start.5 = (s32[256]{0:T(256)S(1)}, s32[256]{0:T(256)}, u32[]{:S(2)}) copy-start(s32[256]{0:T(256)} %param.13) | copy-start | bytes 3076
  37.6 8.3 %copy-start.6 = (s32[256]{0:T(256)S(1)}, s32[256]{0:T(256)}, u32[]{:S(2)}) copy-start(s32[256]{0:T(256)} %param.12) | copy-start | bytes 3076
  37.6 41.9 %all-to-all-start = ((bf16[8,192,512]{2,1,0:T(8,128)(2,1)}), bf16[8,192,512]{2,1,0:T(8,128)(2,1)S(1)}, u32[]{:S(2)}, u32[]{:S(2)}) async-start(bf16[8,192,512]{2,1,0:T(8,128)(2,1)} %bitcast.32), calls=%async_computation | async-start | bytes 3145728 | tf_op jit(solution)/shard_map/all_to_all | solution.py:184
  42.3 12.1 %collective-permute-start = (bf16[1408,256]{1,0:T(8,128)(2,1)}, bf16[1408,256]{1,0:T(8,128)(2,1)S(1)}, u32[]{:S(2)}, u32[]{:S(2)}) collective-permute-start(bf16[1408,256]{1,0:T(8,128)(2,1)} %slice.4), channel_id=1, source_target_pairs={{0,8},{8,16},{16,24},{24,32},{32,40},{40,48},{48,56},{56,64},{64,7... | collective-permute-start | bytes 2162696 | tf_op jit(solution)/shard_map/ppermute | solution.py:180
  98.2 1.1 copy-start.1
  99.3 53.7 %all-to-all-start.2 = ((bf16[64,12,8,128]{3,2,1,0:T(8,128)(2,1)}), bf16[64,12,8,128]{3,2,1,0:T(8,128)(2,1)S(1)}, u32[]{:S(2)}, u32[]{:S(2)}) async-start(bf16[64,12,8,128]{3,2,1,0:T(8,128)(2,1)} %copy-done.1), calls=%async_computation.2 | async-start | bytes 3145728 | tf_op jit(solution)/shard_map/all_to_all | solution.py:203

commit v2 on v1

v2 whole, which is shorter than its diff:
```python
import functools
import math

import jax
import jax.numpy as jnp
from jax import lax
from jax.experimental import pallas as pl
from jax.experimental.pallas import tpu as pltpu
from jax.sharding import PartitionSpec as P

HEAD_WIDTH = 128
BLOCK = 128
HALF = 64
QUAD = 4
MASKED = -1e30
EXP2_SCALE = math.log2(math.e) / math.sqrt(HEAD_WIDTH)


def pack_kernel(*refs, pieces):
    out_hbm, sems = refs[-2:]
    copies = []
    for g in range(out_hbm.shape[0]):
        at = 0
        for n, (start, width) in enumerate(pieces):
            source = refs[n]
            first = g * (source.shape[1] // out_hbm.shape[0]) + start
            copies.append(
                pltpu.make_async_copy(
                    source.at[:, pl.ds(first, width)],
                    out_hbm.at[g, :, pl.ds(at, width)],
                    sems.at[n, g],
                )
            )
            at += width
    for copy in copies:
        copy.start()
    for copy in copies:
        copy.wait()


def pack(arrays, pieces, groups):
    tokens = arrays[0].shape[0]
    width = sum(width for _, width in pieces)
    return pl.pallas_call(
        functools.partial(pack_kernel, pieces=pieces),
        out_shape=jax.ShapeDtypeStruct((groups, tokens, width), arrays[0].dtype),
        in_specs=[pl.BlockSpec(memory_space=pl.ANY)] * len(arrays),
        out_specs=pl.BlockSpec(memory_space=pl.ANY),
        scratch_shapes=[pltpu.SemaphoreType.DMA((len(arrays), groups))],
        name="pack",
    )(*arrays)


def attend_block(lengths, q_ref, key_ref, turned_ref, out_ref, score_ref, acc_ref):
    block = pl.program_id(0)
    heads = q_ref.shape[1] // HEAD_WIDTH
    rows = heads * BLOCK
    length = lengths[block]
    chunks = (length + 1) // 2
    newest = key_ref.shape[0] // BLOCK - pl.num_programs(0) + block
    q = jnp.concatenate(
        [q_ref[:, h * HEAD_WIDTH : (h + 1) * HEAD_WIDTH] for h in range(heads)], axis=0
    )

    def scores_of(chunk):
        first = pl.multiple_of((newest - 1 - 2 * chunk) * BLOCK, BLOCK)
        keys = key_ref[pl.ds(first, 2 * BLOCK), :]
        s = lax.dot_general(keys, q, (((1,), (1,)), ((), ())), preferred_element_type=jnp.float32)
        return jnp.where(2 * chunk + 2 <= length, s[:BLOCK], MASKED), s[BLOCK:]

    def fold(x, op):
        return op(x.reshape(BLOCK // 8, 8, rows), axis=0)

    older, newer = scores_of(0)
    key_ids = lax.broadcasted_iota(jnp.int32, (BLOCK, rows), 0)
    query_ids = lax.broadcasted_iota(jnp.int32, (BLOCK, rows), 1) % BLOCK
    newer = jnp.where(key_ids <= query_ids, newer, MASKED)
    score_ref[0, :BLOCK] = older
    score_ref[0, BLOCK:] = newer

    def first_pass(chunk, top):
        older, newer = scores_of(chunk)
        score_ref[chunk, :BLOCK] = older
        score_ref[chunk, BLOCK:] = newer
        return jnp.maximum(top, fold(jnp.maximum(older, newer), jnp.max))

    top = lax.fori_loop(1, chunks, first_pass, fold(jnp.maximum(older, newer), jnp.max))
    shift = jnp.max(top, axis=0, keepdims=True) * EXP2_SCALE

    def weigh(chunk):
        weights = jnp.exp2(score_ref[chunk] * EXP2_SCALE - shift)
        total = fold(weights[:BLOCK] + weights[BLOCK:], jnp.sum)
        at = newest - 1 - 2 * chunk
        vals = jnp.concatenate([turned_ref[at], turned_ref[at + 1]], axis=1)
        out = jnp.dot(vals, weights.astype(jnp.bfloat16), preferred_element_type=jnp.float32)
        return total, out

    total, out = weigh(0)
    acc_ref[...] = out

    def second_pass(chunk, total):
        more, out = weigh(chunk)
        acc_ref[...] += out
        return total + more

    total = lax.fori_loop(1, chunks, second_pass, total)
    out = acc_ref[...] * (1.0 / jnp.sum(total, axis=0, keepdims=True))
    low = lax.broadcasted_iota(jnp.int32, (HALF, HEAD_WIDTH), 0) % (2 * QUAD) < QUAD
    quads = HALF // QUAD
    for h in range(heads):
        placed = out[:, h * BLOCK : (h + 1) * BLOCK].T
        upper = placed[:HALF]
        lower = placed[HALF:]
        even = jnp.where(low, upper, pltpu.roll(lower, QUAD, 0))
        odd = jnp.where(low, pltpu.roll(upper, HALF - QUAD, 0), lower)
        for k in range(quads // 2):
            tile = slice(2 * QUAD * k, 2 * QUAD * (k + 1))
            out_ref[h * quads + 2 * k, 0] = even[tile].astype(jnp.bfloat16)
            out_ref[h * quads + 2 * k + 1, 0] = odd[tile].astype(jnp.bfloat16)


def attend_first_kernel(
    lengths, q_ref, kv_hbm, halo_hbm, out_ref, turned_ref, key_ref, value_ref, score_ref, acc_ref, sems
):
    @pl.when(pl.program_id(0) == 0)
    def _():
        before = pl.ds(0, halo_hbm.shape[0])
        own = pl.ds(halo_hbm.shape[0], kv_hbm.shape[0])
        low = pl.ds(0, HEAD_WIDTH)
        high = pl.ds(HEAD_WIDTH, HEAD_WIDTH)
        copies = [
            pltpu.make_async_copy(kv_hbm.at[:, high], value_ref.at[own], sems.at[0]),
            pltpu.make_async_copy(halo_hbm.at[:, high], value_ref.at[before], sems.at[1]),
            pltpu.make_async_copy(kv_hbm.at[:, low], key_ref.at[own], sems.at[2]),
            pltpu.make_async_copy(halo_hbm.at[:, low], key_ref.at[before], sems.at[3]),
        ]
        for copy in copies:
            copy.start()
        for copy in copies:
            copy.wait()

        def turn(n, carry):
            first = pl.multiple_of(n * BLOCK, BLOCK)
            part = value_ref[pl.ds(first, BLOCK), :].astype(jnp.float32)
            turned_ref[n] = part.T.astype(jnp.bfloat16)
            return carry

        lax.fori_loop(0, turned_ref.shape[0], turn, 0)

    attend_block(lengths, q_ref, key_ref, turned_ref, out_ref, score_ref, acc_ref)


def attend_second_kernel(
    lengths,
    q_ref,
    kv_hbm,
    halo_hbm,
    turned_hbm,
    done_hbm,
    out_ref,
    key_ref,
    turned_ref,
    score_ref,
    acc_ref,
    sems,
):
    del done_hbm

    @pl.when(pl.program_id(0) == 0)
    def _():
        before = pl.ds(0, halo_hbm.shape[0])
        own = pl.ds(halo_hbm.shape[0], kv_hbm.shape[0])
        low = pl.ds(0, HEAD_WIDTH)
        copies = [
            pltpu.make_async_copy(kv_hbm.at[:, low], key_ref.at[own], sems.at[0]),
            pltpu.make_async_copy(halo_hbm.at[:, low], key_ref.at[before], sems.at[1]),
            pltpu.make_async_copy(turned_hbm, turned_ref, sems.at[2]),
        ]
        for copy in copies:
            copy.start()
        for copy in copies:
            copy.wait()

    attend_block(lengths, q_ref, key_ref, turned_ref, out_ref, score_ref, acc_ref)


def attend(lengths, q, kv, halo, earlier=None):
    blocks = q.shape[0] // BLOCK
    heads = q.shape[1] // HEAD_WIDTH
    units = HALF // QUAD * heads
    window = kv.shape[0] + halo.shape[0]
    rows = heads * BLOCK
    out_shape = jax.ShapeDtypeStruct((2 * units, blocks, 2 * QUAD, HEAD_WIDTH), jnp.bfloat16)
    turned_shape = (window // BLOCK, HEAD_WIDTH, BLOCK)
    hbm = pl.BlockSpec(memory_space=pl.ANY)
    turned_spec = pl.BlockSpec(turned_shape, lambda b, lengths: (0, 0, 0))
    specs = [pl.BlockSpec((BLOCK, q.shape[1]), lambda b, lengths: (b, 0)), hbm, hbm]
    part = 0 if earlier is None else 1
    out_spec = pl.BlockSpec(
        (units, 1, 2 * QUAD, HEAD_WIDTH), lambda b, lengths: (part, b, 0, 0)
    )
    keys = pltpu.VMEM((window, HEAD_WIDTH), jnp.bfloat16)
    work = [
        pltpu.VMEM(((blocks + 1) // 2, 2 * BLOCK, rows), jnp.float32),
        pltpu.VMEM((HEAD_WIDTH, rows), jnp.float32),
    ]
    params = pltpu.CompilerParams(
        dimension_semantics=("arbitrary",), vmem_limit_bytes=32 << 20
    )
    if earlier is None:
        return pl.pallas_call(
            attend_first_kernel,
            out_shape=(out_shape, jax.ShapeDtypeStruct(turned_shape, jnp.bfloat16)),
            grid_spec=pltpu.PrefetchScalarGridSpec(
                num_scalar_prefetch=1,
                grid=(blocks,),
                in_specs=specs,
                out_specs=(out_spec, turned_spec),
                scratch_shapes=[keys, keys] + work + [pltpu.SemaphoreType.DMA((4,))],
            ),
            compiler_params=params,
            name="attend_first",
        )(lengths, q, kv, halo)
    done, turned = earlier
    return pl.pallas_call(
        attend_second_kernel,
        out_shape=out_shape,
        grid_spec=pltpu.PrefetchScalarGridSpec(
            num_scalar_prefetch=1,
            grid=(blocks,),
            in_specs=specs + [hbm, hbm],
            out_specs=out_spec,
            scratch_shapes=[keys, pltpu.VMEM(turned_shape, jnp.bfloat16)]
            + work
            + [pltpu.SemaphoreType.DMA((3,))],
        ),
        input_output_aliases={5: 0},
        compiler_params=params,
        name="attend_second",
    )(lengths, q, kv, halo, turned, done)


def route_kernel(index, x_ref, y_ref):
    def step(n, carry):
        for u in range(16):
            y_ref[n * 16 + u] = x_ref[index[n * 16 + u]]
        return carry

    lax.fori_loop(0, y_ref.shape[0] // 16, step, 0)


def route(index, x):
    return pl.pallas_call(
        route_kernel,
        out_shape=jax.ShapeDtypeStruct(x.shape, x.dtype),
        grid_spec=pltpu.PrefetchScalarGridSpec(
            num_scalar_prefetch=1,
            grid=(1,),
            in_specs=[pl.BlockSpec(x.shape, lambda i, index: (0, 0, 0))],
            out_specs=pl.BlockSpec(x.shape, lambda i, index: (0, 0, 0)),
        ),
        compiler_params=pltpu.CompilerParams(vmem_limit_bytes=32 << 20),
        name="route",
    )(index, x)


def on_device(queries, keys, values, doc_start, doc_blocks, doc_rank, doc_slot):
    ctx_count = lax.axis_size("ctx")
    head_count = lax.axis_size("head")
    rank_index = lax.axis_index("ctx")
    tokens = queries.shape[0]
    rows_per_rank = tokens * head_count
    blocks = rows_per_rank // BLOCK
    key_width = keys.shape[1] // head_count
    query_width = queries.shape[1] // head_count
    heads = query_width // HEAD_WIDTH

    half_width = query_width // 2

    def gather_heads(x):
        x = lax.all_to_all(x, "head", split_axis=0, concat_axis=0, tiled=True)
        return x.reshape(rows_per_rank, x.shape[2])

    kv = gather_heads(pack((keys, values), ((0, key_width), (0, key_width)), head_count))
    halo = lax.ppermute(
        kv[BLOCK:], "ctx", [(i, (i + 1) % ctx_count) for i in range(ctx_count)]
    )
    q_first = gather_heads(pack((queries,), ((0, half_width),), head_count))
    packed = pack((queries,), ((half_width, half_width),), head_count)
    packed, q_first, halo = lax.optimization_barrier((packed, q_first, halo))
    q_second = gather_heads(packed)

    own_blocks = rank_index * blocks + jnp.arange(blocks, dtype=jnp.int32)
    holds = (doc_start[None, :] <= own_blocks[:, None]) & (
        own_blocks[:, None] < (doc_start + doc_blocks)[None, :]
    )
    lengths = own_blocks + 1 - jnp.sum(jnp.where(holds, doc_start[None, :], 0), axis=1)

    new_blocks = jnp.arange(ctx_count * blocks, dtype=jnp.int32)
    first_new = doc_rank * blocks + doc_slot
    lands = (first_new[None, :] <= new_blocks[:, None]) & (
        new_blocks[:, None] < (first_new + doc_blocks)[None, :]
    )
    sources = new_blocks + jnp.sum(
        jnp.where(lands, (doc_start - first_new)[None, :], 0), axis=1
    )

    dealt = attend(lengths, q_second, kv, halo, attend(lengths, q_first, kv, halo))
    dealt = lax.all_to_all(dealt, "ctx", split_axis=0, concat_axis=0, tiled=True)
    dealt = dealt.reshape(ctx_count * blocks, 2 * QUAD, HEAD_WIDTH)
    moved = route(sources, dealt)
    parts = tokens // HALF
    moved = moved.reshape(ctx_count * head_count, parts, QUAD, HEAD_WIDTH)
    placed = lax.all_to_all(moved, ("ctx", "head"), split_axis=0, concat_axis=0, tiled=True)
    placed = placed.reshape(heads, HALF // QUAD, head_count, parts, QUAD, HEAD_WIDTH)
    return placed.transpose(3, 1, 4, 2, 0, 5).reshape(tokens, queries.shape[1])


def solution(mesh):
    return jax.shard_map(
        on_device,
        mesh=mesh,
        in_specs=(
            P(("ctx", "head"), None),
            P(("ctx", "head"), None),
            P(("ctx", "head"), None),
            P(),
            P(),
            P(),
            P(),
        ),
        out_specs=P(("ctx", "head"), None),
        check_vma=False,
    )
```

time: 212 us -> 255 us (1.20)
  Pallas kernels: 20.3 us -> 103 us
  waiting for transfers between devices: 95.2 us -> 47.3 us
  starting transfers between devices: 32.1 us -> 42.5 us
  local copies, waits for them, and re-layouts: 8.74 us -> 5.7 us
    pallas_call x1 -> x5, Pallas kernels: 18.6 us -> 102 us  [the longest x3 75.1 us: pack(): pl.pallas_call(functools.partial(pack_kernel, pieces=pieces), out_shape=j...]
    all_to_all x2 -> x3, waiting for transfers between devices: 47.4 us -> 7.72 us  [gather_heads(): x = lax.all_to_all(x, 'head', split_axis=0, concat_axis=0, tiled=True)]
    all_to_all x2 -> x3, starting transfers between devices: 14.6 us -> 24.5 us  [gather_heads(): x = lax.all_to_all(x, 'head', split_axis=0, concat_axis=0, tiled=True)]
    ppermute x1, waiting for transfers between devices: 8.26 us -> 0.01 us  [on_device(): lax.ppermute(kv[BLOCK:], 'ctx', [(i, (i + 1) % ctx_count) for i in range(...]
    reshape x4 -> x2, local copies, waits for them, and re-layouts: 5.68 us -> 3.61 us  [the longest x1 2.39 us: on_device(): return placed.transpose(3, 1, 4, 2, 0, 5).reshape(tokens, queries.shape[1])]
  transfers between devices with their start and end apart: 4 -> 5, of which waited for: 4 -> 2; matrix products, arithmetic and copies ran while one was open for 1% -> 0% of each run, Pallas kernels for 0% -> 25%
where the time goes in v2:
time: 255 us
  Pallas kernels  103 us (40%)
  blocking collectives  55.7 us (22%)
  waiting for transfers between devices  47.3 us (19%)
  starting transfers between devices  42.5 us (17%)
  local copies, waits for them, and re-layouts  5.7 us (2%)
    pallas_call x3, Pallas kernels, pack(): pl.pallas_call(functools.partial(pack_kernel, pieces=pieces), out_shape=j...  75.1 us
    all_to_all x1, blocking collectives, on_device(): lax.all_to_all(moved, ('ctx', 'head'), split_axis=0, concat_axis=0, tiled...  55.7 us
    all_to_all x1, waiting for transfers between devices, on_device(): lax.all_to_all(dealt, 'ctx', split_axis=0, concat_axis=0, tiled=True)  39.6 us
    all_to_all x3, starting transfers between devices, gather_heads(): x = lax.all_to_all(x, 'head', split_axis=0, concat_axis=0, tiled=True)  24.5 us
    pallas_call x1, Pallas kernels, attend(): pl.pallas_call(attend_first_kernel, out_shape=(out_shape, jax.ShapeDtypeS...  14.3 us
    all_to_all x1, starting transfers between devices, on_device(): lax.all_to_all(dealt, 'ctx', split_axis=0, concat_axis=0, tiled=True)  13.3 us
    pallas_call x1, Pallas kernels, attend(): pl.pallas_call(attend_second_kernel, out_shape=out_shape, grid_spec=pltpu...  12.2 us
    all_to_all x3, waiting for transfers between devices, gather_heads(): x = lax.all_to_all(x, 'head', split_axis=0, concat_axis=0, tiled=True)  7.72 us
  transfers between devices with their start and end apart: 5, of which 2 were waited for; matrix products, arithmetic and copies ran while one was open for 0% of the time, Pallas kernels for 25%

profile of v2, /device:TPU:1, one launch (start us, length us, event | category | flops | bytes accessed | tf_op | source)
XLA Modules:
  0.0 255.0 jit_solution(7992690294036925542)
XLA Ops:
  0.0 25.1 %pack.5 = bf16[8,192,256]{2,1,0:T(8,128)(2,1)} custom-call(bf16[192,1024]{1,0:T(8,128)(2,1)} %refs_0_.5, bf16[192,1024]{1,0:T(8,128)(2,1)} %refs_1_.1), custom_call_target="tpu_custom_call" | custom-call | tf_op jit(solution)/shard_map/pack/pallas_call | solution.py:44
  25.1 10.9 %all-to-all-start.1 = ((bf16[8,192,256]{2,1,0:T(8,128)(2,1)}), bf16[8,192,256]{2,1,0:T(8,128)(2,1)S(1)}, u32[]{:S(2)}, u32[]{:S(2)}) async-start(bf16[8,192,256]{2,1,0:T(8,128)(2,1)} %pack.5), calls=%async_computation.1 | async-start | bytes 1572864 | tf_op jit(solution)/shard_map/all_to_all | solution.py:281
  36.0 25.0 %pack.4 = bf16[8,192,256]{2,1,0:T(8,128)(2,1)} custom-call(bf16[192,4096]{1,0:T(8,128)(2,1)} %refs_0_.4), custom_call_target="tpu_custom_call" | custom-call | tf_op jit(solution)/shard_map/pack/pallas_call | solution.py:44
  61.0 0.0 all-to-all-done.1
  61.0 6.7 %all-to-all-start = ((bf16[8,192,256]{2,1,0:T(8,128)(2,1)}), bf16[8,192,256]{2,1,0:T(8,128)(2,1)S(1)}, u32[]{:S(2)}, u32[]{:S(2)}) async-start(bf16[8,192,256]{2,1,0:T(8,128)(2,1)} %pack.4), calls=%async_computation | async-start | bytes 1572864 | tf_op jit(solution)/shard_map/all_to_all | solution.py:281
  67.7 0.0 copy-start.2
  67.7 0.0 copy-start.3
  67.7 0.0 copy-start.4
  67.7 0.0 copy-start.5
  67.7 4.7 %collective-permute-start = (bf16[1408,256]{1,0:T(8,128)(2,1)S(1)}, bf16[1408,256]{1,0:T(8,128)(2,1)S(1)}, u32[]{:S(2)}, u32[]{:S(2)}) collective-permute-start(bf16[1408,256]{1,0:T(8,128)(2,1)S(1)} %slice.4), channel_id=1, source_target_pairs={{0,8},{8,16},{16,24},{24,32},{32,40},{40,48},{48,56},{56,64},{64,7... | collective-permute-start | bytes 2162696 | tf_op jit(solution)/shard_map/ppermute | solution.py:285
  72.5 25.0 %pack.3 = bf16[8,192,256]{2,1,0:T(8,128)(2,1)} custom-call(bf16[192,4096]{1,0:T(8,128)(2,1)} %refs_0_.4), custom_call_target="tpu_custom_call" | custom-call | tf_op jit(solution)/shard_map/pack/pallas_call | solution.py:44
  97.5 0.0 all-to-all-done
  97.5 0.0 collective-permute-done.halo_hbm
  97.5 6.9 %all-to-all-start.2 = ((bf16[8,192,256]{2,1,0:T(8,128)(2,1)}), bf16[8,192,256]{2,1,0:T(8,128)(2,1)S(1)}, u32[]{:S(2)}, u32[]{:S(2)}) async-start(bf16[8,192,256]{2,1,0:T(8,128)(2,1)} %pack.3), calls=%async_computation.2 | async-start | bytes 1572864 | tf_op jit(solution)/shard_map/all_to_all | solution.py:281
  104.4 0.0 copy-done.2
  104.4 0.0 copy-done.3
  104.5 0.0 copy-done.4
  104.5 0.0 copy-done.5
  104.5 0.2 select_reduce_fusion.1
  104.7 14.3 %attend_first.1 = (bf16[64,12,8,128]{3,2,1,0:T(8,128)(2,1)}, bf16[23,128,128]{2,1,0:T(8,128)(2,1)S(1)}) custom-call(s32[12]{0:T(128)S(1)} %add_subtract_fusion.lengths, bf16[1536,256]{1,0:T(8,128)(2,1)S(1)} %bitcast.14, bf16[1536,256]{1,0:T(8,128)(2,1)S(1)} %bitcast.10, bf16[1408,256]{1,0:T(8,128)(2,1)S(1)} %collective-permute-done.halo_hbm), custom_call_target="tpu_custom_call" | custom-call | tf_op jit(solution)/shard_map/attend_first/pallas_call | solution.py:211
  119.0 0.0 copy-start
  119.0 0.9 copy-done
  119.9 7.7 %all-to-all-done.2 = bf16[8,192,256]{2,1,0:T(8,128)(2,1)S(1)} async-done(((bf16[8,192,256]{2,1,0:T(8,128)(2,1)}), bf16[8,192,256]{2,1,0:T(8,128)(2,1)S(1)}, u32[]{:S(2)}, u32[]{:S(2)}) %all-to-all-start.2) | async-done | bytes 786464 | tf_op jit(solution)/shard_map/all_to_all | solution.py:281
  127.6 1.1 copy-done.1
  128.8 12.2 %attend_second.1 = bf16[64,12,8,128]{3,2,1,0:T(8,128)(2,1)} custom-call(s32[12]{0:T(128)S(1)} %add_subtract_fusion.lengths, bf16[1536,256]{1,0:T(8,128)(2,1)S(1)} %bitcast.15, bf16[1536,256]{1,0:T(8,128)(2,1)S(1)} %bitcast.11, bf16[1408,256]{1,0:T(8,128)(2,1)S(1)} %collective-permute-done.halo_hbm, ...), custom_call_target="tpu_custom_call", output_to_operand_aliasing={{}: (5, {})} | custom-call | tf_op jit(solution)/shard_map/attend_second/pallas_call | solution.py:225
  140.9 13.3 %all-to-all-start.3 = ((bf16[64,12,8,128]{3,2,1,0:T(8,128)(2,1)}), bf16[64,12,8,128]{3,2,1,0:T(8,128)(2,1)S(1)}, u32[]{:S(2)}, u32[]{:S(2)}) async-start(bf16[64,12,8,128]{3,2,1,0:T(8,128)(2,1)} %attend_second.1), calls=%async_computation.3 | async-start | bytes 3145728 | tf_op jit(solution)/shard_map/all_to_all | solution.py:309
  154.2 0.2 select_reduce_fusion
  154.4 39.6 %all-to-all-done.3 = bf16[64,12,8,128]{3,2,1,0:T(8,128)(2,1)S(1)} async-done(((bf16[64,12,8,128]{3,2,1,0:T(8,128)(2,1)}), bf16[64,12,8,128]{3,2,1,0:T(8,128)(2,1)S(1)}, u32[]{:S(2)}, u32[]{:S(2)}) %all-to-all-start.3) | async-done | bytes 1572896 | tf_op jit(solution)/shard_map/all_to_all | solution.py:309
  194.0 1.6 route.1
  195.6 55.7 %all_to_all.25 = bf16[512,3,4,128]{3,2,1,0:T(4,128)(2,1)S(1)} all-to-all(bf16[512,3,4,128]{3,2,1,0:T(4,128)(2,1)S(1)} %bitcast.13), channel_id=1, replica_groups=mesh['ctx'=64,'head'=8] {'ctx','head'}, dimensions={0} | all-to-all | bytes 3145728 | tf_op jit(solution)/shard_map/all_to_all | solution.py:314
  251.4 1.2 copy.12
  252.6 2.4 reshape.36
  (7 shorter events, 0.1 us)
Async XLA Ops:
  25.1 35.9 %all-to-all-start.1 = ((bf16[8,192,256]{2,1,0:T(8,128)(2,1)}), bf16[8,192,256]{2,1,0:T(8,128)(2,1)S(1)}, u32[]{:S(2)}, u32[]{:S(2)}) async-start(bf16[8,192,256]{2,1,0:T(8,128)(2,1)} %pack.5), calls=%async_computation.1 | async-start | bytes 1572864 | tf_op jit(solution)/shard_map/all_to_all | solution.py:281
  61.0 36.5 %all-to-all-start = ((bf16[8,192,256]{2,1,0:T(8,128)(2,1)}), bf16[8,192,256]{2,1,0:T(8,128)(2,1)S(1)}, u32[]{:S(2)}, u32[]{:S(2)}) async-start(bf16[8,192,256]{2,1,0:T(8,128)(2,1)} %pack.4), calls=%async_computation | async-start | bytes 1572864 | tf_op jit(solution)/shard_map/all_to_all | solution.py:281
  67.7 36.8 %copy-start.2 = (s32[256]{0:T(256)S(1)}, s32[256]{0:T(256)}, u32[]{:S(2)}) copy-start(s32[256]{0:T(256)} %param.10) | copy-start | bytes 3076
  67.7 36.8 %copy-start.3 = (s32[256]{0:T(256)S(1)}, s32[256]{0:T(256)}, u32[]{:S(2)}) copy-start(s32[256]{0:T(256)} %param.11) | copy-start | bytes 3076
  67.7 36.8 %copy-start.4 = (s32[256]{0:T(256)S(1)}, s32[256]{0:T(256)}, u32[]{:S(2)}) copy-start(s32[256]{0:T(256)} %param.13) | copy-start | bytes 3076
  67.7 36.8 %copy-start.5 = (s32[256]{0:T(256)S(1)}, s32[256]{0:T(256)}, u32[]{:S(2)}) copy-start(s32[256]{0:T(256)} %param.12) | copy-start | bytes 3076
  67.7 29.8 %collective-permute-start = (bf16[1408,256]{1,0:T(8,128)(2,1)S(1)}, bf16[1408,256]{1,0:T(8,128)(2,1)S(1)}, u32[]{:S(2)}, u32[]{:S(2)}) collective-permute-start(bf16[1408,256]{1,0:T(8,128)(2,1)S(1)} %slice.4), channel_id=1, source_target_pairs={{0,8},{8,16},{16,24},{24,32},{32,40},{40,48},{48,56},{56,64},{64,7... | collective-permute-start | bytes 2162696 | tf_op jit(solution)/shard_map/ppermute | solution.py:285
  97.5 30.1 %all-to-all-start.2 = ((bf16[8,192,256]{2,1,0:T(8,128)(2,1)}), bf16[8,192,256]{2,1,0:T(8,128)(2,1)S(1)}, u32[]{:S(2)}, u32[]{:S(2)}) async-start(bf16[8,192,256]{2,1,0:T(8,128)(2,1)} %pack.3), calls=%async_computation.2 | async-start | bytes 1572864 | tf_op jit(solution)/shard_map/all_to_all | solution.py:281
  119.0 0.9 copy-start
  127.6 1.1 copy-start.1
  140.9 53.1 %all-to-all-start.3 = ((bf16[64,12,8,128]{3,2,1,0:T(8,128)(2,1)}), bf16[64,12,8,128]{3,2,1,0:T(8,128)(2,1)S(1)}, u32[]{:S(2)}, u32[]{:S(2)}) async-start(bf16[64,12,8,128]{3,2,1,0:T(8,128)(2,1)} %attend_second.1), calls=%async_computation.3 | async-start | bytes 3145728 | tf_op jit(solution)/shard_map/all_to_all | solution.py:309

commit v3 on v2

v3 whole, which is shorter than its diff:
```python
import functools
import math

import jax
import jax.numpy as jnp
from jax import lax
from jax.experimental import pallas as pl
from jax.experimental.pallas import tpu as pltpu
from jax.sharding import PartitionSpec as P

HEAD_WIDTH = 128
BLOCK = 128
HALF = 64
QUAD = 4
STEP = 4
MASKED = -1e30
EXP2_SCALE = math.log2(math.e) / math.sqrt(HEAD_WIDTH)


def pack_kernel(*refs, pieces):
    out_hbm, packed_ref, in_sems, out_sems = refs[-4:]
    groups = out_hbm.shape[0]
    loads = []
    stores = []
    for g in range(groups):
        at = 0
        for n, (start, width) in enumerate(pieces):
            source = refs[n]
            first = g * (source.shape[1] // groups) + start
            loads.append(
                pltpu.make_async_copy(
                    source.at[:, pl.ds(first, width)],
                    packed_ref.at[g, :, pl.ds(at, width)],
                    in_sems.at[g, n],
                )
            )
            at += width
        stores.append(pltpu.make_async_copy(packed_ref.at[g], out_hbm.at[g], out_sems.at[g]))
    for load in loads:
        load.start()
    for g in range(groups):
        for load in loads[g * len(pieces) : (g + 1) * len(pieces)]:
            load.wait()
        stores[g].start()
    for store in stores:
        store.wait()


def pack(arrays, pieces, groups):
    tokens = arrays[0].shape[0]
    shape = (groups, tokens, sum(width for _, width in pieces))
    return pl.pallas_call(
        functools.partial(pack_kernel, pieces=pieces),
        out_shape=jax.ShapeDtypeStruct(shape, arrays[0].dtype),
        in_specs=[pl.BlockSpec(memory_space=pl.ANY)] * len(arrays),
        out_specs=pl.BlockSpec(memory_space=pl.ANY),
        scratch_shapes=[
            pltpu.VMEM(shape, arrays[0].dtype),
            pltpu.SemaphoreType.DMA((groups, len(arrays))),
            pltpu.SemaphoreType.DMA((groups,)),
        ],
        name="pack",
    )(*arrays)


def attend_blocks(lengths, q_ref, key_ref, turned_ref, result_ref, out_hbm, part, sems):
    heads = q_ref.shape[1] // HEAD_WIDTH
    rows = heads * BLOCK
    blocks = result_ref.shape[0]
    units = result_ref.shape[1]
    before = key_ref.shape[0] // BLOCK - blocks
    quads = HALF // QUAD

    def store_of(block):
        return pltpu.make_async_copy(
            result_ref.at[block], out_hbm.at[pl.ds(part * units, units), block], sems.at[block]
        )

    def window(block, length, size):
        first = pl.multiple_of((before + block + 1 - size) * BLOCK, BLOCK)
        row = pl.multiple_of(block * BLOCK, BLOCK)
        q = jnp.concatenate(
            [
                q_ref[pl.ds(row, BLOCK), h * HEAD_WIDTH : (h + 1) * HEAD_WIDTH]
                for h in range(heads)
            ],
            axis=0,
        )
        keys = key_ref[pl.ds(first, size * BLOCK), :HEAD_WIDTH]
        s = lax.dot_general(keys, q, (((1,), (1,)), ((), ())), preferred_element_type=jnp.float32)
        pieces = [s[n * BLOCK : (n + 1) * BLOCK] for n in range(size)]
        for n in range(min(STEP, size) - 1):
            pieces[n] = jnp.where(size - n <= length, pieces[n], MASKED)
        key_ids = lax.broadcasted_iota(jnp.int32, (BLOCK, rows), 0)
        query_ids = lax.broadcasted_iota(jnp.int32, (BLOCK, rows), 1) % BLOCK
        pieces[-1] = jnp.where(key_ids <= query_ids, pieces[-1], MASKED)
        top = functools.reduce(jnp.maximum, pieces)
        shift = jnp.max(top, axis=0, keepdims=True) * EXP2_SCALE
        pieces = [jnp.exp2(piece * EXP2_SCALE - shift) for piece in pieces]
        total = jnp.sum(functools.reduce(jnp.add, pieces), axis=0, keepdims=True)
        weights = jnp.concatenate([piece.astype(jnp.bfloat16) for piece in pieces], axis=0)
        vals = jnp.concatenate(
            [turned_ref[before + block + 1 - size + n] for n in range(size)], axis=1
        )
        out = jnp.dot(vals, weights, preferred_element_type=jnp.float32) * (1.0 / total)
        low = lax.broadcasted_iota(jnp.int32, (HALF, HEAD_WIDTH), 0) % (2 * QUAD) < QUAD
        for h in range(heads):
            placed = out[:, h * BLOCK : (h + 1) * BLOCK].T
            upper = placed[:HALF]
            lower = placed[HALF:]
            even = jnp.where(low, upper, pltpu.roll(lower, QUAD, 0))
            odd = jnp.where(low, pltpu.roll(upper, HALF - QUAD, 0), lower)
            for k in range(quads // 2):
                tile = slice(2 * QUAD * k, 2 * QUAD * (k + 1))
                result_ref[block, h * quads + 2 * k] = even[tile].astype(jnp.bfloat16)
                result_ref[block, h * quads + 2 * k + 1] = odd[tile].astype(jnp.bfloat16)

    def step(block, carry):
        length = lengths[block]
        for size in range(STEP, blocks + STEP, STEP):

            @pl.when((length > size - STEP) & (length <= size))
            def _():
                window(block, length, min(size, before + 1))

        store_of(block).start()
        return carry

    lax.fori_loop(0, blocks, step, 0)
    for block in range(blocks):
        store_of(block).wait()


def attend_first_kernel(
    lengths,
    q_hbm,
    kv_hbm,
    halo_hbm,
    out_hbm,
    turned_hbm,
    q_ref,
    kv_ref,
    turned_ref,
    result_ref,
    in_sems,
    sems,
):
    before = halo_hbm.shape[0]
    copies = [
        pltpu.make_async_copy(q_hbm, q_ref, in_sems.at[0]),
        pltpu.make_async_copy(kv_hbm, kv_ref.at[pl.ds(before, kv_hbm.shape[0])], in_sems.at[1]),
        pltpu.make_async_copy(halo_hbm, kv_ref.at[pl.ds(0, before)], in_sems.at[2]),
    ]
    for copy in copies:
        copy.start()
    for copy in copies:
        copy.wait()

    def turn(n, carry):
        first = pl.multiple_of(n * BLOCK, BLOCK)
        part = kv_ref[pl.ds(first, BLOCK), HEAD_WIDTH:].astype(jnp.float32)
        turned_ref[n] = part.T.astype(jnp.bfloat16)
        return carry

    lax.fori_loop(0, turned_ref.shape[0], turn, 0)
    keep = pltpu.make_async_copy(turned_ref, turned_hbm, in_sems.at[3])
    keep.start()
    attend_blocks(lengths, q_ref, kv_ref, turned_ref, result_ref, out_hbm, 0, sems)
    keep.wait()


def attend_second_kernel(
    lengths,
    q_hbm,
    kv_hbm,
    halo_hbm,
    turned_hbm,
    done_hbm,
    out_hbm,
    q_ref,
    key_ref,
    turned_ref,
    result_ref,
    in_sems,
    sems,
):
    del done_hbm
    before = halo_hbm.shape[0]
    low = pl.ds(0, HEAD_WIDTH)
    own = pl.ds(before, kv_hbm.shape[0])
    copies = [
        pltpu.make_async_copy(q_hbm, q_ref, in_sems.at[0]),
        pltpu.make_async_copy(kv_hbm.at[:, low], key_ref.at[own], in_sems.at[1]),
        pltpu.make_async_copy(halo_hbm.at[:, low], key_ref.at[pl.ds(0, before)], in_sems.at[2]),
        pltpu.make_async_copy(turned_hbm, turned_ref, in_sems.at[3]),
    ]
    for copy in copies:
        copy.start()
    for copy in copies:
        copy.wait()
    attend_blocks(lengths, q_ref, key_ref, turned_ref, result_ref, out_hbm, 1, sems)


def attend(lengths, q, kv, halo, earlier=None):
    blocks = q.shape[0] // BLOCK
    units = HALF // QUAD * (q.shape[1] // HEAD_WIDTH)
    window = kv.shape[0] + halo.shape[0]
    out_shape = jax.ShapeDtypeStruct((2 * units, blocks, 2 * QUAD, HEAD_WIDTH), jnp.bfloat16)
    turned_shape = (window // BLOCK, HEAD_WIDTH, BLOCK)
    hbm = pl.BlockSpec(memory_space=pl.ANY)
    smem = pl.BlockSpec(memory_space=pltpu.SMEM)
    result = pltpu.VMEM((blocks, units, 2 * QUAD, HEAD_WIDTH), jnp.bfloat16)
    stores = pltpu.SemaphoreType.DMA((blocks,))
    params = pltpu.CompilerParams(vmem_limit_bytes=32 << 20)
    if earlier is None:
        return pl.pallas_call(
            attend_first_kernel,
            out_shape=(out_shape, jax.ShapeDtypeStruct(turned_shape, jnp.bfloat16)),
            in_specs=[smem, hbm, hbm, hbm],
            out_specs=(hbm, hbm),
            scratch_shapes=[
                pltpu.VMEM(q.shape, q.dtype),
                pltpu.VMEM((window, kv.shape[1]), kv.dtype),
                pltpu.VMEM(turned_shape, jnp.bfloat16),
                result,
                pltpu.SemaphoreType.DMA((4,)),
                stores,
            ],
            compiler_params=params,
            name="attend_first",
        )(lengths, q, kv, halo)
    done, turned = earlier
    return pl.pallas_call(
        attend_second_kernel,
        out_shape=out_shape,
        in_specs=[smem] + [hbm] * 5,
        out_specs=hbm,
        scratch_shapes=[
            pltpu.VMEM(q.shape, q.dtype),
            pltpu.VMEM((window, HEAD_WIDTH), kv.dtype),
            pltpu.VMEM(turned_shape, jnp.bfloat16),
            result,
            pltpu.SemaphoreType.DMA((4,)),
            stores,
        ],
        input_output_aliases={5: 0},
        compiler_params=params,
        name="attend_second",
    )(lengths, q, kv, halo, turned, done)


def route_kernel(index, x_ref, y_ref):
    def step(n, carry):
        for u in range(16):
            y_ref[n * 16 + u] = x_ref[index[n * 16 + u]]
        return carry

    lax.fori_loop(0, y_ref.shape[0] // 16, step, 0)


def route(index, x):
    return pl.pallas_call(
        route_kernel,
        out_shape=jax.ShapeDtypeStruct(x.shape, x.dtype),
        grid_spec=pltpu.PrefetchScalarGridSpec(
            num_scalar_prefetch=1,
            grid=(1,),
            in_specs=[pl.BlockSpec(x.shape, lambda i, index: (0, 0, 0))],
            out_specs=pl.BlockSpec(x.shape, lambda i, index: (0, 0, 0)),
        ),
        compiler_params=pltpu.CompilerParams(vmem_limit_bytes=32 << 20),
        name="route",
    )(index, x)


def on_device(queries, keys, values, doc_start, doc_blocks, doc_rank, doc_slot):
    ctx_count = lax.axis_size("ctx")
    head_count = lax.axis_size("head")
    rank_index = lax.axis_index("ctx")
    tokens = queries.shape[0]
    rows_per_rank = tokens * head_count
    blocks = rows_per_rank // BLOCK
    key_width = keys.shape[1] // head_count
    query_width = queries.shape[1] // head_count
    heads = query_width // HEAD_WIDTH

    half_width = query_width // 2

    def gather_heads(x):
        x = lax.all_to_all(x, "head", split_axis=0, concat_axis=0, tiled=True)
        return x.reshape(rows_per_rank, x.shape[2])

    kv = gather_heads(pack((keys, values), ((0, key_width), (0, key_width)), head_count))
    halo = lax.ppermute(
        kv[BLOCK:], "ctx", [(i, (i + 1) % ctx_count) for i in range(ctx_count)]
    )
    q_first = gather_heads(pack((queries,), ((0, half_width),), head_count))
    packed = pack((queries,), ((half_width, half_width),), head_count)
    packed, q_first, halo = lax.optimization_barrier((packed, q_first, halo))
    q_second = gather_heads(packed)

    own_blocks = rank_index * blocks + jnp.arange(blocks, dtype=jnp.int32)
    holds = (doc_start[None, :] <= own_blocks[:, None]) & (
        own_blocks[:, None] < (doc_start + doc_blocks)[None, :]
    )
    lengths = own_blocks + 1 - jnp.sum(jnp.where(holds, doc_start[None, :], 0), axis=1)

    new_blocks = jnp.arange(ctx_count * blocks, dtype=jnp.int32)
    first_new = doc_rank * blocks + doc_slot
    lands = (first_new[None, :] <= new_blocks[:, None]) & (
        new_blocks[:, None] < (first_new + doc_blocks)[None, :]
    )
    sources = new_blocks + jnp.sum(
        jnp.where(lands, (doc_start - first_new)[None, :], 0), axis=1
    )

    dealt = attend(lengths, q_second, kv, halo, attend(lengths, q_first, kv, halo))
    dealt = lax.all_to_all(dealt, "ctx", split_axis=0, concat_axis=0, tiled=True)
    dealt = dealt.reshape(ctx_count * blocks, 2 * QUAD, HEAD_WIDTH)
    moved = route(sources, dealt)
    parts = tokens // HALF
    moved = moved.reshape(ctx_count * head_count, parts, QUAD, HEAD_WIDTH)
    placed = lax.all_to_all(moved, ("ctx", "head"), split_axis=0, concat_axis=0, tiled=True)
    placed = placed.reshape(heads, HALF // QUAD, head_count, parts, QUAD, HEAD_WIDTH)
    return placed.transpose(3, 1, 4, 2, 0, 5).reshape(tokens, queries.shape[1])


def solution(mesh):
    return jax.shard_map(
        on_device,
        mesh=mesh,
        in_specs=(
            P(("ctx", "head"), None),
            P(("ctx", "head"), None),
            P(("ctx", "head"), None),
            P(),
            P(),
            P(),
            P(),
        ),
        out_specs=P(("ctx", "head"), None),
        check_vma=False,
    )
```

time: 255 us -> 213 us (0.84)
  Pallas kernels: 103 us -> 31.2 us
  waiting for transfers between devices: 47.3 us -> 88.1 us
  starting transfers between devices: 42.5 us -> 33.9 us
    pallas_call x3, Pallas kernels: 75.1 us -> 6 us  [pack(): pl.pallas_call(functools.partial(pack_kernel, pieces=pieces), out_shape=j...]
    all_to_all x3, waiting for transfers between devices: 7.72 us -> 48.6 us  [gather_heads(): x = lax.all_to_all(x, 'head', split_axis=0, concat_axis=0, tiled=True)]
    all_to_all x3, starting transfers between devices: 24.5 us -> 18 us  [gather_heads(): x = lax.all_to_all(x, 'head', split_axis=0, concat_axis=0, tiled=True)]
  transfers between devices with their start and end apart: 5 -> 5, of which waited for: 2 -> 4; matrix products, arithmetic and copies ran while one was open for 0% -> 0% of each run, Pallas kernels for 25% -> 8%
where the time goes in v3:
time: 213 us
  waiting for transfers between devices  88.1 us (41%)
  blocking collectives  53.3 us (25%)
  starting transfers between devices  33.9 us (16%)
  Pallas kernels  31.2 us (15%)
  local copies, waits for them, and re-layouts  5.7 us (3%)
    all_to_all x1, blocking collectives, on_device(): lax.all_to_all(moved, ('ctx', 'head'), split_axis=0, concat_axis=0, tiled...  53.3 us
    all_to_all x3, waiting for transfers between devices, gather_heads(): x = lax.all_to_all(x, 'head', split_axis=0, concat_axis=0, tiled=True)  48.6 us
    all_to_all x1, waiting for transfers between devices, on_device(): lax.all_to_all(dealt, 'ctx', split_axis=0, concat_axis=0, tiled=True)  39.6 us
    all_to_all x3, starting transfers between devices, gather_heads(): x = lax.all_to_all(x, 'head', split_axis=0, concat_axis=0, tiled=True)  18 us
    pallas_call x1, Pallas kernels, attend(): pl.pallas_call(attend_first_kernel, out_shape=(out_shape, jax.ShapeDtypeS...  13.1 us
    all_to_all x1, starting transfers between devices, on_device(): lax.all_to_all(dealt, 'ctx', split_axis=0, concat_axis=0, tiled=True)  12.2 us
    pallas_call x1, Pallas kernels, attend(): pl.pallas_call(attend_second_kernel, out_shape=out_shape, in_specs=[smem]...  10.5 us
    pallas_call x3, Pallas kernels, pack(): pl.pallas_call(functools.partial(pack_kernel, pieces=pieces), out_shape=j...  6 us
  transfers between devices with their start and end apart: 5, of which 4 were waited for; matrix products, arithmetic and copies ran while one was open for 0% of the time, Pallas kernels for 8%

profile of v3, /device:TPU:1, one launch (start us, length us, event | category | flops | bytes accessed | tf_op | source)
XLA Modules:
  0.0 212.8 jit_solution(7650022777483452394)
XLA Ops:
  0.0 2.0 pack.5
  2.0 10.9 %all-to-all-start.1 = ((bf16[8,192,256]{2,1,0:T(8,128)(2,1)}), bf16[8,192,256]{2,1,0:T(8,128)(2,1)S(1)}, u32[]{:S(2)}, u32[]{:S(2)}) async-start(bf16[8,192,256]{2,1,0:T(8,128)(2,1)} %pack.5), calls=%async_computation.1 | async-start | bytes 1572864 | tf_op jit(solution)/shard_map/all_to_all | solution.py:290
  12.9 2.0 pack.4
  14.9 21.6 %all-to-all-done.1 = bf16[8,192,256]{2,1,0:T(8,128)(2,1)S(1)} async-done(((bf16[8,192,256]{2,1,0:T(8,128)(2,1)}), bf16[8,192,256]{2,1,0:T(8,128)(2,1)S(1)}, u32[]{:S(2)}, u32[]{:S(2)}) %all-to-all-start.1) | async-done | bytes 786464 | tf_op jit(solution)/shard_map/all_to_all | solution.py:290
  36.5 3.5 %all-to-all-start = ((bf16[8,192,256]{2,1,0:T(8,128)(2,1)}), bf16[8,192,256]{2,1,0:T(8,128)(2,1)S(1)}, u32[]{:S(2)}, u32[]{:S(2)}) async-start(bf16[8,192,256]{2,1,0:T(8,128)(2,1)} %pack.4), calls=%async_computation | async-start | bytes 1572864 | tf_op jit(solution)/shard_map/all_to_all | solution.py:290
  40.1 0.0 copy-start.2
  40.1 0.0 copy-start.3
  40.1 0.0 copy-start.4
  40.1 0.0 copy-start.5
  40.1 3.7 %collective-permute-start = (bf16[1408,256]{1,0:T(8,128)(2,1)S(1)}, bf16[1408,256]{1,0:T(8,128)(2,1)S(1)}, u32[]{:S(2)}, u32[]{:S(2)}) collective-permute-start(bf16[1408,256]{1,0:T(8,128)(2,1)S(1)} %slice.4), channel_id=1, source_target_pairs={{0,8},{8,16},{16,24},{24,32},{32,40},{40,48},{48,56},{56,64},{64,7... | collective-permute-start | bytes 2162696 | tf_op jit(solution)/shard_map/ppermute | solution.py:294
  43.8 2.0 pack.3
  45.9 17.7 %all-to-all-done = bf16[8,192,256]{2,1,0:T(8,128)(2,1)S(1)} async-done(((bf16[8,192,256]{2,1,0:T(8,128)(2,1)}), bf16[8,192,256]{2,1,0:T(8,128)(2,1)S(1)}, u32[]{:S(2)}, u32[]{:S(2)}) %all-to-all-start) | async-done | bytes 786464 | tf_op jit(solution)/shard_map/all_to_all | solution.py:290
  63.5 0.0 collective-permute-done.halo_hbm
  63.5 3.5 %all-to-all-start.2 = ((bf16[8,192,256]{2,1,0:T(8,128)(2,1)}), bf16[8,192,256]{2,1,0:T(8,128)(2,1)S(1)}, u32[]{:S(2)}, u32[]{:S(2)}) async-start(bf16[8,192,256]{2,1,0:T(8,128)(2,1)} %pack.3), calls=%async_computation.2 | async-start | bytes 1572864 | tf_op jit(solution)/shard_map/all_to_all | solution.py:290
  67.1 0.0 copy-done.2
  67.1 0.0 copy-done.3
  67.1 0.0 copy-done.4
  67.2 0.0 copy-done.5
  67.2 0.2 select_reduce_fusion.1
  67.4 13.1 %attend_first.1 = (bf16[64,12,8,128]{3,2,1,0:T(8,128)(2,1)}, bf16[23,128,128]{2,1,0:T(8,128)(2,1)S(1)}) custom-call(s32[12]{0:T(128)S(1)} %add_subtract_fusion.lengths, bf16[1536,256]{1,0:T(8,128)(2,1)S(1)} %bitcast.14, bf16[1536,256]{1,0:T(8,128)(2,1)S(1)} %bitcast.10, bf16[1408,256]{1,0:T(8,128)(2,1)S(1)} %collective-permute-done.halo_hbm), custom_call_target="tpu_custom_call" | custom-call | tf_op jit(solution)/shard_map/attend_first/pallas_call | solution.py:216
  80.4 0.0 copy-start
  80.5 0.9 copy-done
  81.3 9.3 %all-to-all-done.2 = bf16[8,192,256]{2,1,0:T(8,128)(2,1)S(1)} async-done(((bf16[8,192,256]{2,1,0:T(8,128)(2,1)}), bf16[8,192,256]{2,1,0:T(8,128)(2,1)S(1)}, u32[]{:S(2)}, u32[]{:S(2)}) %all-to-all-start.2) | async-done | bytes 786464 | tf_op jit(solution)/shard_map/all_to_all | solution.py:290
  90.6 1.1 copy-done.1
  91.8 10.5 %attend_second.1 = bf16[64,12,8,128]{3,2,1,0:T(8,128)(2,1)} custom-call(s32[12]{0:T(128)S(1)} %add_subtract_fusion.lengths, bf16[1536,256]{1,0:T(8,128)(2,1)S(1)} %bitcast.15, bf16[1536,256]{1,0:T(8,128)(2,1)S(1)} %bitcast.11, bf16[1408,256]{1,0:T(8,128)(2,1)S(1)} %collective-permute-done.halo_hbm, ...), custom_call_target="tpu_custom_call", output_to_operand_aliasing={{}: (5, {})} | custom-call | tf_op jit(solution)/shard_map/attend_second/pallas_call | solution.py:233
  102.3 12.2 %all-to-all-start.3 = ((bf16[64,12,8,128]{3,2,1,0:T(8,128)(2,1)}), bf16[64,12,8,128]{3,2,1,0:T(8,128)(2,1)S(1)}, u32[]{:S(2)}, u32[]{:S(2)}) async-start(bf16[64,12,8,128]{3,2,1,0:T(8,128)(2,1)} %attend_second.1), calls=%async_computation.3 | async-start | bytes 3145728 | tf_op jit(solution)/shard_map/all_to_all | solution.py:318
  114.5 0.2 select_reduce_fusion
  114.7 39.6 %all-to-all-done.3 = bf16[64,12,8,128]{3,2,1,0:T(8,128)(2,1)S(1)} async-done(((bf16[64,12,8,128]{3,2,1,0:T(8,128)(2,1)}), bf16[64,12,8,128]{3,2,1,0:T(8,128)(2,1)S(1)}, u32[]{:S(2)}, u32[]{:S(2)}) %all-to-all-start.3) | async-done | bytes 1572896 | tf_op jit(solution)/shard_map/all_to_all | solution.py:318
  154.3 1.6 route.1
  155.9 53.3 %all_to_all.25 = bf16[512,3,4,128]{3,2,1,0:T(4,128)(2,1)S(1)} all-to-all(bf16[512,3,4,128]{3,2,1,0:T(4,128)(2,1)S(1)} %bitcast.13), channel_id=1, replica_groups=mesh['ctx'=64,'head'=8] {'ctx','head'}, dimensions={0} | all-to-all | bytes 3145728 | tf_op jit(solution)/shard_map/all_to_all | solution.py:323
  209.2 1.2 copy.12
  210.4 2.4 %reshape.36 = bf16[192,4096]{1,0:T(8,128)(2,1)} reshape(bf16[3,16,4,8,4,128]{5,4,3,2,1,0:T(4,128)(2,1)S(1)} %bitcast.17) | data formatting | bytes 3145728 | tf_op jit(solution)/shard_map/reshape | solution.py:325
  (7 shorter events, 0.1 us)
Async XLA Ops:
  2.0 34.5 %all-to-all-start.1 = ((bf16[8,192,256]{2,1,0:T(8,128)(2,1)}), bf16[8,192,256]{2,1,0:T(8,128)(2,1)S(1)}, u32[]{:S(2)}, u32[]{:S(2)}) async-start(bf16[8,192,256]{2,1,0:T(8,128)(2,1)} %pack.5), calls=%async_computation.1 | async-start | bytes 1572864 | tf_op jit(solution)/shard_map/all_to_all | solution.py:290
  36.5 27.1 %all-to-all-start = ((bf16[8,192,256]{2,1,0:T(8,128)(2,1)}), bf16[8,192,256]{2,1,0:T(8,128)(2,1)S(1)}, u32[]{:S(2)}, u32[]{:S(2)}) async-start(bf16[8,192,256]{2,1,0:T(8,128)(2,1)} %pack.4), calls=%async_computation | async-start | bytes 1572864 | tf_op jit(solution)/shard_map/all_to_all | solution.py:290
  40.1 27.1 %copy-start.2 = (s32[256]{0:T(256)S(1)}, s32[256]{0:T(256)}, u32[]{:S(2)}) copy-start(s32[256]{0:T(256)} %param.10) | copy-start | bytes 3076
  40.1 27.1 %copy-start.3 = (s32[256]{0:T(256)S(1)}, s32[256]{0:T(256)}, u32[]{:S(2)}) copy-start(s32[256]{0:T(256)} %param.11) | copy-start | bytes 3076
  40.1 27.1 %copy-start.4 = (s32[256]{0:T(256)S(1)}, s32[256]{0:T(256)}, u32[]{:S(2)}) copy-start(s32[256]{0:T(256)} %param.13) | copy-start | bytes 3076
  40.1 27.1 %copy-start.5 = (s32[256]{0:T(256)S(1)}, s32[256]{0:T(256)}, u32[]{:S(2)}) copy-start(s32[256]{0:T(256)} %param.12) | copy-start | bytes 3076
  40.1 23.4 %collective-permute-start = (bf16[1408,256]{1,0:T(8,128)(2,1)S(1)}, bf16[1408,256]{1,0:T(8,128)(2,1)S(1)}, u32[]{:S(2)}, u32[]{:S(2)}) collective-permute-start(bf16[1408,256]{1,0:T(8,128)(2,1)S(1)} %slice.4), channel_id=1, source_target_pairs={{0,8},{8,16},{16,24},{24,32},{32,40},{40,48},{48,56},{56,64},{64,7... | collective-permute-start | bytes 2162696 | tf_op jit(solution)/shard_map/ppermute | solution.py:294
  63.5 27.1 %all-to-all-start.2 = ((bf16[8,192,256]{2,1,0:T(8,128)(2,1)}), bf16[8,192,256]{2,1,0:T(8,128)(2,1)S(1)}, u32[]{:S(2)}, u32[]{:S(2)}) async-start(bf16[8,192,256]{2,1,0:T(8,128)(2,1)} %pack.3), calls=%async_computation.2 | async-start | bytes 1572864 | tf_op jit(solution)/shard_map/all_to_all | solution.py:290
  80.4 0.9 copy-start
  90.6 1.1 copy-start.1
  102.3 52.0 %all-to-all-start.3 = ((bf16[64,12,8,128]{3,2,1,0:T(8,128)(2,1)}), bf16[64,12,8,128]{3,2,1,0:T(8,128)(2,1)S(1)}, u32[]{:S(2)}, u32[]{:S(2)}) async-start(bf16[64,12,8,128]{3,2,1,0:T(8,128)(2,1)} %attend_second.1), calls=%async_computation.3 | async-start | bytes 3145728 | tf_op jit(solution)/shard_map/all_to_all | solution.py:318

commit v4 on v3

v4 whole, which is shorter than its diff:
```python
import functools
import math

import jax
import jax.numpy as jnp
from jax import lax
from jax.experimental import pallas as pl
from jax.experimental.pallas import tpu as pltpu
from jax.sharding import PartitionSpec as P

HEAD_WIDTH = 128
BLOCK = 128
HALF = 64
QUAD = 4
STEP = 2
MASKED = -1e30
EXP2_SCALE = math.log2(math.e) / math.sqrt(HEAD_WIDTH)


def pack_kernel(*refs, pieces):
    out_hbm, packed_ref, in_sems, out_sems = refs[-4:]
    groups = out_hbm.shape[0]
    loads = []
    stores = []
    for g in range(groups):
        at = 0
        for n, (start, width) in enumerate(pieces):
            source = refs[n]
            first = g * (source.shape[1] // groups) + start
            loads.append(
                pltpu.make_async_copy(
                    source.at[:, pl.ds(first, width)],
                    packed_ref.at[g, :, pl.ds(at, width)],
                    in_sems.at[g, n],
                )
            )
            at += width
        stores.append(pltpu.make_async_copy(packed_ref.at[g], out_hbm.at[g], out_sems.at[g]))
    for load in loads:
        load.start()
    for g in range(groups):
        for load in loads[g * len(pieces) : (g + 1) * len(pieces)]:
            load.wait()
        stores[g].start()
    for store in stores:
        store.wait()


def pack(arrays, pieces, groups):
    tokens = arrays[0].shape[0]
    shape = (groups, tokens, sum(width for _, width in pieces))
    return pl.pallas_call(
        functools.partial(pack_kernel, pieces=pieces),
        out_shape=jax.ShapeDtypeStruct(shape, arrays[0].dtype),
        in_specs=[pl.BlockSpec(memory_space=pl.ANY)] * len(arrays),
        out_specs=pl.BlockSpec(memory_space=pl.ANY),
        scratch_shapes=[
            pltpu.VMEM(shape, arrays[0].dtype),
            pltpu.SemaphoreType.DMA((groups, len(arrays))),
            pltpu.SemaphoreType.DMA((groups,)),
        ],
        name="pack",
    )(*arrays)


def prepare_kernel(kv_ref, halo_ref, key_ref, turned_ref):
    before = halo_ref.shape[0]
    key_ref[:before] = halo_ref[:, :HEAD_WIDTH]
    key_ref[before:] = kv_ref[:, :HEAD_WIDTH]

    def turn_from(source_ref, at):
        def turn(n, carry):
            first = pl.multiple_of(n * BLOCK, BLOCK)
            part = source_ref[pl.ds(first, BLOCK), HEAD_WIDTH:].astype(jnp.float32)
            turned_ref[at + n] = part.T.astype(jnp.bfloat16)
            return carry

        lax.fori_loop(0, source_ref.shape[0] // BLOCK, turn, 0)

    turn_from(halo_ref, 0)
    turn_from(kv_ref, before // BLOCK)


def prepare(kv, halo):
    window = kv.shape[0] + halo.shape[0]
    vmem = pl.BlockSpec(memory_space=pltpu.VMEM)
    return pl.pallas_call(
        prepare_kernel,
        out_shape=(
            jax.ShapeDtypeStruct((window, HEAD_WIDTH), kv.dtype),
            jax.ShapeDtypeStruct((window // BLOCK, HEAD_WIDTH, BLOCK), kv.dtype),
        ),
        in_specs=[vmem, vmem],
        out_specs=(vmem, vmem),
        compiler_params=pltpu.CompilerParams(vmem_limit_bytes=8 << 20),
        name="prepare",
    )(kv, halo)


def attend_kernel(
    lengths, q_ref, key_ref, turned_ref, out_hbm, order_ref, acc_ref, result_ref, sems
):
    heads = q_ref.shape[1] // HEAD_WIDTH
    rows = heads * BLOCK
    blocks = q_ref.shape[0] // BLOCK
    before = key_ref.shape[0] // BLOCK - blocks
    quads = HALF // QUAD

    def store_of(block):
        return pltpu.make_async_copy(
            result_ref.at[block + 1], out_hbm.at[:, block], sems.at[block]
        )

    out_ids = lax.broadcasted_iota(jnp.int32, (BLOCK, BLOCK), 0)
    from_ids = out_ids // (2 * QUAD) * QUAD + out_ids % (2 * QUAD) // QUAD * HALF + out_ids % QUAD
    query_ids = lax.broadcasted_iota(jnp.int32, (BLOCK, BLOCK), 1)
    order_ref[...] = (from_ids == query_ids).astype(jnp.bfloat16)

    def finish(slot):
        order = order_ref[...]
        for h in range(heads):
            placed = lax.dot_general(
                order,
                acc_ref[:, h * BLOCK : (h + 1) * BLOCK],
                (((1,), (1,)), ((), ())),
                preferred_element_type=jnp.float32,
            )
            result_ref[slot, h * quads : (h + 1) * quads] = placed.reshape(
                quads, 2 * QUAD, HEAD_WIDTH
            ).astype(jnp.bfloat16)

    def window(block, length, size):
        finish(block)
        first = pl.multiple_of((before + block + 1 - size) * BLOCK, BLOCK)
        row = pl.multiple_of(block * BLOCK, BLOCK)
        q = jnp.concatenate(
            [
                q_ref[pl.ds(row, BLOCK), h * HEAD_WIDTH : (h + 1) * HEAD_WIDTH]
                for h in range(heads)
            ],
            axis=0,
        )
        keys = key_ref[pl.ds(first, size * BLOCK), :]
        s = lax.dot_general(keys, q, (((1,), (1,)), ((), ())), preferred_element_type=jnp.float32)
        pieces = [s[n * BLOCK : (n + 1) * BLOCK] for n in range(size)]
        for n in range(min(STEP, size) - 1):
            pieces[n] = jnp.where(size - n <= length, pieces[n], MASKED)
        key_ids = lax.broadcasted_iota(jnp.int32, (BLOCK, rows), 0)
        query_ids = lax.broadcasted_iota(jnp.int32, (BLOCK, rows), 1) % BLOCK
        pieces[-1] = jnp.where(key_ids <= query_ids, pieces[-1], MASKED)
        top = functools.reduce(jnp.maximum, pieces)
        shift = jnp.max(top, axis=0, keepdims=True) * EXP2_SCALE
        pieces = [jnp.exp2(piece * EXP2_SCALE - shift) for piece in pieces]
        total = jnp.sum(functools.reduce(jnp.add, pieces), axis=0, keepdims=True)
        weights = jnp.concatenate([piece.astype(jnp.bfloat16) for piece in pieces], axis=0)
        vals = jnp.concatenate(
            [turned_ref[before + block + 1 - size + n] for n in range(size)], axis=1
        )
        out = jnp.dot(vals, weights, preferred_element_type=jnp.float32)
        acc_ref[...] = (out * (1.0 / total)).astype(jnp.bfloat16)

    def step(block, carry):
        length = lengths[block]
        for size in range(STEP, blocks + STEP, STEP):

            @pl.when((length > size - STEP) & (length <= size))
            def _():
                window(block, length, min(size, before + 1))

        @pl.when(block > 0)
        def _():
            store_of(block - 1).start()

        return carry

    lax.fori_loop(0, blocks, step, 0)
    finish(blocks)
    store_of(blocks - 1).start()
    for block in range(blocks):
        store_of(block).wait()


def attend(lengths, q, keys, turned):
    blocks = q.shape[0] // BLOCK
    heads = q.shape[1] // HEAD_WIDTH
    units = HALF // QUAD * heads
    vmem = pl.BlockSpec(memory_space=pltpu.VMEM)
    tile = (2 * QUAD, HEAD_WIDTH)
    return pl.pallas_call(
        attend_kernel,
        out_shape=jax.ShapeDtypeStruct((units, blocks) + tile, jnp.bfloat16),
        in_specs=[pl.BlockSpec(memory_space=pltpu.SMEM), vmem, vmem, vmem],
        out_specs=pl.BlockSpec(memory_space=pl.ANY),
        scratch_shapes=[
            pltpu.VMEM((BLOCK, BLOCK), jnp.bfloat16),
            pltpu.VMEM((HEAD_WIDTH, heads * BLOCK), jnp.bfloat16),
            pltpu.VMEM((blocks + 1, units) + tile, jnp.bfloat16),
            pltpu.SemaphoreType.DMA((blocks,)),
        ],
        compiler_params=pltpu.CompilerParams(vmem_limit_bytes=20 << 20),
        name="attend",
    )(lengths, q, keys, turned)


def route_kernel(index, x_ref, y_ref):
    def step(n, carry):
        for u in range(16):
            y_ref[n * 16 + u] = x_ref[index[n * 16 + u]]
        return carry

    lax.fori_loop(0, y_ref.shape[0] // 16, step, 0)


def route(index, x):
    vmem = pl.BlockSpec(memory_space=pltpu.VMEM)
    return pl.pallas_call(
        route_kernel,
        out_shape=jax.ShapeDtypeStruct(x.shape, x.dtype),
        in_specs=[pl.BlockSpec(memory_space=pltpu.SMEM), vmem],
        out_specs=vmem,
        compiler_params=pltpu.CompilerParams(vmem_limit_bytes=8 << 20),
        name="route",
    )(index, x)


def settle_kernel(x_ref, y_ref):
    heads, quads, groups, parts = x_ref.shape[:4]

    def step(n, carry):
        half = n % 2
        pair = n // 2
        for p in range(parts):
            for g in range(groups):
                for h in range(heads):
                    y_ref[p * (quads // 2) + pair, g * heads + h, half] = x_ref[h, n, g, p]
        return carry

    lax.fori_loop(0, quads, step, 0)


def settle(x):
    heads, quads, groups, parts = x.shape[:4]
    vmem = pl.BlockSpec(memory_space=pltpu.VMEM)
    return pl.pallas_call(
        settle_kernel,
        out_shape=jax.ShapeDtypeStruct(
            (parts * quads // 2, groups * heads, 2) + x.shape[4:], x.dtype
        ),
        in_specs=[vmem],
        out_specs=vmem,
        compiler_params=pltpu.CompilerParams(vmem_limit_bytes=8 << 20),
        name="settle",
    )(x)


def on_device(queries, keys, values, doc_start, doc_blocks, doc_rank, doc_slot):
    ctx_count = lax.axis_size("ctx")
    head_count = lax.axis_size("head")
    rank_index = lax.axis_index("ctx")
    tokens = queries.shape[0]
    rows_per_rank = tokens * head_count
    blocks = rows_per_rank // BLOCK
    key_width = keys.shape[1] // head_count
    query_width = queries.shape[1] // head_count
    heads = query_width // HEAD_WIDTH


    def gather_heads(x):
        x = lax.all_to_all(x, "head", split_axis=0, concat_axis=0, tiled=True)
        return x.reshape(rows_per_rank, x.shape[2])

    kv = gather_heads(pack((keys, values), ((0, key_width), (0, key_width)), head_count))
    halo = lax.ppermute(
        kv[BLOCK:], "ctx", [(i, (i + 1) % ctx_count) for i in range(ctx_count)]
    )
    keys, turned = prepare(kv, halo)
    q = gather_heads(pack((queries,), ((0, query_width),), head_count))

    own_blocks = rank_index * blocks + jnp.arange(blocks, dtype=jnp.int32)
    holds = (doc_start[None, :] <= own_blocks[:, None]) & (
        own_blocks[:, None] < (doc_start + doc_blocks)[None, :]
    )
    lengths = own_blocks + 1 - jnp.sum(jnp.where(holds, doc_start[None, :], 0), axis=1)

    new_blocks = jnp.arange(ctx_count * blocks, dtype=jnp.int32)
    first_new = doc_rank * blocks + doc_slot
    lands = (first_new[None, :] <= new_blocks[:, None]) & (
        new_blocks[:, None] < (first_new + doc_blocks)[None, :]
    )
    sources = new_blocks + jnp.sum(
        jnp.where(lands, (doc_start - first_new)[None, :], 0), axis=1
    )

    dealt = attend(lengths, q, keys, turned)
    dealt = lax.all_to_all(dealt, "ctx", split_axis=0, concat_axis=0, tiled=True)
    dealt = dealt.reshape(ctx_count * blocks, 2 * QUAD, HEAD_WIDTH)
    moved = route(sources, dealt)
    parts = tokens // HALF
    moved = moved.reshape(ctx_count * head_count, parts, QUAD, HEAD_WIDTH)
    placed = lax.all_to_all(moved, ("ctx", "head"), split_axis=0, concat_axis=0, tiled=True)
    placed = placed.reshape(heads, HALF // QUAD, head_count, parts, QUAD, HEAD_WIDTH)
    settled = settle(placed)
    settled = settled.reshape(settled.shape[:2] + (2 * QUAD, HEAD_WIDTH))
    return settled.transpose(0, 2, 1, 3).reshape(tokens, queries.shape[1])


def solution(mesh):
    return jax.shard_map(
        on_device,
        mesh=mesh,
        in_specs=(
            P(("ctx", "head"), None),
            P(("ctx", "head"), None),
            P(("ctx", "head"), None),
            P(),
            P(),
            P(),
            P(),
        ),
        out_specs=P(("ctx", "head"), None),
        check_vma=False,
    )
```

time: 213 us -> 201 us (0.944)
  Pallas kernels: 31.2 us -> 20.7 us
    pallas_call x2 -> x3, Pallas kernels: 23.6 us -> 14.8 us  [the longest x1 10.5 us: attend(): pl.pallas_call(attend_kernel, out_shape=jax.ShapeDtypeStruct((units, bloc...]
    ppermute x1, waiting for transfers between devices: 0.01 us -> 8.26 us  [on_device(): lax.ppermute(kv[BLOCK:], 'ctx', [(i, (i + 1) % ctx_count) for i in range(...]
    all_to_all x3 -> x2, waiting for transfers between devices: 48.6 us -> 41 us  [gather_heads(): x = lax.all_to_all(x, 'head', split_axis=0, concat_axis=0, tiled=True)]
    reshape x2 -> x0, local copies, waits for them, and re-layouts: 3.61 us -> none  [the longest x1 2.39 us: on_device(): return placed.transpose(3, 1, 4, 2, 0, 5).reshape(tokens, queries.shape[1])]
    all_to_all x3 -> x2, starting transfers between devices: 18 us -> 14.5 us  [gather_heads(): x = lax.all_to_all(x, 'head', split_axis=0, concat_axis=0, tiled=True)]
    pallas_call x3 -> x2, Pallas kernels: 6 us -> 4.29 us  [pack(): pl.pallas_call(functools.partial(pack_kernel, pieces=pieces), out_shape=j...]
  transfers between devices with their start and end apart: 5 -> 4, of which waited for: 4 -> 4; matrix products, arithmetic and copies ran while one was open for 0% -> 1% of each run, Pallas kernels for 8% -> 2%
where the time goes in v4:
time: 201 us; the launch traced here: 200 us
  waiting for transfers between devices  88.9 us (44%)
  blocking collectives  53.3 us (27%)
  starting transfers between devices  31.8 us (16%)
  Pallas kernels  20.7 us (10%)
  local copies, waits for them, and re-layouts  4.89 us (2%)
    all_to_all x1, blocking collectives, on_device(): lax.all_to_all(moved, ('ctx', 'head'), split_axis=0, concat_axis=0, tiled...  53.3 us
    all_to_all x2, waiting for transfers between devices, gather_heads(): x = lax.all_to_all(x, 'head', split_axis=0, concat_axis=0, tiled=True)  41 us
    all_to_all x1, waiting for transfers between devices, on_device(): lax.all_to_all(dealt, 'ctx', split_axis=0, concat_axis=0, tiled=True)  39.6 us
    all_to_all x2, starting transfers between devices, gather_heads(): x = lax.all_to_all(x, 'head', split_axis=0, concat_axis=0, tiled=True)  14.5 us
    all_to_all x1, starting transfers between devices, on_device(): lax.all_to_all(dealt, 'ctx', split_axis=0, concat_axis=0, tiled=True)  13.7 us
    pallas_call x1, Pallas kernels, attend(): pl.pallas_call(attend_kernel, out_shape=jax.ShapeDtypeStruct((units, bloc...  10.5 us
    ppermute x1, waiting for transfers between devices, on_device(): lax.ppermute(kv[BLOCK:], 'ctx', [(i, (i + 1) % ctx_count) for i in range(...  8.26 us
    pallas_call x2, Pallas kernels, pack(): pl.pallas_call(functools.partial(pack_kernel, pieces=pieces), out_shape=j...  4.29 us
  transfers between devices with their start and end apart: 4, of which 4 were waited for; matrix products, arithmetic and copies ran while one was open for 1% of the time, Pallas kernels for 2%

profile of v4, /device:TPU:1, one launch (start us, length us, event | category | flops | bytes accessed | tf_op | source)
XLA Modules:
  0.0 200.2 jit_solution(10717650727613092371)
XLA Ops:
  0.0 2.0 pack.3
  2.0 10.9 %all-to-all-start.1 = ((bf16[8,192,256]{2,1,0:T(8,128)(2,1)}), bf16[8,192,256]{2,1,0:T(8,128)(2,1)S(1)}, u32[]{:S(2)}, u32[]{:S(2)}) async-start(bf16[8,192,256]{2,1,0:T(8,128)(2,1)} %pack.3), calls=%async_computation.1 | async-start | bytes 1572864 | tf_op jit(solution)/shard_map/all_to_all | solution.py:269
  12.9 2.3 %pack.2 = bf16[8,192,512]{2,1,0:T(8,128)(2,1)} custom-call(bf16[192,4096]{1,0:T(8,128)(2,1)} %refs_0_.2), custom_call_target="tpu_custom_call" | custom-call | tf_op jit(solution)/shard_map/pack/pallas_call | solution.py:52
  15.2 0.0 copy-start.4
  15.2 0.0 copy-start.5
  15.2 0.0 copy-start.6
  15.2 0.0 copy-start.7
  15.2 21.2 %all-to-all-done.1 = bf16[8,192,256]{2,1,0:T(8,128)(2,1)S(1)} async-done(((bf16[8,192,256]{2,1,0:T(8,128)(2,1)}), bf16[8,192,256]{2,1,0:T(8,128)(2,1)S(1)}, u32[]{:S(2)}, u32[]{:S(2)}) %all-to-all-start.1) | async-done | bytes 786464 | tf_op jit(solution)/shard_map/all_to_all | solution.py:269
  36.5 3.6 %all-to-all-start = ((bf16[8,192,512]{2,1,0:T(8,128)(2,1)}), bf16[8,192,512]{2,1,0:T(8,128)(2,1)S(1)}, u32[]{:S(2)}, u32[]{:S(2)}) async-start(bf16[8,192,512]{2,1,0:T(8,128)(2,1)} %pack.2), calls=%async_computation | async-start | bytes 3145728 | tf_op jit(solution)/shard_map/all_to_all | solution.py:269
  40.0 0.9 slice.4
  41.0 3.6 %collective-permute-start = (bf16[1408,256]{1,0:T(8,128)(2,1)}, bf16[1408,256]{1,0:T(8,128)(2,1)S(1)}, u32[]{:S(2)}, u32[]{:S(2)}) collective-permute-start(bf16[1408,256]{1,0:T(8,128)(2,1)} %slice.4), channel_id=1, source_target_pairs={{0,8},{8,16},{16,24},{24,32},{32,40},{40,48},{48,56},{56,64},{64,7... | collective-permute-start | bytes 2162696 | tf_op jit(solution)/shard_map/ppermute | solution.py:273
  44.5 0.0 copy-done.4
  44.6 0.0 copy-done.5
  44.6 0.0 copy-done.6
  44.6 0.0 copy-done.7
  44.6 0.2 select_reduce_fusion.1
  44.8 8.3 %collective-permute-done.halo_ref = bf16[1408,256]{1,0:T(8,128)(2,1)S(1)} collective-permute-done((bf16[1408,256]{1,0:T(8,128)(2,1)}, bf16[1408,256]{1,0:T(8,128)(2,1)S(1)}, u32[]{:S(2)}, u32[]{:S(2)}) %collective-permute-start) | collective-permute-done | bytes 720928 | tf_op jit(solution)/shard_map/ppermute | solution.py:273
  53.1 0.0 copy-start.2
  53.1 0.9 copy-done.2
  53.9 1.1 copy-done.3
  55.0 2.5 %prepare.1 = (bf16[2944,128]{1,0:T(8,128)(2,1)S(1)}, bf16[23,128,128]{2,1,0:T(8,128)(2,1)S(1)}) custom-call(bf16[1536,256]{1,0:T(8,128)(2,1)S(1)} %bitcast.11, bf16[1408,256]{1,0:T(8,128)(2,1)S(1)} %copy-done.3), custom_call_target="tpu_custom_call" | custom-call | tf_op jit(solution)/shard_map/prepare/pallas_call | solution.py:87
  57.5 0.0 copy-start
  57.5 0.9 copy-done
  58.4 19.8 %all-to-all-done = bf16[8,192,512]{2,1,0:T(8,128)(2,1)S(1)} async-done(((bf16[8,192,512]{2,1,0:T(8,128)(2,1)}), bf16[8,192,512]{2,1,0:T(8,128)(2,1)S(1)}, u32[]{:S(2)}, u32[]{:S(2)}) %all-to-all-start) | async-done | bytes 1572896 | tf_op jit(solution)/shard_map/all_to_all | solution.py:269
  78.2 1.1 copy-done.1
  79.3 10.5 %attend.1 = bf16[64,12,8,128]{3,2,1,0:T(8,128)(2,1)} custom-call(s32[12]{0:T(128)S(1)} %add_subtract_fusion.lengths, bf16[1536,512]{1,0:T(8,128)(2,1)S(1)} %bitcast.15, bf16[2944,128]{1,0:T(8,128)(2,1)S(1)} %get-tuple-element.7.key_ref, bf16[23,128,128]{2,1,0:T(8,128)(2,1)S(1)} %copy-done.1), custom_call_target="tpu_custom_call" | custom-call | tf_op jit(solution)/shard_map/attend/pallas_call | solution.py:189
  89.9 13.7 %all-to-all-start.2 = ((bf16[64,12,8,128]{3,2,1,0:T(8,128)(2,1)}), bf16[64,12,8,128]{3,2,1,0:T(8,128)(2,1)S(1)}, u32[]{:S(2)}, u32[]{:S(2)}) async-start(bf16[64,12,8,128]{3,2,1,0:T(8,128)(2,1)} %attend.1), calls=%async_computation.2 | async-start | bytes 3145728 | tf_op jit(solution)/shard_map/all_to_all | solution.py:295
  103.6 0.2 select_reduce_fusion
  103.8 39.6 %all-to-all-done.2 = bf16[64,12,8,128]{3,2,1,0:T(8,128)(2,1)S(1)} async-done(((bf16[64,12,8,128]{3,2,1,0:T(8,128)(2,1)}), bf16[64,12,8,128]{3,2,1,0:T(8,128)(2,1)S(1)}, u32[]{:S(2)}, u32[]{:S(2)}) %all-to-all-start.2) | async-done | bytes 1572896 | tf_op jit(solution)/shard_map/all_to_all | solution.py:295
  143.4 1.6 route.1
  145.0 53.3 %all_to_all.20 = bf16[512,3,4,128]{3,2,1,0:T(4,128)(2,1)S(1)} all-to-all(bf16[512,3,4,128]{3,2,1,0:T(4,128)(2,1)S(1)} %bitcast.13), channel_id=1, replica_groups=mesh['ctx'=64,'head'=8] {'ctx','head'}, dimensions={0} | all-to-all | bytes 3145728 | tf_op jit(solution)/shard_map/all_to_all | solution.py:300
  198.3 1.8 settle.1
  (7 shorter events, 0.0 us)
Async XLA Ops:
  2.0 34.5 %all-to-all-start.1 = ((bf16[8,192,256]{2,1,0:T(8,128)(2,1)}), bf16[8,192,256]{2,1,0:T(8,128)(2,1)S(1)}, u32[]{:S(2)}, u32[]{:S(2)}) async-start(bf16[8,192,256]{2,1,0:T(8,128)(2,1)} %pack.3), calls=%async_computation.1 | async-start | bytes 1572864 | tf_op jit(solution)/shard_map/all_to_all | solution.py:269
  15.2 29.4 %copy-start.4 = (s32[256]{0:T(256)S(1)}, s32[256]{0:T(256)}, u32[]{:S(2)}) copy-start(s32[256]{0:T(256)} %param.10) | copy-start | bytes 3076
  15.2 29.4 %copy-start.5 = (s32[256]{0:T(256)S(1)}, s32[256]{0:T(256)}, u32[]{:S(2)}) copy-start(s32[256]{0:T(256)} %param.11) | copy-start | bytes 3076
  15.2 29.4 %copy-start.6 = (s32[256]{0:T(256)S(1)}, s32[256]{0:T(256)}, u32[]{:S(2)}) copy-start(s32[256]{0:T(256)} %param.13) | copy-start | bytes 3076
  15.2 29.4 %copy-start.7 = (s32[256]{0:T(256)S(1)}, s32[256]{0:T(256)}, u32[]{:S(2)}) copy-start(s32[256]{0:T(256)} %param.12) | copy-start | bytes 3076
  36.5 41.7 %all-to-all-start = ((bf16[8,192,512]{2,1,0:T(8,128)(2,1)}), bf16[8,192,512]{2,1,0:T(8,128)(2,1)S(1)}, u32[]{:S(2)}, u32[]{:S(2)}) async-start(bf16[8,192,512]{2,1,0:T(8,128)(2,1)} %pack.2), calls=%async_computation | async-start | bytes 3145728 | tf_op jit(solution)/shard_map/all_to_all | solution.py:269
  41.0 12.1 %collective-permute-start = (bf16[1408,256]{1,0:T(8,128)(2,1)}, bf16[1408,256]{1,0:T(8,128)(2,1)S(1)}, u32[]{:S(2)}, u32[]{:S(2)}) collective-permute-start(bf16[1408,256]{1,0:T(8,128)(2,1)} %slice.4), channel_id=1, source_target_pairs={{0,8},{8,16},{16,24},{24,32},{32,40},{40,48},{48,56},{56,64},{64,7... | collective-permute-start | bytes 2162696 | tf_op jit(solution)/shard_map/ppermute | solution.py:273
  53.1 0.9 copy-start.2
  53.9 1.1 copy-start.3
  57.5 0.9 copy-start
  78.2 1.1 copy-start.1
  89.9 53.5 %all-to-all-start.2 = ((bf16[64,12,8,128]{3,2,1,0:T(8,128)(2,1)}), bf16[64,12,8,128]{3,2,1,0:T(8,128)(2,1)S(1)}, u32[]{:S(2)}, u32[]{:S(2)}) async-start(bf16[64,12,8,128]{3,2,1,0:T(8,128)(2,1)} %attend.1), calls=%async_computation.2 | async-start | bytes 3145728 | tf_op jit(solution)/shard_map/all_to_all | solution.py:295

commit v5 on v4

--- a/solution.py
+++ b/solution.py
@@ -63,6 +63,72 @@
     )(*arrays)
 
 
+def pack_turns_kernel(at, source, *refs):
+    outs = refs[:-3]
+    packed_ref, in_sems, out_sems = refs[-3:]
+    groups = len(outs)
+    width = packed_ref.shape[2]
+    pitch = source.shape[1] // groups
+    loads = []
+    stores = []
+    for k in range(groups):
+        group = lax.rem(at[0] + k, groups)
+        first = pl.multiple_of(group * pitch + (pitch - width), HEAD_WIDTH)
+        loads.append(
+            pltpu.make_async_copy(
+                source.at[:, pl.ds(first, width)], packed_ref.at[k], in_sems.at[k]
+            )
+        )
+        stores.append(pltpu.make_async_copy(packed_ref.at[k], outs[k], out_sems.at[k]))
+    for load in loads:
+        load.start()
+    for load, store in zip(loads, stores):
+        load.wait()
+        store.start()
+    for store in stores:
+        store.wait()
+
+
+def pack_turns(at, array, width, groups):
+    shape = (array.shape[0], width)
+    hbm = pl.BlockSpec(memory_space=pl.ANY)
+    return pl.pallas_call(
+        pack_turns_kernel,
+        out_shape=(jax.ShapeDtypeStruct(shape, array.dtype),) * groups,
+        in_specs=[pl.BlockSpec(memory_space=pltpu.SMEM), hbm],
+        out_specs=(hbm,) * groups,
+        scratch_shapes=[
+            pltpu.VMEM((groups,) + shape, array.dtype),
+            pltpu.SemaphoreType.DMA((groups,)),
+            pltpu.SemaphoreType.DMA((groups,)),
+        ],
+        name="pack_turns",
+    )(at, array)
+
+
+def join_kernel(at, *refs):
+    pieces = refs[:-1]
+    out_ref = refs[-1]
+    groups = len(pieces)
+    rows = pieces[0].shape[0]
+    for k in range(groups):
+        first = pl.multiple_of(lax.rem(at[0] + groups - k, groups) * rows, HALF)
+        out_ref[pl.ds(first, rows), :] = pieces[k][...]
+
+
+def join(at, pieces):
+    rows, width = pieces[0].shape
+    vmem = pl.BlockSpec(memory_space=pltpu.VMEM)
+    return pl.pallas_call(
+        join_kernel,
+        out_shape=jax.ShapeDtypeStruct((rows * len(pieces), width), pieces[0].dtype),
+        in_specs=[pl.BlockSpec(memory_space=pltpu.SMEM)] + [vmem] * len(pieces),
+        out_specs=vmem,
+        compiler_params=pltpu.CompilerParams(vmem_limit_bytes=8 << 20),
+        name="join",
+    )(at, *pieces)
+
+
 def prepare_kernel(kv_ref, halo_ref, key_ref, turned_ref):
     before = halo_ref.shape[0]
     key_ref[:before] = halo_ref[:, :HEAD_WIDTH]
@@ -98,7 +164,7 @@
 
 
 def attend_kernel(
-    lengths, q_ref, key_ref, turned_ref, out_hbm, order_ref, acc_ref, result_ref, sems
+    lengths, q_ref, key_ref, turned_ref, out_hbm, order_ref, acc_ref, result_ref, sems, *, flip
 ):
     heads = q_ref.shape[1] // HEAD_WIDTH
     rows = heads * BLOCK
@@ -111,9 +177,9 @@
             result_ref.at[block + 1], out_hbm.at[:, block], sems.at[block]
         )
 
-    out_ids = lax.broadcasted_iota(jnp.int32, (BLOCK, BLOCK), 0)
-    from_ids = out_ids // (2 * QUAD) * QUAD + out_ids % (2 * QUAD) // QUAD * HALF + out_ids % QUAD
-    query_ids = lax.broadcasted_iota(jnp.int32, (BLOCK, BLOCK), 1)
+    out_ids = lax.broadcasted_iota(jnp.int32, (2 * BLOCK, BLOCK), 0)
+    from_ids = out_ids // (2 * QUAD) * QUAD + out_ids % QUAD
+    query_ids = lax.broadcasted_iota(jnp.int32, (2 * BLOCK, BLOCK), 1)
     order_ref[...] = (from_ids == query_ids).astype(jnp.bfloat16)
 
     def finish(slot):
@@ -125,9 +191,10 @@
                 (((1,), (1,)), ((), ())),
                 preferred_element_type=jnp.float32,
             )
-            result_ref[slot, h * quads : (h + 1) * quads] = placed.reshape(
-                quads, 2 * QUAD, HEAD_WIDTH
-            ).astype(jnp.bfloat16)
+            placed = placed.reshape(2 * quads, 2 * QUAD, HEAD_WIDTH)[:, :QUAD].astype(jnp.bfloat16)
+            for half in range(2):
+                first = ((half + flip) % 2 * heads + h) * quads
+                result_ref[slot, first : first + quads] = placed[half * quads : (half + 1) * quads]
 
     def window(block, length, size):
         finish(block)
@@ -180,19 +247,19 @@
         store_of(block).wait()
 
 
-def attend(lengths, q, keys, turned):
+def attend(lengths, q, keys, turned, flip):
     blocks = q.shape[0] // BLOCK
     heads = q.shape[1] // HEAD_WIDTH
-    units = HALF // QUAD * heads
+    units = BLOCK // QUAD * heads
     vmem = pl.BlockSpec(memory_space=pltpu.VMEM)
-    tile = (2 * QUAD, HEAD_WIDTH)
-    return pl.pallas_call(
-        attend_kernel,
+    tile = (QUAD, HEAD_WIDTH)
+    return pl.pallas_call(
+        functools.partial(attend_kernel, flip=flip),
         out_shape=jax.ShapeDtypeStruct((units, blocks) + tile, jnp.bfloat16),
         in_specs=[pl.BlockSpec(memory_space=pltpu.SMEM), vmem, vmem, vmem],
         out_specs=pl.BlockSpec(memory_space=pl.ANY),
         scratch_shapes=[
-            pltpu.VMEM((BLOCK, BLOCK), jnp.bfloat16),
+            pltpu.VMEM((2 * BLOCK, BLOCK), jnp.bfloat16),
             pltpu.VMEM((HEAD_WIDTH, heads * BLOCK), jnp.bfloat16),
             pltpu.VMEM((blocks + 1, units) + tile, jnp.bfloat16),
             pltpu.SemaphoreType.DMA((blocks,)),
@@ -202,55 +269,72 @@
     )(lengths, q, keys, turned)
 
 
-def route_kernel(index, x_ref, y_ref):
-    def step(n, carry):
-        for u in range(16):
-            y_ref[n * 16 + u] = x_ref[index[n * 16 + u]]
-        return carry
-
-    lax.fori_loop(0, y_ref.shape[0] // 16, step, 0)
-
-
-def route(index, x):
+def route_kernel(index, upper_half, first_ref, second_ref, y_ref):
+    def copy_from(refs):
+        def step(n, carry):
+            for u in range(8):
+                block = n * 8 + u
+                source = index[block]
+                y_ref[2 * block] = refs[0][source]
+                y_ref[2 * block + 1] = refs[1][source]
+            return carry
+
+        lax.fori_loop(0, first_ref.shape[0] // 8, step, 0)
+
+    @pl.when(upper_half[0] == 0)
+    def _():
+        copy_from((first_ref, second_ref))
+
+    @pl.when(upper_half[0] != 0)
+    def _():
+        copy_from((second_ref, first_ref))
+
+
+def route(index, upper_half, first, second):
     vmem = pl.BlockSpec(memory_space=pltpu.VMEM)
+    smem = pl.BlockSpec(memory_space=pltpu.SMEM)
     return pl.pallas_call(
         route_kernel,
-        out_shape=jax.ShapeDtypeStruct(x.shape, x.dtype),
-        in_specs=[pl.BlockSpec(memory_space=pltpu.SMEM), vmem],
+        out_shape=jax.ShapeDtypeStruct((2 * first.shape[0],) + first.shape[1:], first.dtype),
+        in_specs=[smem, smem, vmem, vmem],
         out_specs=vmem,
         compiler_params=pltpu.CompilerParams(vmem_limit_bytes=8 << 20),
         name="route",
-    )(index, x)
-
-
-def settle_kernel(x_ref, y_ref):
-    heads, quads, groups, parts = x_ref.shape[:4]
+    )(index, upper_half, first, second)
+
+
+def settle_kernel(at, x_ref, y_ref):
+    swaps, heads, quads, groups, parts = x_ref.shape[:5]
 
     def step(n, carry):
         half = n % 2
         pair = n // 2
         for p in range(parts):
-            for g in range(groups):
-                for h in range(heads):
-                    y_ref[p * (quads // 2) + pair, g * heads + h, half] = x_ref[h, n, g, p]
+            odd = (at[0] + p) % 2
+            for c in range(swaps):
+                side = lax.rem(odd + c, swaps)
+                for g in range(groups):
+                    for h in range(heads):
+                        lane = (g * swaps + c) * heads + h
+                        y_ref[p * (quads // 2) + pair, lane, half] = x_ref[side, h, n, g, p]
         return carry
 
     lax.fori_loop(0, quads, step, 0)
 
 
-def settle(x):
-    heads, quads, groups, parts = x.shape[:4]
+def settle(at, x):
+    swaps, heads, quads, groups, parts = x.shape[:5]
     vmem = pl.BlockSpec(memory_space=pltpu.VMEM)
     return pl.pallas_call(
         settle_kernel,
         out_shape=jax.ShapeDtypeStruct(
-            (parts * quads // 2, groups * heads, 2) + x.shape[4:], x.dtype
+            (parts * quads // 2, groups * swaps * heads, 2) + x.shape[5:], x.dtype
         ),
-        in_specs=[vmem],
+        in_specs=[pl.BlockSpec(memory_space=pltpu.SMEM), vmem],
         out_specs=vmem,
         compiler_params=pltpu.CompilerParams(vmem_limit_bytes=8 << 20),
         name="settle",
-    )(x)
+    )(at, x)
 
 
 def on_device(queries, keys, values, doc_start, doc_blocks, doc_rank, doc_slot):
@@ -274,7 +358,10 @@
         kv[BLOCK:], "ctx", [(i, (i + 1) % ctx_count) for i in range(ctx_count)]
     )
     keys, turned = prepare(kv, halo)
-    q = gather_heads(pack((queries,), ((0, query_width),), head_count))
+    half_width = query_width // 2
+    place = jnp.reshape(lax.axis_index("head"), (1,))
+    q_first = gather_heads(pack((queries,), ((0, half_width),), head_count))
+    pieces = pack_turns(place, queries, half_width, head_count)
 
     own_blocks = rank_index * blocks + jnp.arange(blocks, dtype=jnp.int32)
     holds = (doc_start[None, :] <= own_blocks[:, None]) & (
@@ -291,15 +378,27 @@
         jnp.where(lands, (doc_start - first_new)[None, :], 0), axis=1
     )
 
-    dealt = attend(lengths, q, keys, turned)
-    dealt = lax.all_to_all(dealt, "ctx", split_axis=0, concat_axis=0, tiled=True)
-    dealt = dealt.reshape(ctx_count * blocks, 2 * QUAD, HEAD_WIDTH)
-    moved = route(sources, dealt)
+    def deal(x):
+        x = lax.all_to_all(x, "ctx", split_axis=0, concat_axis=0, tiled=True)
+        return x.reshape(ctx_count * blocks, QUAD, HEAD_WIDTH)
+
+    done = attend(lengths, q_first, keys, turned, 0)
+    done, *pieces = lax.optimization_barrier((done, *pieces))
+    first = deal(done)
+    pieces = [pieces[0]] + [
+        lax.ppermute(
+            pieces[k], "head", [(i, (i + k) % head_count) for i in range(head_count)]
+        )
+        for k in range(1, head_count)
+    ]
+    second = deal(attend(lengths, join(place, pieces), keys, turned, 1))
+    upper_half = jnp.reshape(rank_index // (ctx_count // 2), (1,))
+    moved = route(sources, upper_half, first, second)
     parts = tokens // HALF
     moved = moved.reshape(ctx_count * head_count, parts, QUAD, HEAD_WIDTH)
     placed = lax.all_to_all(moved, ("ctx", "head"), split_axis=0, concat_axis=0, tiled=True)
-    placed = placed.reshape(heads, HALF // QUAD, head_count, parts, QUAD, HEAD_WIDTH)
-    settled = settle(placed)
+    placed = placed.reshape(2, heads // 2, HALF // QUAD, head_count, parts, QUAD, HEAD_WIDTH)
+    settled = settle(place, placed)
     settled = settled.reshape(settled.shape[:2] + (2 * QUAD, HEAD_WIDTH))
     return settled.transpose(0, 2, 1, 3).reshape(tokens, queries.shape[1])
 

time: 201 us -> 218 us (1.085)
  starting transfers between devices: 31.8 us -> 63 us
  waiting for transfers between devices: 88.9 us -> 66 us
  Pallas kernels: 20.7 us -> 29.9 us
  local copies, waits for them, and re-layouts: 4.89 us -> 2.08 us
  blocking collectives: 53.3 us -> 55.7 us
    ppermute x0 -> x7, starting transfers between devices: none -> 23.2 us  [on_device(): lax.ppermute(pieces[k], 'head', [(i, (i + k) % head_count) for i in range...]
    all_to_all x1 -> x2, waiting for transfers between devices: 39.6 us -> 22.7 us  [deal(): x = lax.all_to_all(x, 'ctx', split_axis=0, concat_axis=0, tiled=True)]
    all_to_all x2, waiting for transfers between devices: 41 us -> 28.7 us  [gather_heads(): x = lax.all_to_all(x, 'head', split_axis=0, concat_axis=0, tiled=True)]
    pallas_call x2 -> x5, Pallas kernels: 12.2 us -> 21.3 us  [the longest x2 17.2 us: attend(): pl.pallas_call(functools.partial(attend_kernel, flip=flip), out_shape=jax...]
    ppermute x0 -> x7, waiting for transfers between devices: none -> 8.64 us  [on_device(): lax.ppermute(pieces[k], 'head', [(i, (i + k) % head_count) for i in range...]
    all_to_all x1 -> x2, starting transfers between devices: 13.7 us -> 21.8 us  [deal(): x = lax.all_to_all(x, 'ctx', split_axis=0, concat_axis=0, tiled=True)]
    all_to_all x1, blocking collectives: 53.3 us -> 55.7 us  [on_device(): lax.all_to_all(moved, ('ctx', 'head'), split_axis=0, concat_axis=0, tiled...]
    ppermute x1, waiting for transfers between devices: 8.26 us -> 5.93 us  [on_device(): lax.ppermute(kv[BLOCK:], 'ctx', [(i, (i + 1) % ctx_count) for i in range(...]
  transfers between devices with their start and end apart: 4 -> 12, of which waited for: 4 -> 6; matrix products, arithmetic and copies ran while one was open for 1% -> 0% of each run, Pallas kernels for 2% -> 7%
where the time goes in v5:
time: 218 us
  waiting for transfers between devices  66 us (30%)
  starting transfers between devices  63 us (29%)
  blocking collectives  55.7 us (26%)
  Pallas kernels  29.9 us (14%)
    all_to_all x1, blocking collectives, on_device(): lax.all_to_all(moved, ('ctx', 'head'), split_axis=0, concat_axis=0, tiled...  55.7 us
    all_to_all x2, waiting for transfers between devices, gather_heads(): x = lax.all_to_all(x, 'head', split_axis=0, concat_axis=0, tiled=True)  28.7 us
    ppermute x7, starting transfers between devices, on_device(): lax.ppermute(pieces[k], 'head', [(i, (i + k) % head_count) for i in range...  23.2 us
    all_to_all x2, waiting for transfers between devices, deal(): x = lax.all_to_all(x, 'ctx', split_axis=0, concat_axis=0, tiled=True)  22.7 us
    all_to_all x2, starting transfers between devices, deal(): x = lax.all_to_all(x, 'ctx', split_axis=0, concat_axis=0, tiled=True)  21.8 us
    pallas_call x2, Pallas kernels, attend(): pl.pallas_call(functools.partial(attend_kernel, flip=flip), out_shape=jax...  17.2 us
    all_to_all x2, starting transfers between devices, gather_heads(): x = lax.all_to_all(x, 'head', split_axis=0, concat_axis=0, tiled=True)  14.4 us
    ppermute x7, waiting for transfers between devices, on_device(): lax.ppermute(pieces[k], 'head', [(i, (i + k) % head_count) for i in range...  8.64 us
  transfers between devices with their start and end apart: 12, of which 6 were waited for; matrix products, arithmetic and copies ran while one was open for 0% of the time, Pallas kernels for 7%

profile of v5, /device:TPU:1, one launch (start us, length us, event | category | flops | bytes accessed | tf_op | source)
XLA Modules:
  0.0 217.6 jit_solution(6643705345551243162)
XLA Ops:
  0.0 2.0 pack.3
  2.0 10.9 %all-to-all-start.1 = ((bf16[8,192,256]{2,1,0:T(8,128)(2,1)}), bf16[8,192,256]{2,1,0:T(8,128)(2,1)S(1)}, u32[]{:S(2)}, u32[]{:S(2)}) async-start(bf16[8,192,256]{2,1,0:T(8,128)(2,1)} %pack.3), calls=%async_computation.1 | async-start | bytes 1572864 | tf_op jit(solution)/shard_map/all_to_all | solution.py:353
  12.9 2.0 pack.2
  14.9 21.6 %all-to-all-done.1 = bf16[8,192,256]{2,1,0:T(8,128)(2,1)S(1)} async-done(((bf16[8,192,256]{2,1,0:T(8,128)(2,1)}), bf16[8,192,256]{2,1,0:T(8,128)(2,1)S(1)}, u32[]{:S(2)}, u32[]{:S(2)}) %all-to-all-start.1) | async-done | bytes 786464 | tf_op jit(solution)/shard_map/all_to_all | solution.py:353
  36.5 3.5 %all-to-all-start = ((bf16[8,192,256]{2,1,0:T(8,128)(2,1)}), bf16[8,192,256]{2,1,0:T(8,128)(2,1)S(1)}, u32[]{:S(2)}, u32[]{:S(2)}) async-start(bf16[8,192,256]{2,1,0:T(8,128)(2,1)} %pack.2), calls=%async_computation | async-start | bytes 1572864 | tf_op jit(solution)/shard_map/all_to_all | solution.py:353
  40.1 3.6 %collective-permute-start = (bf16[1408,256]{1,0:T(8,128)(2,1)S(1)}, bf16[1408,256]{1,0:T(8,128)(2,1)S(1)}, u32[]{:S(2)}, u32[]{:S(2)}) collective-permute-start(bf16[1408,256]{1,0:T(8,128)(2,1)S(1)} %slice.4), channel_id=1, source_target_pairs={{0,8},{8,16},{16,24},{24,32},{32,40},{40,48},{48,56},{56,64},{64,7... | collective-permute-start | bytes 2162696 | tf_op jit(solution)/shard_map/ppermute | solution.py:357
  43.7 2.0 pack_turns.1
  45.8 0.2 select_reduce_fusion.1
  46.0 5.9 %collective-permute-done.halo_ref = bf16[1408,256]{1,0:T(8,128)(2,1)S(1)} collective-permute-done((bf16[1408,256]{1,0:T(8,128)(2,1)S(1)}, bf16[1408,256]{1,0:T(8,128)(2,1)S(1)}, u32[]{:S(2)}, u32[]{:S(2)}) %collective-permute-start) | collective-permute-done | bytes 720928 | tf_op jit(solution)/shard_map/ppermute | solution.py:357
  51.9 0.9 copy-done
  52.8 1.1 copy-done.1
  53.9 2.5 %prepare.1 = (bf16[2944,128]{1,0:T(8,128)(2,1)S(1)}, bf16[23,128,128]{2,1,0:T(8,128)(2,1)S(1)}) custom-call(bf16[1536,256]{1,0:T(8,128)(2,1)S(1)} %bitcast.14, bf16[1408,256]{1,0:T(8,128)(2,1)S(1)} %copy-done.1), custom_call_target="tpu_custom_call" | custom-call | tf_op jit(solution)/shard_map/prepare/pallas_call | solution.py:153
  56.4 7.2 %all-to-all-done = bf16[8,192,256]{2,1,0:T(8,128)(2,1)S(1)} async-done(((bf16[8,192,256]{2,1,0:T(8,128)(2,1)}), bf16[8,192,256]{2,1,0:T(8,128)(2,1)S(1)}, u32[]{:S(2)}, u32[]{:S(2)}) %all-to-all-start) | async-done | bytes 786464 | tf_op jit(solution)/shard_map/all_to_all | solution.py:353
  63.6 8.6 %attend.2 = bf16[64,12,4,128]{3,2,1,0:T(4,128)(2,1)} custom-call(s32[12]{0:T(128)S(1)} %add_subtract_fusion.lengths, bf16[1536,256]{1,0:T(8,128)(2,1)S(1)} %bitcast.18, bf16[2944,128]{1,0:T(8,128)(2,1)S(1)} %get-tuple-element.24.key_ref, bf16[23,128,128]{2,1,0:T(8,128)(2,1)S(1)} %get-tuple-element.25.turned_ref), custom_call_target="tpu_custom_call" | custom-call | tf_op jit(solution)/shard_map/attend/pallas_call | solution.py:256
  72.2 10.7 %all-to-all-start.2 = ((bf16[64,12,4,128]{3,2,1,0:T(4,128)(2,1)}), bf16[64,12,4,128]{3,2,1,0:T(4,128)(2,1)S(1)}, u32[]{:S(2)}, u32[]{:S(2)}) async-start(bf16[64,12,4,128]{3,2,1,0:T(4,128)(2,1)} %attend.2), calls=%async_computation.2 | async-start | bytes 1572864 | tf_op jit(solution)/shard_map/all_to_all | solution.py:382
  83.0 2.0 collective-permute-start.1
  85.0 1.9 collective-permute-start.2
  86.9 4.2 %collective-permute-start.3 = (bf16[192,256]{1,0:T(8,128)(2,1)S(1)}, bf16[192,256]{1,0:T(8,128)(2,1)S(1)}, u32[]{:S(2)}, u32[]{:S(2)}) collective-permute-start(bf16[192,256]{1,0:T(8,128)(2,1)S(1)} %copy-done.11), channel_id=1, source_target_pairs={{0,3},{1,4},{2,5},{3,6},{4,7},{5,0},{6,1},{7,2},{8,11},{9,12},{10,... | collective-permute-start | bytes 294920 | tf_op jit(solution)/shard_map/ppermute | solution.py:389
  91.1 5.2 %collective-permute-start.4 = (bf16[192,256]{1,0:T(8,128)(2,1)S(1)}, bf16[192,256]{1,0:T(8,128)(2,1)S(1)}, u32[]{:S(2)}, u32[]{:S(2)}) collective-permute-start(bf16[192,256]{1,0:T(8,128)(2,1)S(1)} %copy-done.10), channel_id=1, source_target_pairs={{0,4},{1,5},{2,6},{3,7},{4,0},{5,1},{6,2},{7,3},{8,12},{9,13},{10,... | collective-permute-start | bytes 294920 | tf_op jit(solution)/shard_map/ppermute | solution.py:389
  96.4 2.8 %collective-permute-start.5 = (bf16[192,256]{1,0:T(8,128)(2,1)S(1)}, bf16[192,256]{1,0:T(8,128)(2,1)S(1)}, u32[]{:S(2)}, u32[]{:S(2)}) collective-permute-start(bf16[192,256]{1,0:T(8,128)(2,1)S(1)} %copy-done.9), channel_id=1, source_target_pairs={{0,5},{1,6},{2,7},{3,0},{4,1},{5,2},{6,3},{7,4},{8,13},{9,14},{10,... | collective-permute-start | bytes 294920 | tf_op jit(solution)/shard_map/ppermute | solution.py:389
  99.2 4.6 %collective-permute-start.6 = (bf16[192,256]{1,0:T(8,128)(2,1)S(1)}, bf16[192,256]{1,0:T(8,128)(2,1)S(1)}, u32[]{:S(2)}, u32[]{:S(2)}) collective-permute-start(bf16[192,256]{1,0:T(8,128)(2,1)S(1)} %copy-done.8), channel_id=1, source_target_pairs={{0,6},{1,7},{2,0},{3,1},{4,2},{5,3},{6,4},{7,5},{8,14},{9,15},{10,... | collective-permute-start | bytes 294920 | tf_op jit(solution)/shard_map/ppermute | solution.py:389
  103.9 2.4 %collective-permute-start.7 = (bf16[192,256]{1,0:T(8,128)(2,1)S(1)}, bf16[192,256]{1,0:T(8,128)(2,1)S(1)}, u32[]{:S(2)}, u32[]{:S(2)}) collective-permute-start(bf16[192,256]{1,0:T(8,128)(2,1)S(1)} %copy-done.7), channel_id=1, source_target_pairs={{0,7},{1,0},{2,1},{3,2},{4,3},{5,4},{6,5},{7,6},{8,15},{9,8},{10,9... | collective-permute-start | bytes 294920 | tf_op jit(solution)/shard_map/ppermute | solution.py:389
  106.3 5.4 %collective-permute-done.6.refs_6_ = bf16[192,256]{1,0:T(8,128)(2,1)S(1)} collective-permute-done((bf16[192,256]{1,0:T(8,128)(2,1)S(1)}, bf16[192,256]{1,0:T(8,128)(2,1)S(1)}, u32[]{:S(2)}, u32[]{:S(2)}) %collective-permute-start.6) | collective-permute-done | bytes 98336 | tf_op jit(solution)/shard_map/ppermute | solution.py:389
  111.7 3.3 %collective-permute-done.7.refs_7_ = bf16[192,256]{1,0:T(8,128)(2,1)S(1)} collective-permute-done((bf16[192,256]{1,0:T(8,128)(2,1)S(1)}, bf16[192,256]{1,0:T(8,128)(2,1)S(1)}, u32[]{:S(2)}, u32[]{:S(2)}) %collective-permute-start.7) | collective-permute-done | bytes 98336 | tf_op jit(solution)/shard_map/ppermute | solution.py:389
  114.9 0.1 join.1.q_ref
  115.0 8.6 %attend.3 = bf16[64,12,4,128]{3,2,1,0:T(4,128)(2,1)} custom-call(s32[12]{0:T(128)S(1)} %add_subtract_fusion.lengths, bf16[1536,256]{1,0:T(8,128)(2,1)S(1)} %join.1.q_ref, bf16[2944,128]{1,0:T(8,128)(2,1)S(1)} %get-tuple-element.24.key_ref, bf16[23,128,128]{2,1,0:T(8,128)(2,1)S(1)} %get-tuple-element.25.turned_ref), custom_call_target="tpu_custom_call" | custom-call | tf_op jit(solution)/shard_map/attend/pallas_call | solution.py:256
  123.6 11.1 %all-to-all-start.3 = ((bf16[64,12,4,128]{3,2,1,0:T(4,128)(2,1)}), bf16[64,12,4,128]{3,2,1,0:T(4,128)(2,1)S(1)}, u32[]{:S(2)}, u32[]{:S(2)}) async-start(bf16[64,12,4,128]{3,2,1,0:T(4,128)(2,1)} %attend.3), calls=%async_computation.3 | async-start | bytes 1572864 | tf_op jit(solution)/shard_map/all_to_all | solution.py:382
  134.7 0.2 select_reduce_fusion
  134.9 22.7 %all-to-all-done.3 = bf16[64,12,4,128]{3,2,1,0:T(4,128)(2,1)S(1)} async-done(((bf16[64,12,4,128]{3,2,1,0:T(4,128)(2,1)}), bf16[64,12,4,128]{3,2,1,0:T(4,128)(2,1)S(1)}, u32[]{:S(2)}, u32[]{:S(2)}) %all-to-all-start.3) | async-done | bytes 786464 | tf_op jit(solution)/shard_map/all_to_all | solution.py:382
  157.7 2.1 route.1
  159.7 55.7 %all_to_all.25 = bf16[512,3,4,128]{3,2,1,0:T(4,128)(2,1)S(1)} all-to-all(bf16[512,3,4,128]{3,2,1,0:T(4,128)(2,1)S(1)} %bitcast.15), channel_id=1, replica_groups=mesh['ctx'=64,'head'=8] {'ctx','head'}, dimensions={0} | all-to-all | bytes 3145728 | tf_op jit(solution)/shard_map/all_to_all | solution.py:399
  215.5 2.1 settle.1
  (38 shorter events, 0.2 us)
Async XLA Ops:
  2.0 34.5 %all-to-all-start.1 = ((bf16[8,192,256]{2,1,0:T(8,128)(2,1)}), bf16[8,192,256]{2,1,0:T(8,128)(2,1)S(1)}, u32[]{:S(2)}, u32[]{:S(2)}) async-start(bf16[8,192,256]{2,1,0:T(8,128)(2,1)} %pack.3), calls=%async_computation.1 | async-start | bytes 1572864 | tf_op jit(solution)/shard_map/all_to_all | solution.py:353
  36.5 27.1 %all-to-all-start = ((bf16[8,192,256]{2,1,0:T(8,128)(2,1)}), bf16[8,192,256]{2,1,0:T(8,128)(2,1)S(1)}, u32[]{:S(2)}, u32[]{:S(2)}) async-start(bf16[8,192,256]{2,1,0:T(8,128)(2,1)} %pack.2), calls=%async_computation | async-start | bytes 1572864 | tf_op jit(solution)/shard_map/all_to_all | solution.py:353
  40.0 5.7 %copy-start.3 = (s32[256]{0:T(256)S(1)}, s32[256]{0:T(256)}, u32[]{:S(2)}) copy-start(s32[256]{0:T(256)} %param.10) | copy-start | bytes 3076
  40.0 5.7 %copy-start.4 = (s32[256]{0:T(256)S(1)}, s32[256]{0:T(256)}, u32[]{:S(2)}) copy-start(s32[256]{0:T(256)} %param.11) | copy-start | bytes 3076
  40.0 5.7 %copy-start.5 = (s32[256]{0:T(256)S(1)}, s32[256]{0:T(256)}, u32[]{:S(2)}) copy-start(s32[256]{0:T(256)} %param.13) | copy-start | bytes 3076
  40.1 5.7 %copy-start.6 = (s32[256]{0:T(256)S(1)}, s32[256]{0:T(256)}, u32[]{:S(2)}) copy-start(s32[256]{0:T(256)} %param.12) | copy-start | bytes 3076
  40.1 11.8 %collective-permute-start = (bf16[1408,256]{1,0:T(8,128)(2,1)S(1)}, bf16[1408,256]{1,0:T(8,128)(2,1)S(1)}, u32[]{:S(2)}, u32[]{:S(2)}) collective-permute-start(bf16[1408,256]{1,0:T(8,128)(2,1)S(1)} %slice.4), channel_id=1, source_target_pairs={{0,8},{8,16},{16,24},{24,32},{32,40},{40,48},{48,56},{56,64},{64,7... | collective-permute-start | bytes 2162696 | tf_op jit(solution)/shard_map/ppermute | solution.py:357
  51.9 0.9 copy-start
  52.8 1.1 copy-start.1
  63.6 32.8 %copy-start.9 = (bf16[192,256]{1,0:T(8,128)(2,1)S(1)}, bf16[192,256]{1,0:T(8,128)(2,1)}, u32[]{:S(2)}) copy-start(bf16[192,256]{1,0:T(8,128)(2,1)} %get-tuple-element.40) | copy-start | bytes 294916
  63.6 35.6 %copy-start.8 = (bf16[192,256]{1,0:T(8,128)(2,1)S(1)}, bf16[192,256]{1,0:T(8,128)(2,1)}, u32[]{:S(2)}) copy-start(bf16[192,256]{1,0:T(8,128)(2,1)} %get-tuple-element.41) | copy-start | bytes 294916
  63.6 40.3 %copy-start.7 = (bf16[192,256]{1,0:T(8,128)(2,1)S(1)}, bf16[192,256]{1,0:T(8,128)(2,1)}, u32[]{:S(2)}) copy-start(bf16[192,256]{1,0:T(8,128)(2,1)} %get-tuple-element.42) | copy-start | bytes 294916
  63.6 51.4 %copy-start.2 = (bf16[192,256]{1,0:T(8,128)(2,1)S(1)}, bf16[192,256]{1,0:T(8,128)(2,1)}, u32[]{:S(2)}) copy-start(bf16[192,256]{1,0:T(8,128)(2,1)} %get-tuple-element.35.refs_0_) | copy-start | bytes 294916
  72.2 10.8 %copy-start.13 = (bf16[192,256]{1,0:T(8,128)(2,1)S(1)}, bf16[192,256]{1,0:T(8,128)(2,1)}, u32[]{:S(2)}) copy-start(bf16[192,256]{1,0:T(8,128)(2,1)} %get-tuple-element.36) | copy-start | bytes 294916
  72.2 12.8 %copy-start.12 = (bf16[192,256]{1,0:T(8,128)(2,1)S(1)}, bf16[192,256]{1,0:T(8,128)(2,1)}, u32[]{:S(2)}) copy-start(bf16[192,256]{1,0:T(8,128)(2,1)} %get-tuple-element.37) | copy-start | bytes 294916
  72.2 14.7 %copy-start.11 = (bf16[192,256]{1,0:T(8,128)(2,1)S(1)}, bf16[192,256]{1,0:T(8,128)(2,1)}, u32[]{:S(2)}) copy-start(bf16[192,256]{1,0:T(8,128)(2,1)} %get-tuple-element.38) | copy-start | bytes 294916
  72.2 18.9 %copy-start.10 = (bf16[192,256]{1,0:T(8,128)(2,1)S(1)}, bf16[192,256]{1,0:T(8,128)(2,1)}, u32[]{:S(2)}) copy-start(bf16[192,256]{1,0:T(8,128)(2,1)} %get-tuple-element.39) | copy-start | bytes 294916
  72.2 51.4 %all-to-all-start.2 = ((bf16[64,12,4,128]{3,2,1,0:T(4,128)(2,1)}), bf16[64,12,4,128]{3,2,1,0:T(4,128)(2,1)S(1)}, u32[]{:S(2)}, u32[]{:S(2)}) async-start(bf16[64,12,4,128]{3,2,1,0:T(4,128)(2,1)} %attend.2), calls=%async_computation.2 | async-start | bytes 1572864 | tf_op jit(solution)/shard_map/all_to_all | solution.py:382
  83.0 16.2 %collective-permute-start.1 = (bf16[192,256]{1,0:T(8,128)(2,1)S(1)}, bf16[192,256]{1,0:T(8,128)(2,1)S(1)}, u32[]{:S(2)}, u32[]{:S(2)}) collective-permute-start(bf16[192,256]{1,0:T(8,128)(2,1)S(1)} %copy-done.13), channel_id=1, source_target_pairs={{0,1},{1,2},{2,3},{3,4},{4,5},{5,6},{6,7},{7,0},{8,9},{9,10},{10,1... | collective-permute-start | bytes 294920 | tf_op jit(solution)/shard_map/ppermute | solution.py:389
  85.0 18.8 %collective-permute-start.2 = (bf16[192,256]{1,0:T(8,128)(2,1)S(1)}, bf16[192,256]{1,0:T(8,128)(2,1)S(1)}, u32[]{:S(2)}, u32[]{:S(2)}) collective-permute-start(bf16[192,256]{1,0:T(8,128)(2,1)S(1)} %copy-done.12), channel_id=1, source_target_pairs={{0,2},{1,3},{2,4},{3,5},{4,6},{5,7},{6,0},{7,1},{8,10},{9,11},{10,... | collective-permute-start | bytes 294920 | tf_op jit(solution)/shard_map/ppermute | solution.py:389
  86.9 19.3 %collective-permute-start.3 = (bf16[192,256]{1,0:T(8,128)(2,1)S(1)}, bf16[192,256]{1,0:T(8,128)(2,1)S(1)}, u32[]{:S(2)}, u32[]{:S(2)}) collective-permute-start(bf16[192,256]{1,0:T(8,128)(2,1)S(1)} %copy-done.11), channel_id=1, source_target_pairs={{0,3},{1,4},{2,5},{3,6},{4,7},{5,0},{6,1},{7,2},{8,11},{9,12},{10,... | collective-permute-start | bytes 294920 | tf_op jit(solution)/shard_map/ppermute | solution.py:389
  91.1 15.1 %collective-permute-start.4 = (bf16[192,256]{1,0:T(8,128)(2,1)S(1)}, bf16[192,256]{1,0:T(8,128)(2,1)S(1)}, u32[]{:S(2)}, u32[]{:S(2)}) collective-permute-start(bf16[192,256]{1,0:T(8,128)(2,1)S(1)} %copy-done.10), channel_id=1, source_target_pairs={{0,4},{1,5},{2,6},{3,7},{4,0},{5,1},{6,2},{7,3},{8,12},{9,13},{10,... | collective-permute-start | bytes 294920 | tf_op jit(solution)/shard_map/ppermute | solution.py:389
  96.4 9.9 %collective-permute-start.5 = (bf16[192,256]{1,0:T(8,128)(2,1)S(1)}, bf16[192,256]{1,0:T(8,128)(2,1)S(1)}, u32[]{:S(2)}, u32[]{:S(2)}) collective-permute-start(bf16[192,256]{1,0:T(8,128)(2,1)S(1)} %copy-done.9), channel_id=1, source_target_pairs={{0,5},{1,6},{2,7},{3,0},{4,1},{5,2},{6,3},{7,4},{8,13},{9,14},{10,... | collective-permute-start | bytes 294920 | tf_op jit(solution)/shard_map/ppermute | solution.py:389
  99.2 12.5 %collective-permute-start.6 = (bf16[192,256]{1,0:T(8,128)(2,1)S(1)}, bf16[192,256]{1,0:T(8,128)(2,1)S(1)}, u32[]{:S(2)}, u32[]{:S(2)}) collective-permute-start(bf16[192,256]{1,0:T(8,128)(2,1)S(1)} %copy-done.8), channel_id=1, source_target_pairs={{0,6},{1,7},{2,0},{3,1},{4,2},{5,3},{6,4},{7,5},{8,14},{9,15},{10,... | collective-permute-start | bytes 294920 | tf_op jit(solution)/shard_map/ppermute | solution.py:389
  103.9 11.1 %collective-permute-start.7 = (bf16[192,256]{1,0:T(8,128)(2,1)S(1)}, bf16[192,256]{1,0:T(8,128)(2,1)S(1)}, u32[]{:S(2)}, u32[]{:S(2)}) collective-permute-start(bf16[192,256]{1,0:T(8,128)(2,1)S(1)} %copy-done.7), channel_id=1, source_target_pairs={{0,7},{1,0},{2,1},{3,2},{4,3},{5,4},{6,5},{7,6},{8,15},{9,8},{10,9... | collective-permute-start | bytes 294920 | tf_op jit(solution)/shard_map/ppermute | solution.py:389
  123.6 34.0 %all-to-all-start.3 = ((bf16[64,12,4,128]{3,2,1,0:T(4,128)(2,1)}), bf16[64,12,4,128]{3,2,1,0:T(4,128)(2,1)S(1)}, u32[]{:S(2)}, u32[]{:S(2)}) async-start(bf16[64,12,4,128]{3,2,1,0:T(4,128)(2,1)} %attend.3), calls=%async_computation.3 | async-start | bytes 1572864 | tf_op jit(solution)/shard_map/all_to_all | solution.py:382

commit v6 on v4

--- a/solution.py
+++ b/solution.py
@@ -12,7 +12,7 @@
 BLOCK = 128
 HALF = 64
 QUAD = 4
-STEP = 2
+STEP = 4
 MASKED = -1e30
 EXP2_SCALE = math.log2(math.e) / math.sqrt(HEAD_WIDTH)
 
@@ -63,22 +63,25 @@
     )(*arrays)
 
 
-def prepare_kernel(kv_ref, halo_ref, key_ref, turned_ref):
+def prepare_kernel(kv_ref, halo_hbm, key_ref, turned_ref, halo_ref, sem):
     before = halo_ref.shape[0]
-    key_ref[:before] = halo_ref[:, :HEAD_WIDTH]
-    key_ref[before:] = kv_ref[:, :HEAD_WIDTH]
-
-    def turn_from(source_ref, at):
+    load = pltpu.make_async_copy(halo_hbm, halo_ref, sem)
+    load.start()
+
+    def place(source_ref, at):
+        key_ref[pl.ds(at, source_ref.shape[0]), :] = source_ref[:, :HEAD_WIDTH]
+
         def turn(n, carry):
             first = pl.multiple_of(n * BLOCK, BLOCK)
-            part = source_ref[pl.ds(first, BLOCK), HEAD_WIDTH:].astype(jnp.float32)
-            turned_ref[at + n] = part.T.astype(jnp.bfloat16)
+            part = source_ref[pl.ds(first, BLOCK), HEAD_WIDTH : 2 * HEAD_WIDTH].astype(jnp.float32)
+            turned_ref[at // BLOCK + n] = part.T.astype(jnp.bfloat16)
             return carry
 
         lax.fori_loop(0, source_ref.shape[0] // BLOCK, turn, 0)
 
-    turn_from(halo_ref, 0)
-    turn_from(kv_ref, before // BLOCK)
+    place(kv_ref, before)
+    load.wait()
+    place(halo_ref, 0)
 
 
 def prepare(kv, halo):
@@ -90,25 +93,31 @@
             jax.ShapeDtypeStruct((window, HEAD_WIDTH), kv.dtype),
             jax.ShapeDtypeStruct((window // BLOCK, HEAD_WIDTH, BLOCK), kv.dtype),
         ),
-        in_specs=[vmem, vmem],
+        in_specs=[vmem, pl.BlockSpec(memory_space=pl.ANY)],
         out_specs=(vmem, vmem),
+        scratch_shapes=[pltpu.VMEM(halo.shape, halo.dtype), pltpu.SemaphoreType.DMA(())],
         compiler_params=pltpu.CompilerParams(vmem_limit_bytes=8 << 20),
         name="prepare",
     )(kv, halo)
 
 
-def attend_kernel(
-    lengths, q_ref, key_ref, turned_ref, out_hbm, order_ref, acc_ref, result_ref, sems
-):
-    heads = q_ref.shape[1] // HEAD_WIDTH
+def attend_kernel(lengths, q_ref, key_ref, turned_hbm, *refs, first_lane, part):
+    out_hbm, turned_ref, order_ref, score_ref, top_ref, acc_ref, result_ref, load_sem, sems = refs[-9:]
+    load = pltpu.make_async_copy(turned_hbm, turned_ref, load_sem)
+    load.start()
+    units = result_ref.shape[1]
+    quads = HALF // QUAD
+    heads = units // quads
     rows = heads * BLOCK
     blocks = q_ref.shape[0] // BLOCK
     before = key_ref.shape[0] // BLOCK - blocks
-    quads = HALF // QUAD
+
+    def fold(x, op):
+        return op(x.reshape(BLOCK // 8, 8, rows), axis=0)
 
     def store_of(block):
         return pltpu.make_async_copy(
-            result_ref.at[block + 1], out_hbm.at[:, block], sems.at[block]
+            result_ref.at[block + 1], out_hbm.at[pl.ds(part * units, units), block], sems.at[block]
         )
 
     out_ids = lax.broadcasted_iota(jnp.int32, (BLOCK, BLOCK), 0)
@@ -129,18 +138,21 @@
                 quads, 2 * QUAD, HEAD_WIDTH
             ).astype(jnp.bfloat16)
 
-    def window(block, length, size):
-        finish(block)
-        first = pl.multiple_of((before + block + 1 - size) * BLOCK, BLOCK)
+    sizes = [min(n, before + 1) for n in range(STEP, blocks + STEP, STEP)]
+
+    def first_of(block, size):
+        return pl.multiple_of((before + block + 1 - size) * BLOCK, BLOCK)
+
+    def score(block, length, size):
         row = pl.multiple_of(block * BLOCK, BLOCK)
         q = jnp.concatenate(
             [
-                q_ref[pl.ds(row, BLOCK), h * HEAD_WIDTH : (h + 1) * HEAD_WIDTH]
+                q_ref[pl.ds(row, BLOCK), pl.ds(first_lane + h * HEAD_WIDTH, HEAD_WIDTH)]
                 for h in range(heads)
             ],
             axis=0,
         )
-        keys = key_ref[pl.ds(first, size * BLOCK), :]
+        keys = key_ref[pl.ds(first_of(block, size), size * BLOCK), :]
         s = lax.dot_general(keys, q, (((1,), (1,)), ((), ())), preferred_element_type=jnp.float32)
         pieces = [s[n * BLOCK : (n + 1) * BLOCK] for n in range(size)]
         for n in range(min(STEP, size) - 1):
@@ -148,58 +160,97 @@
         key_ids = lax.broadcasted_iota(jnp.int32, (BLOCK, rows), 0)
         query_ids = lax.broadcasted_iota(jnp.int32, (BLOCK, rows), 1) % BLOCK
         pieces[-1] = jnp.where(key_ids <= query_ids, pieces[-1], MASKED)
-        top = functools.reduce(jnp.maximum, pieces)
-        shift = jnp.max(top, axis=0, keepdims=True) * EXP2_SCALE
-        pieces = [jnp.exp2(piece * EXP2_SCALE - shift) for piece in pieces]
-        total = jnp.sum(functools.reduce(jnp.add, pieces), axis=0, keepdims=True)
+        slot = block % 2
+        for n in range(size):
+            score_ref[slot, n * BLOCK : (n + 1) * BLOCK] = pieces[n]
+        top_ref[slot] = functools.reduce(jnp.maximum, [fold(piece, jnp.max) for piece in pieces])
+
+    def weigh(block, size):
+        slot = block % 2
+        shift = jnp.max(top_ref[slot], axis=0, keepdims=True) * EXP2_SCALE
+        pieces = [
+            jnp.exp2(score_ref[slot, n * BLOCK : (n + 1) * BLOCK] * EXP2_SCALE - shift)
+            for n in range(size)
+        ]
+        total = functools.reduce(jnp.add, [fold(piece, jnp.sum) for piece in pieces])
+        total = jnp.sum(total, axis=0, keepdims=True)
         weights = jnp.concatenate([piece.astype(jnp.bfloat16) for piece in pieces], axis=0)
-        vals = jnp.concatenate(
-            [turned_ref[before + block + 1 - size + n] for n in range(size)], axis=1
-        )
+        at = before + block + 1 - size
+        vals = jnp.concatenate([turned_ref[at + n] for n in range(size)], axis=1)
         out = jnp.dot(vals, weights, preferred_element_type=jnp.float32)
         acc_ref[...] = (out * (1.0 / total)).astype(jnp.bfloat16)
 
+    def fits(length, size):
+        return (length > size - STEP) & (length <= size)
+
+    for size in sizes:
+
+        @pl.when(fits(lengths[0], size))
+        def _():
+            score(0, lengths[0], size)
+
+    load.wait()
+
     def step(block, carry):
         length = lengths[block]
-        for size in range(STEP, blocks + STEP, STEP):
-
-            @pl.when((length > size - STEP) & (length <= size))
-            def _():
-                window(block, length, min(size, before + 1))
-
-        @pl.when(block > 0)
+        earlier = lengths[block - 1]
+        for size in sizes:
+            for earlier_size in sizes:
+
+                @pl.when(fits(length, size) & fits(earlier, earlier_size))
+                def _():
+                    finish(block - 1)
+                    weigh(block - 1, earlier_size)
+                    score(block, length, size)
+
+        @pl.when(block > 1)
         def _():
-            store_of(block - 1).start()
+            store_of(block - 2).start()
 
         return carry
 
-    lax.fori_loop(0, blocks, step, 0)
+    lax.fori_loop(1, blocks, step, 0)
+    finish(blocks - 1)
+    store_of(blocks - 2).start()
+    for size in sizes:
+
+        @pl.when(fits(lengths[blocks - 1], size))
+        def _():
+            weigh(blocks - 1, size)
+
     finish(blocks)
     store_of(blocks - 1).start()
     for block in range(blocks):
         store_of(block).wait()
 
 
-def attend(lengths, q, keys, turned):
+def attend(lengths, q, first_lane, heads, keys, turned, earlier=None):
     blocks = q.shape[0] // BLOCK
-    heads = q.shape[1] // HEAD_WIDTH
     units = HALF // QUAD * heads
+    rows = heads * BLOCK
     vmem = pl.BlockSpec(memory_space=pltpu.VMEM)
+    hbm = pl.BlockSpec(memory_space=pl.ANY)
     tile = (2 * QUAD, HEAD_WIDTH)
-    return pl.pallas_call(
-        attend_kernel,
-        out_shape=jax.ShapeDtypeStruct((units, blocks) + tile, jnp.bfloat16),
-        in_specs=[pl.BlockSpec(memory_space=pltpu.SMEM), vmem, vmem, vmem],
-        out_specs=pl.BlockSpec(memory_space=pl.ANY),
+    chained = earlier is not None
+    return pl.pallas_call(
+        functools.partial(attend_kernel, first_lane=first_lane, part=int(chained)),
+        out_shape=jax.ShapeDtypeStruct((2 * units, blocks) + tile, jnp.bfloat16),
+        in_specs=[pl.BlockSpec(memory_space=pltpu.SMEM), vmem, vmem, hbm] + [hbm] * chained,
+        out_specs=hbm,
         scratch_shapes=[
+            pltpu.VMEM(turned.shape, turned.dtype),
             pltpu.VMEM((BLOCK, BLOCK), jnp.bfloat16),
-            pltpu.VMEM((HEAD_WIDTH, heads * BLOCK), jnp.bfloat16),
+            pltpu.VMEM((2, blocks * BLOCK, rows), jnp.float32),
+            pltpu.VMEM((2, 8, rows), jnp.float32),
+            pltpu.VMEM((HEAD_WIDTH, rows), jnp.bfloat16),
             pltpu.VMEM((blocks + 1, units) + tile, jnp.bfloat16),
+            pltpu.SemaphoreType.DMA(()),
             pltpu.SemaphoreType.DMA((blocks,)),
         ],
+        input_output_aliases={4: 0} if chained else {},
         compiler_params=pltpu.CompilerParams(vmem_limit_bytes=20 << 20),
-        name="attend",
-    )(lengths, q, keys, turned)
+        name="attend_second" if chained else "attend_first",
+    )(lengths, q, keys, turned, *([earlier] if chained else []))
 
 
 def route_kernel(index, x_ref, y_ref):
@@ -269,12 +320,21 @@
         x = lax.all_to_all(x, "head", split_axis=0, concat_axis=0, tiled=True)
         return x.reshape(rows_per_rank, x.shape[2])
 
-    kv = gather_heads(pack((keys, values), ((0, key_width), (0, key_width)), head_count))
+    half_width = query_width // 2
+    firsts = gather_heads(
+        pack(
+            (keys, values, queries),
+            ((0, key_width), (0, key_width), (0, half_width)),
+            head_count,
+        )
+    )
     halo = lax.ppermute(
-        kv[BLOCK:], "ctx", [(i, (i + 1) % ctx_count) for i in range(ctx_count)]
-    )
-    keys, turned = prepare(kv, halo)
-    q = gather_heads(pack((queries,), ((0, query_width),), head_count))
+        firsts[BLOCK:, : 2 * key_width],
+        "ctx",
+        [(i, (i + 1) % ctx_count) for i in range(ctx_count)],
+    )
+    q_second = gather_heads(pack((queries,), ((half_width, half_width),), head_count))
+    keys, turned = prepare(firsts, halo)
 
     own_blocks = rank_index * blocks + jnp.arange(blocks, dtype=jnp.int32)
     holds = (doc_start[None, :] <= own_blocks[:, None]) & (
@@ -291,7 +351,8 @@
         jnp.where(lands, (doc_start - first_new)[None, :], 0), axis=1
     )
 
-    dealt = attend(lengths, q, keys, turned)
+    done = attend(lengths, firsts, 2 * key_width, heads // 2, keys, turned)
+    dealt = attend(lengths, q_second, 0, heads // 2, keys, turned, done)
     dealt = lax.all_to_all(dealt, "ctx", split_axis=0, concat_axis=0, tiled=True)
     dealt = dealt.reshape(ctx_count * blocks, 2 * QUAD, HEAD_WIDTH)
     moved = route(sources, dealt)

time: 201 us -> 205 us (1.020)
  waiting for transfers between devices: 88.9 us -> 84 us
  blocking collectives: 53.3 us -> 57.8 us
  Pallas kernels: 20.7 us -> 23.7 us
  starting transfers between devices: 31.8 us -> 33.9 us
    all_to_all x2, waiting for transfers between devices: 41 us -> 36.2 us  [gather_heads(): x = lax.all_to_all(x, 'head', split_axis=0, concat_axis=0, tiled=True)]
    all_to_all x1, blocking collectives: 53.3 us -> 57.8 us  [on_device(): lax.all_to_all(moved, ('ctx', 'head'), split_axis=0, concat_axis=0, tiled...]
    pallas_call x1 -> x2, Pallas kernels: 10.5 us -> 13.1 us  [attend(): pl.pallas_call(functools.partial(attend_kernel, first_lane=first_lane, pa...]
    ppermute x1, starting transfers between devices: 3.57 us -> 5.73 us  [on_device(): lax.ppermute(firsts[BLOCK:, :2 * key_width], 'ctx', [(i, (i + 1) % ctx_co...]
  transfers between devices with their start and end apart: 4 -> 4, of which waited for: 4 -> 3; matrix products, arithmetic and copies ran while one was open for 1% -> 1% of each run, Pallas kernels for 2% -> 6%
where the time goes in v6:
time: 205 us
  waiting for transfers between devices  84 us (41%)
  blocking collectives  57.8 us (28%)
  starting transfers between devices  33.9 us (17%)
  Pallas kernels  23.7 us (12%)
  local copies, waits for them, and re-layouts  4.91 us (2%)
    all_to_all x1, blocking collectives, on_device(): lax.all_to_all(moved, ('ctx', 'head'), split_axis=0, concat_axis=0, tiled...  57.8 us
    all_to_all x1, waiting for transfers between devices, on_device(): lax.all_to_all(dealt, 'ctx', split_axis=0, concat_axis=0, tiled=True)  39.6 us
    all_to_all x2, waiting for transfers between devices, gather_heads(): x = lax.all_to_all(x, 'head', split_axis=0, concat_axis=0, tiled=True)  36.2 us
    all_to_all x2, starting transfers between devices, gather_heads(): x = lax.all_to_all(x, 'head', split_axis=0, concat_axis=0, tiled=True)  14.4 us
    all_to_all x1, starting transfers between devices, on_device(): lax.all_to_all(dealt, 'ctx', split_axis=0, concat_axis=0, tiled=True)  13.7 us
    pallas_call x2, Pallas kernels, attend(): pl.pallas_call(functools.partial(attend_kernel, first_lane=first_lane, pa...  13.1 us
    ppermute x1, waiting for transfers between devices, on_device(): lax.ppermute(firsts[BLOCK:, :2 * key_width], 'ctx', [(i, (i + 1) % ctx_co...  8.26 us
    ppermute x1, starting transfers between devices, on_device(): lax.ppermute(firsts[BLOCK:, :2 * key_width], 'ctx', [(i, (i + 1) % ctx_co...  5.73 us
  transfers between devices with their start and end apart: 4, of which 3 were waited for; matrix products, arithmetic and copies ran while one was open for 1% of the time, Pallas kernels for 6%

profile of v6, /device:TPU:1, one launch (start us, length us, event | category | flops | bytes accessed | tf_op | source)
XLA Modules:
  0.0 204.9 jit_solution(16880741535773945200)
XLA Ops:
  0.0 2.4 %pack.3 = bf16[8,192,512]{2,1,0:T(8,128)(2,1)} custom-call(bf16[192,1024]{1,0:T(8,128)(2,1)} %refs_0_.3, bf16[192,1024]{1,0:T(8,128)(2,1)} %refs_1_.1, bf16[192,4096]{1,0:T(8,128)(2,1)} %refs_2_.1), custom_call_target="tpu_custom_call" | custom-call | tf_op jit(solution)/shard_map/pack/pallas_call | solution.py:52
  2.5 10.9 %all-to-all-start.1 = ((bf16[8,192,512]{2,1,0:T(8,128)(2,1)}), bf16[8,192,512]{2,1,0:T(8,128)(2,1)S(1)}, u32[]{:S(2)}, u32[]{:S(2)}) async-start(bf16[8,192,512]{2,1,0:T(8,128)(2,1)} %pack.3), calls=%async_computation.1 | async-start | bytes 3145728 | tf_op jit(solution)/shard_map/all_to_all | solution.py:320
  13.3 2.0 pack.2
  15.3 0.0 copy-start.4
  15.4 0.0 copy-start.5
  15.4 0.0 copy-start.6
  15.4 0.0 copy-start.7
  15.4 36.2 %all-to-all-done.1 = bf16[8,192,512]{2,1,0:T(8,128)(2,1)S(1)} async-done(((bf16[8,192,512]{2,1,0:T(8,128)(2,1)}), bf16[8,192,512]{2,1,0:T(8,128)(2,1)S(1)}, u32[]{:S(2)}, u32[]{:S(2)}) %all-to-all-start.1) | async-done | bytes 1572896 | tf_op jit(solution)/shard_map/all_to_all | solution.py:320
  51.6 3.5 %all-to-all-start = ((bf16[8,192,256]{2,1,0:T(8,128)(2,1)}), bf16[8,192,256]{2,1,0:T(8,128)(2,1)S(1)}, u32[]{:S(2)}, u32[]{:S(2)}) async-start(bf16[8,192,256]{2,1,0:T(8,128)(2,1)} %pack.2), calls=%async_computation | async-start | bytes 1572864 | tf_op jit(solution)/shard_map/all_to_all | solution.py:320
  55.2 0.9 slice.4
  56.1 5.7 %collective-permute-start = (bf16[1408,256]{1,0:T(8,128)(2,1)}, bf16[1408,256]{1,0:T(8,128)(2,1)S(1)}, u32[]{:S(2)}, u32[]{:S(2)}) collective-permute-start(bf16[1408,256]{1,0:T(8,128)(2,1)} %slice.4), channel_id=1, source_target_pairs={{0,8},{8,16},{16,24},{24,32},{32,40},{40,48},{48,56},{56,64},{64,7... | collective-permute-start | bytes 2162696 | tf_op jit(solution)/shard_map/ppermute | solution.py:331
  61.8 0.0 copy-done.4
  61.8 0.0 copy-done.5
  61.8 0.0 copy-done.6
  61.8 0.0 copy-done.7
  61.9 0.2 select_reduce_fusion.1
  62.1 8.3 %collective-permute-done.halo_hbm = bf16[1408,256]{1,0:T(8,128)(2,1)S(1)} collective-permute-done((bf16[1408,256]{1,0:T(8,128)(2,1)}, bf16[1408,256]{1,0:T(8,128)(2,1)S(1)}, u32[]{:S(2)}, u32[]{:S(2)}) %collective-permute-start) | collective-permute-done | bytes 720928 | tf_op jit(solution)/shard_map/ppermute | solution.py:331
  70.3 0.9 copy-done.2
  71.2 1.1 copy-done.3
  72.3 2.8 %prepare.1 = (bf16[2944,128]{1,0:T(8,128)(2,1)S(1)}, bf16[23,128,128]{2,1,0:T(8,128)(2,1)S(1)}) custom-call(bf16[1536,512]{1,0:T(8,128)(2,1)S(1)} %bitcast.11, bf16[1408,256]{1,0:T(8,128)(2,1)S(1)} %copy-done.3), custom_call_target="tpu_custom_call" | custom-call | tf_op jit(solution)/shard_map/prepare/pallas_call | solution.py:90
  75.1 6.5 %attend_first.1.refs_0_ = bf16[64,12,8,128]{3,2,1,0:T(8,128)(2,1)} custom-call(s32[12]{0:T(128)S(1)} %add_subtract_fusion.lengths, bf16[1536,512]{1,0:T(8,128)(2,1)S(1)} %bitcast.12, bf16[2944,128]{1,0:T(8,128)(2,1)S(1)} %get-tuple-element.7.key_ref, bf16[23,128,128]{2,1,0:T(8,128)(2,1)S(1)} %get-tuple-element.8.turned_hbm), custom_call_target="tpu_custom_call" | custom-call | tf_op jit(solution)/shard_map/attend_first/pallas_call | solution.py:235
  81.6 0.0 copy-start
  81.6 0.9 copy-done
  82.5 0.0 all-to-all-done
  82.5 1.1 copy-done.1
  83.6 6.5 %attend_second.1 = bf16[64,12,8,128]{3,2,1,0:T(8,128)(2,1)} custom-call(s32[12]{0:T(128)S(1)} %add_subtract_fusion.lengths, bf16[1536,256]{1,0:T(8,128)(2,1)S(1)} %bitcast.16, bf16[2944,128]{1,0:T(8,128)(2,1)S(1)} %get-tuple-element.7.key_ref, bf16[23,128,128]{2,1,0:T(8,128)(2,1)S(1)} %copy-done.1, ...), custom_call_target="tpu_custom_call", output_to_operand_aliasing={{}: (4, {})} | custom-call | tf_op jit(solution)/shard_map/attend_second/pallas_call | solution.py:235
  90.2 13.7 %all-to-all-start.2 = ((bf16[64,12,8,128]{3,2,1,0:T(8,128)(2,1)}), bf16[64,12,8,128]{3,2,1,0:T(8,128)(2,1)S(1)}, u32[]{:S(2)}, u32[]{:S(2)}) async-start(bf16[64,12,8,128]{3,2,1,0:T(8,128)(2,1)} %attend_second.1), calls=%async_computation.2 | async-start | bytes 3145728 | tf_op jit(solution)/shard_map/all_to_all | solution.py:356
  103.9 0.2 select_reduce_fusion
  104.1 39.6 %all-to-all-done.2 = bf16[64,12,8,128]{3,2,1,0:T(8,128)(2,1)S(1)} async-done(((bf16[64,12,8,128]{3,2,1,0:T(8,128)(2,1)}), bf16[64,12,8,128]{3,2,1,0:T(8,128)(2,1)S(1)}, u32[]{:S(2)}, u32[]{:S(2)}) %all-to-all-start.2) | async-done | bytes 1572896 | tf_op jit(solution)/shard_map/all_to_all | solution.py:356
  143.7 1.6 route.1
  145.3 57.8 %all_to_all.20 = bf16[512,3,4,128]{3,2,1,0:T(4,128)(2,1)S(1)} all-to-all(bf16[512,3,4,128]{3,2,1,0:T(4,128)(2,1)S(1)} %bitcast.14), channel_id=1, replica_groups=mesh['ctx'=64,'head'=8] {'ctx','head'}, dimensions={0} | all-to-all | bytes 3145728 | tf_op jit(solution)/shard_map/all_to_all | solution.py:361
  203.1 1.8 settle.1
  (8 shorter events, 0.0 us)
Async XLA Ops:
  2.5 49.1 %all-to-all-start.1 = ((bf16[8,192,512]{2,1,0:T(8,128)(2,1)}), bf16[8,192,512]{2,1,0:T(8,128)(2,1)S(1)}, u32[]{:S(2)}, u32[]{:S(2)}) async-start(bf16[8,192,512]{2,1,0:T(8,128)(2,1)} %pack.3), calls=%async_computation.1 | async-start | bytes 3145728 | tf_op jit(solution)/shard_map/all_to_all | solution.py:320
  15.3 46.5 %copy-start.4 = (s32[256]{0:T(256)S(1)}, s32[256]{0:T(256)}, u32[]{:S(2)}) copy-start(s32[256]{0:T(256)} %param.10) | copy-start | bytes 3076
  15.4 46.5 %copy-start.5 = (s32[256]{0:T(256)S(1)}, s32[256]{0:T(256)}, u32[]{:S(2)}) copy-start(s32[256]{0:T(256)} %param.11) | copy-start | bytes 3076
  15.4 46.5 %copy-start.6 = (s32[256]{0:T(256)S(1)}, s32[256]{0:T(256)}, u32[]{:S(2)}) copy-start(s32[256]{0:T(256)} %param.13) | copy-start | bytes 3076
  15.4 46.5 %copy-start.7 = (s32[256]{0:T(256)S(1)}, s32[256]{0:T(256)}, u32[]{:S(2)}) copy-start(s32[256]{0:T(256)} %param.12) | copy-start | bytes 3076
  51.6 30.9 %all-to-all-start = ((bf16[8,192,256]{2,1,0:T(8,128)(2,1)}), bf16[8,192,256]{2,1,0:T(8,128)(2,1)S(1)}, u32[]{:S(2)}, u32[]{:S(2)}) async-start(bf16[8,192,256]{2,1,0:T(8,128)(2,1)} %pack.2), calls=%async_computation | async-start | bytes 1572864 | tf_op jit(solution)/shard_map/all_to_all | solution.py:320
  56.1 14.3 %collective-permute-start = (bf16[1408,256]{1,0:T(8,128)(2,1)}, bf16[1408,256]{1,0:T(8,128)(2,1)S(1)}, u32[]{:S(2)}, u32[]{:S(2)}) collective-permute-start(bf16[1408,256]{1,0:T(8,128)(2,1)} %slice.4), channel_id=1, source_target_pairs={{0,8},{8,16},{16,24},{24,32},{32,40},{40,48},{48,56},{56,64},{64,7... | collective-permute-start | bytes 2162696 | tf_op jit(solution)/shard_map/ppermute | solution.py:331
  70.3 0.9 copy-start.2
  71.2 1.1 copy-start.3
  81.6 0.9 copy-start
  82.5 1.1 copy-start.1
  90.2 53.5 %all-to-all-start.2 = ((bf16[64,12,8,128]{3,2,1,0:T(8,128)(2,1)}), bf16[64,12,8,128]{3,2,1,0:T(8,128)(2,1)S(1)}, u32[]{:S(2)}, u32[]{:S(2)}) async-start(bf16[64,12,8,128]{3,2,1,0:T(8,128)(2,1)} %attend_second.1), calls=%async_computation.2 | async-start | bytes 3145728 | tf_op jit(solution)/shard_map/all_to_all | solution.py:356

commit v7 on v6

--- a/solution.py
+++ b/solution.py
@@ -13,6 +13,7 @@
 HALF = 64
 QUAD = 4
 STEP = 4
+LEAD_HEADS = 1
 MASKED = -1e30
 EXP2_SCALE = math.log2(math.e) / math.sqrt(HEAD_WIDTH)
 
@@ -101,7 +102,7 @@
     )(kv, halo)
 
 
-def attend_kernel(lengths, q_ref, key_ref, turned_hbm, *refs, first_lane, part):
+def attend_kernel(lengths, q_ref, key_ref, turned_hbm, *refs, first_lane, first_head):
     out_hbm, turned_ref, order_ref, score_ref, top_ref, acc_ref, result_ref, load_sem, sems = refs[-9:]
     load = pltpu.make_async_copy(turned_hbm, turned_ref, load_sem)
     load.start()
@@ -117,7 +118,9 @@
 
     def store_of(block):
         return pltpu.make_async_copy(
-            result_ref.at[block + 1], out_hbm.at[pl.ds(part * units, units), block], sems.at[block]
+            result_ref.at[block + 1],
+            out_hbm.at[pl.ds(first_head * quads, units), block],
+            sems.at[block],
         )
 
     out_ids = lax.broadcasted_iota(jnp.int32, (BLOCK, BLOCK), 0)
@@ -224,7 +227,7 @@
         store_of(block).wait()
 
 
-def attend(lengths, q, first_lane, heads, keys, turned, earlier=None):
+def attend(lengths, q, first_lane, first_head, heads, all_heads, keys, turned, earlier=None):
     blocks = q.shape[0] // BLOCK
     units = HALF // QUAD * heads
     rows = heads * BLOCK
@@ -233,8 +236,8 @@
     tile = (2 * QUAD, HEAD_WIDTH)
     chained = earlier is not None
     return pl.pallas_call(
-        functools.partial(attend_kernel, first_lane=first_lane, part=int(chained)),
-        out_shape=jax.ShapeDtypeStruct((2 * units, blocks) + tile, jnp.bfloat16),
+        functools.partial(attend_kernel, first_lane=first_lane, first_head=first_head),
+        out_shape=jax.ShapeDtypeStruct((HALF // QUAD * all_heads, blocks) + tile, jnp.bfloat16),
         in_specs=[pl.BlockSpec(memory_space=pltpu.SMEM), vmem, vmem, hbm] + [hbm] * chained,
         out_specs=hbm,
         scratch_shapes=[
@@ -320,11 +323,12 @@
         x = lax.all_to_all(x, "head", split_axis=0, concat_axis=0, tiled=True)
         return x.reshape(rows_per_rank, x.shape[2])
 
-    half_width = query_width // 2
+    lead = LEAD_HEADS * HEAD_WIDTH
+    rest = query_width - lead
     firsts = gather_heads(
         pack(
             (keys, values, queries),
-            ((0, key_width), (0, key_width), (0, half_width)),
+            ((0, key_width), (0, key_width), (0, lead)),
             head_count,
         )
     )
@@ -333,7 +337,7 @@
         "ctx",
         [(i, (i + 1) % ctx_count) for i in range(ctx_count)],
     )
-    q_second = gather_heads(pack((queries,), ((half_width, half_width),), head_count))
+    q_second = gather_heads(pack((queries,), ((lead, rest),), head_count))
     keys, turned = prepare(firsts, halo)
 
     own_blocks = rank_index * blocks + jnp.arange(blocks, dtype=jnp.int32)
@@ -351,8 +355,10 @@
         jnp.where(lands, (doc_start - first_new)[None, :], 0), axis=1
     )
 
-    done = attend(lengths, firsts, 2 * key_width, heads // 2, keys, turned)
-    dealt = attend(lengths, q_second, 0, heads // 2, keys, turned, done)
+    done = attend(lengths, firsts, 2 * key_width, 0, LEAD_HEADS, heads, keys, turned)
+    dealt = attend(
+        lengths, q_second, 0, LEAD_HEADS, heads - LEAD_HEADS, heads, keys, turned, done
+    )
     dealt = lax.all_to_all(dealt, "ctx", split_axis=0, concat_axis=0, tiled=True)
     dealt = dealt.reshape(ctx_count * blocks, 2 * QUAD, HEAD_WIDTH)
     moved = route(sources, dealt)

time: 205 us -> 199 us (0.971)
  blocking collectives: 57.8 us -> 53.3 us
  starting transfers between devices: 33.9 us -> 30.6 us
  Pallas kernels: 23.7 us -> 26.3 us
    all_to_all x1, blocking collectives: 57.8 us -> 53.3 us  [on_device(): lax.all_to_all(moved, ('ctx', 'head'), split_axis=0, concat_axis=0, tiled...]
    pallas_call x2, Pallas kernels: 13.1 us -> 15.7 us  [attend(): pl.pallas_call(functools.partial(attend_kernel, first_lane=first_lane, fi...]
    ppermute x1, starting transfers between devices: 5.73 us -> 3.57 us  [on_device(): lax.ppermute(firsts[BLOCK:, :2 * key_width], 'ctx', [(i, (i + 1) % ctx_co...]
  transfers between devices with their start and end apart: 4 -> 4, of which waited for: 3 -> 4; matrix products, arithmetic and copies ran while one was open for 1% -> 1% of each run, Pallas kernels for 6% -> 6%
where the time goes in v7:
time: 199 us; the launch traced here: 198 us
  waiting for transfers between devices  82.4 us (41%)
  blocking collectives  53.3 us (27%)
  starting transfers between devices  30.6 us (15%)
  Pallas kernels  26.3 us (13%)
  local copies, waits for them, and re-layouts  4.92 us (2%)
    all_to_all x1, blocking collectives, on_device(): lax.all_to_all(moved, ('ctx', 'head'), split_axis=0, concat_axis=0, tiled...  53.3 us
    all_to_all x1, waiting for transfers between devices, on_device(): lax.all_to_all(dealt, 'ctx', split_axis=0, concat_axis=0, tiled=True)  39.6 us
    all_to_all x2, waiting for transfers between devices, gather_heads(): x = lax.all_to_all(x, 'head', split_axis=0, concat_axis=0, tiled=True)  34.5 us
    pallas_call x2, Pallas kernels, attend(): pl.pallas_call(functools.partial(attend_kernel, first_lane=first_lane, fi...  15.7 us
    all_to_all x2, starting transfers between devices, gather_heads(): x = lax.all_to_all(x, 'head', split_axis=0, concat_axis=0, tiled=True)  14.4 us
    all_to_all x1, starting transfers between devices, on_device(): lax.all_to_all(dealt, 'ctx', split_axis=0, concat_axis=0, tiled=True)  12.6 us
    ppermute x1, waiting for transfers between devices, on_device(): lax.ppermute(firsts[BLOCK:, :2 * key_width], 'ctx', [(i, (i + 1) % ctx_co...  8.26 us
    pallas_call x2, Pallas kernels, pack(): pl.pallas_call(functools.partial(pack_kernel, pieces=pieces), out_shape=j...  4.38 us
  transfers between devices with their start and end apart: 4, of which 4 were waited for; matrix products, arithmetic and copies ran while one was open for 1% of the time, Pallas kernels for 6%

profile of v7, /device:TPU:1, one launch (start us, length us, event | category | flops | bytes accessed | tf_op | source)
XLA Modules:
  0.0 198.2 jit_solution(3438878661551100109)
XLA Ops:
  0.0 2.2 %pack.3 = bf16[8,192,384]{2,1,0:T(8,128)(2,1)} custom-call(bf16[192,1024]{1,0:T(8,128)(2,1)} %refs_0_.3, bf16[192,1024]{1,0:T(8,128)(2,1)} %refs_1_.1, bf16[192,4096]{1,0:T(8,128)(2,1)} %refs_2_.1), custom_call_target="tpu_custom_call" | custom-call | tf_op jit(solution)/shard_map/pack/pallas_call | solution.py:53
  2.2 10.9 %all-to-all-start.1 = ((bf16[8,192,384]{2,1,0:T(8,128)(2,1)}), bf16[8,192,384]{2,1,0:T(8,128)(2,1)S(1)}, u32[]{:S(2)}, u32[]{:S(2)}) async-start(bf16[8,192,384]{2,1,0:T(8,128)(2,1)} %pack.3), calls=%async_computation.1 | async-start | bytes 2359296 | tf_op jit(solution)/shard_map/all_to_all | solution.py:323
  13.1 2.2 %pack.2 = bf16[8,192,384]{2,1,0:T(8,128)(2,1)} custom-call(bf16[192,4096]{1,0:T(8,128)(2,1)} %refs_2_.1), custom_call_target="tpu_custom_call" | custom-call | tf_op jit(solution)/shard_map/pack/pallas_call | solution.py:53
  15.3 0.0 copy-start.4
  15.3 0.0 copy-start.5
  15.3 0.0 copy-start.6
  15.3 0.0 copy-start.7
  15.3 29.8 %all-to-all-done.1 = bf16[8,192,384]{2,1,0:T(8,128)(2,1)S(1)} async-done(((bf16[8,192,384]{2,1,0:T(8,128)(2,1)}), bf16[8,192,384]{2,1,0:T(8,128)(2,1)S(1)}, u32[]{:S(2)}, u32[]{:S(2)}) %all-to-all-start.1) | async-done | bytes 1179680 | tf_op jit(solution)/shard_map/all_to_all | solution.py:323
  45.1 3.6 %all-to-all-start = ((bf16[8,192,384]{2,1,0:T(8,128)(2,1)}), bf16[8,192,384]{2,1,0:T(8,128)(2,1)S(1)}, u32[]{:S(2)}, u32[]{:S(2)}) async-start(bf16[8,192,384]{2,1,0:T(8,128)(2,1)} %pack.2), calls=%async_computation | async-start | bytes 2359296 | tf_op jit(solution)/shard_map/all_to_all | solution.py:323
  48.7 0.9 slice.4
  49.6 3.6 %collective-permute-start = (bf16[1408,256]{1,0:T(8,128)(2,1)}, bf16[1408,256]{1,0:T(8,128)(2,1)S(1)}, u32[]{:S(2)}, u32[]{:S(2)}) collective-permute-start(bf16[1408,256]{1,0:T(8,128)(2,1)} %slice.4), channel_id=1, source_target_pairs={{0,8},{8,16},{16,24},{24,32},{32,40},{40,48},{48,56},{56,64},{64,7... | collective-permute-start | bytes 2162696 | tf_op jit(solution)/shard_map/ppermute | solution.py:335
  53.2 0.0 copy-done.4
  53.2 0.0 copy-done.5
  53.2 0.0 copy-done.6
  53.3 0.0 copy-done.7
  53.3 0.2 select_reduce_fusion.1
  53.5 8.3 %collective-permute-done.halo_hbm = bf16[1408,256]{1,0:T(8,128)(2,1)S(1)} collective-permute-done((bf16[1408,256]{1,0:T(8,128)(2,1)}, bf16[1408,256]{1,0:T(8,128)(2,1)S(1)}, u32[]{:S(2)}, u32[]{:S(2)}) %collective-permute-start) | collective-permute-done | bytes 720928 | tf_op jit(solution)/shard_map/ppermute | solution.py:335
  61.7 0.9 copy-done.2
  62.6 1.1 copy-done.3
  63.7 2.8 %prepare.1 = (bf16[2944,128]{1,0:T(8,128)(2,1)S(1)}, bf16[23,128,128]{2,1,0:T(8,128)(2,1)S(1)}) custom-call(bf16[1536,384]{1,0:T(8,128)(2,1)S(1)} %bitcast.11, bf16[1408,256]{1,0:T(8,128)(2,1)S(1)} %copy-done.3), custom_call_target="tpu_custom_call" | custom-call | tf_op jit(solution)/shard_map/prepare/pallas_call | solution.py:91
  66.5 6.4 %attend_first.1.refs_0_ = bf16[64,12,8,128]{3,2,1,0:T(8,128)(2,1)} custom-call(s32[12]{0:T(128)S(1)} %add_subtract_fusion.lengths, bf16[1536,384]{1,0:T(8,128)(2,1)S(1)} %bitcast.12, bf16[2944,128]{1,0:T(8,128)(2,1)S(1)} %get-tuple-element.7.key_ref, bf16[23,128,128]{2,1,0:T(8,128)(2,1)S(1)} %get-tuple-element.8.turned_hbm), custom_call_target="tpu_custom_call" | custom-call | tf_op jit(solution)/shard_map/attend_first/pallas_call | solution.py:238
  72.9 0.0 copy-start
  72.9 0.9 copy-done
  73.8 4.7 %all-to-all-done = bf16[8,192,384]{2,1,0:T(8,128)(2,1)S(1)} async-done(((bf16[8,192,384]{2,1,0:T(8,128)(2,1)}), bf16[8,192,384]{2,1,0:T(8,128)(2,1)S(1)}, u32[]{:S(2)}, u32[]{:S(2)}) %all-to-all-start) | async-done | bytes 1179680 | tf_op jit(solution)/shard_map/all_to_all | solution.py:323
  78.5 1.1 copy-done.1
  79.6 9.4 %attend_second.1 = bf16[64,12,8,128]{3,2,1,0:T(8,128)(2,1)} custom-call(s32[12]{0:T(128)S(1)} %add_subtract_fusion.lengths, bf16[1536,384]{1,0:T(8,128)(2,1)S(1)} %bitcast.16, bf16[2944,128]{1,0:T(8,128)(2,1)S(1)} %get-tuple-element.7.key_ref, bf16[23,128,128]{2,1,0:T(8,128)(2,1)S(1)} %copy-done.1, ...), custom_call_target="tpu_custom_call", output_to_operand_aliasing={{}: (4, {})} | custom-call | tf_op jit(solution)/shard_map/attend_second/pallas_call | solution.py:238
  89.0 12.6 %all-to-all-start.2 = ((bf16[64,12,8,128]{3,2,1,0:T(8,128)(2,1)}), bf16[64,12,8,128]{3,2,1,0:T(8,128)(2,1)S(1)}, u32[]{:S(2)}, u32[]{:S(2)}) async-start(bf16[64,12,8,128]{3,2,1,0:T(8,128)(2,1)} %attend_second.1), calls=%async_computation.2 | async-start | bytes 3145728 | tf_op jit(solution)/shard_map/all_to_all | solution.py:362
  101.6 0.2 select_reduce_fusion
  101.8 39.6 %all-to-all-done.2 = bf16[64,12,8,128]{3,2,1,0:T(8,128)(2,1)S(1)} async-done(((bf16[64,12,8,128]{3,2,1,0:T(8,128)(2,1)}), bf16[64,12,8,128]{3,2,1,0:T(8,128)(2,1)S(1)}, u32[]{:S(2)}, u32[]{:S(2)}) %all-to-all-start.2) | async-done | bytes 1572896 | tf_op jit(solution)/shard_map/all_to_all | solution.py:362
  141.4 1.6 route.1
  143.0 53.3 %all_to_all.20 = bf16[512,3,4,128]{3,2,1,0:T(4,128)(2,1)S(1)} all-to-all(bf16[512,3,4,128]{3,2,1,0:T(4,128)(2,1)S(1)} %bitcast.14), channel_id=1, replica_groups=mesh['ctx'=64,'head'=8] {'ctx','head'}, dimensions={0} | all-to-all | bytes 3145728 | tf_op jit(solution)/shard_map/all_to_all | solution.py:367
  196.3 1.8 settle.1
  (8 shorter events, 0.0 us)
Async XLA Ops:
  2.2 42.9 %all-to-all-start.1 = ((bf16[8,192,384]{2,1,0:T(8,128)(2,1)}), bf16[8,192,384]{2,1,0:T(8,128)(2,1)S(1)}, u32[]{:S(2)}, u32[]{:S(2)}) async-start(bf16[8,192,384]{2,1,0:T(8,128)(2,1)} %pack.3), calls=%async_computation.1 | async-start | bytes 2359296 | tf_op jit(solution)/shard_map/all_to_all | solution.py:323
  15.3 37.9 %copy-start.4 = (s32[256]{0:T(256)S(1)}, s32[256]{0:T(256)}, u32[]{:S(2)}) copy-start(s32[256]{0:T(256)} %param.10) | copy-start | bytes 3076
  15.3 37.9 %copy-start.5 = (s32[256]{0:T(256)S(1)}, s32[256]{0:T(256)}, u32[]{:S(2)}) copy-start(s32[256]{0:T(256)} %param.11) | copy-start | bytes 3076
  15.3 37.9 %copy-start.6 = (s32[256]{0:T(256)S(1)}, s32[256]{0:T(256)}, u32[]{:S(2)}) copy-start(s32[256]{0:T(256)} %param.13) | copy-start | bytes 3076
  15.3 37.9 %copy-start.7 = (s32[256]{0:T(256)S(1)}, s32[256]{0:T(256)}, u32[]{:S(2)}) copy-start(s32[256]{0:T(256)} %param.12) | copy-start | bytes 3076
  45.1 33.3 %all-to-all-start = ((bf16[8,192,384]{2,1,0:T(8,128)(2,1)}), bf16[8,192,384]{2,1,0:T(8,128)(2,1)S(1)}, u32[]{:S(2)}, u32[]{:S(2)}) async-start(bf16[8,192,384]{2,1,0:T(8,128)(2,1)} %pack.2), calls=%async_computation | async-start | bytes 2359296 | tf_op jit(solution)/shard_map/all_to_all | solution.py:323
  49.6 12.1 %collective-permute-start = (bf16[1408,256]{1,0:T(8,128)(2,1)}, bf16[1408,256]{1,0:T(8,128)(2,1)S(1)}, u32[]{:S(2)}, u32[]{:S(2)}) collective-permute-start(bf16[1408,256]{1,0:T(8,128)(2,1)} %slice.4), channel_id=1, source_target_pairs={{0,8},{8,16},{16,24},{24,32},{32,40},{40,48},{48,56},{56,64},{64,7... | collective-permute-start | bytes 2162696 | tf_op jit(solution)/shard_map/ppermute | solution.py:335
  61.7 0.9 copy-start.2
  62.6 1.1 copy-start.3
  72.9 0.9 copy-start
  78.5 1.1 copy-start.1
  89.0 52.4 %all-to-all-start.2 = ((bf16[64,12,8,128]{3,2,1,0:T(8,128)(2,1)}), bf16[64,12,8,128]{3,2,1,0:T(8,128)(2,1)S(1)}, u32[]{:S(2)}, u32[]{:S(2)}) async-start(bf16[64,12,8,128]{3,2,1,0:T(8,128)(2,1)} %attend_second.1), calls=%async_computation.2 | async-start | bytes 3145728 | tf_op jit(solution)/shard_map/all_to_all | solution.py:362

commit v8 on v7

--- a/solution.py
+++ b/solution.py
@@ -12,7 +12,7 @@
 BLOCK = 128
 HALF = 64
 QUAD = 4
-STEP = 4
+STEP = 3
 LEAD_HEADS = 1
 MASKED = -1e30
 EXP2_SCALE = math.log2(math.e) / math.sqrt(HEAD_WIDTH)

time: 199 us -> 198 us (level)
  no operation moved by 1% of the time
where the time goes in v8:
time: 198 us
  waiting for transfers between devices  82.4 us (42%)
  blocking collectives  53.4 us (27%)
  starting transfers between devices  31.1 us (16%)
  Pallas kernels  25.4 us (13%)
  local copies, waits for them, and re-layouts  4.92 us (2%)
    all_to_all x1, blocking collectives, on_device(): lax.all_to_all(moved, ('ctx', 'head'), split_axis=0, concat_axis=0, tiled...  53.4 us
    all_to_all x1, waiting for transfers between devices, on_device(): lax.all_to_all(dealt, 'ctx', split_axis=0, concat_axis=0, tiled=True)  39.6 us
    all_to_all x2, waiting for transfers between devices, gather_heads(): x = lax.all_to_all(x, 'head', split_axis=0, concat_axis=0, tiled=True)  34.6 us
    pallas_call x2, Pallas kernels, attend(): pl.pallas_call(functools.partial(attend_kernel, first_lane=first_lane, fi...  14.8 us
    all_to_all x2, starting transfers between devices, gather_heads(): x = lax.all_to_all(x, 'head', split_axis=0, concat_axis=0, tiled=True)  14.4 us
    all_to_all x1, starting transfers between devices, on_device(): lax.all_to_all(dealt, 'ctx', split_axis=0, concat_axis=0, tiled=True)  13.1 us
    ppermute x1, waiting for transfers between devices, on_device(): lax.ppermute(firsts[BLOCK:, :2 * key_width], 'ctx', [(i, (i + 1) % ctx_co...  8.26 us
    pallas_call x2, Pallas kernels, pack(): pl.pallas_call(functools.partial(pack_kernel, pieces=pieces), out_shape=j...  4.38 us
  transfers between devices with their start and end apart: 4, of which 4 were waited for; matrix products, arithmetic and copies ran while one was open for 1% of the time, Pallas kernels for 6%

profile of v8, /device:TPU:1, one launch (start us, length us, event | category | flops | bytes accessed | tf_op | source)
XLA Modules:
  0.0 197.8 jit_solution(15655856131698276671)
XLA Ops:
  0.0 2.2 %pack.3 = bf16[8,192,384]{2,1,0:T(8,128)(2,1)} custom-call(bf16[192,1024]{1,0:T(8,128)(2,1)} %refs_0_.3, bf16[192,1024]{1,0:T(8,128)(2,1)} %refs_1_.1, bf16[192,4096]{1,0:T(8,128)(2,1)} %refs_2_.1), custom_call_target="tpu_custom_call" | custom-call | tf_op jit(solution)/shard_map/pack/pallas_call | solution.py:53
  2.2 10.9 %all-to-all-start.1 = ((bf16[8,192,384]{2,1,0:T(8,128)(2,1)}), bf16[8,192,384]{2,1,0:T(8,128)(2,1)S(1)}, u32[]{:S(2)}, u32[]{:S(2)}) async-start(bf16[8,192,384]{2,1,0:T(8,128)(2,1)} %pack.3), calls=%async_computation.1 | async-start | bytes 2359296 | tf_op jit(solution)/shard_map/all_to_all | solution.py:323
  13.1 2.2 %pack.2 = bf16[8,192,384]{2,1,0:T(8,128)(2,1)} custom-call(bf16[192,4096]{1,0:T(8,128)(2,1)} %refs_2_.1), custom_call_target="tpu_custom_call" | custom-call | tf_op jit(solution)/shard_map/pack/pallas_call | solution.py:53
  15.3 0.0 copy-start.4
  15.3 0.0 copy-start.5
  15.3 0.0 copy-start.6
  15.3 0.0 copy-start.7
  15.3 29.8 %all-to-all-done.1 = bf16[8,192,384]{2,1,0:T(8,128)(2,1)S(1)} async-done(((bf16[8,192,384]{2,1,0:T(8,128)(2,1)}), bf16[8,192,384]{2,1,0:T(8,128)(2,1)S(1)}, u32[]{:S(2)}, u32[]{:S(2)}) %all-to-all-start.1) | async-done | bytes 1179680 | tf_op jit(solution)/shard_map/all_to_all | solution.py:323
  45.1 3.6 %all-to-all-start = ((bf16[8,192,384]{2,1,0:T(8,128)(2,1)}), bf16[8,192,384]{2,1,0:T(8,128)(2,1)S(1)}, u32[]{:S(2)}, u32[]{:S(2)}) async-start(bf16[8,192,384]{2,1,0:T(8,128)(2,1)} %pack.2), calls=%async_computation | async-start | bytes 2359296 | tf_op jit(solution)/shard_map/all_to_all | solution.py:323
  48.7 0.9 slice.4
  49.6 3.6 %collective-permute-start = (bf16[1408,256]{1,0:T(8,128)(2,1)}, bf16[1408,256]{1,0:T(8,128)(2,1)S(1)}, u32[]{:S(2)}, u32[]{:S(2)}) collective-permute-start(bf16[1408,256]{1,0:T(8,128)(2,1)} %slice.4), channel_id=1, source_target_pairs={{0,8},{8,16},{16,24},{24,32},{32,40},{40,48},{48,56},{56,64},{64,7... | collective-permute-start | bytes 2162696 | tf_op jit(solution)/shard_map/ppermute | solution.py:335
  53.2 0.0 copy-done.4
  53.2 0.0 copy-done.5
  53.2 0.0 copy-done.6
  53.3 0.0 copy-done.7
  53.3 0.2 select_reduce_fusion.1
  53.5 8.3 %collective-permute-done.halo_hbm = bf16[1408,256]{1,0:T(8,128)(2,1)S(1)} collective-permute-done((bf16[1408,256]{1,0:T(8,128)(2,1)}, bf16[1408,256]{1,0:T(8,128)(2,1)S(1)}, u32[]{:S(2)}, u32[]{:S(2)}) %collective-permute-start) | collective-permute-done | bytes 720928 | tf_op jit(solution)/shard_map/ppermute | solution.py:335
  61.7 0.9 copy-done.2
  62.6 1.1 copy-done.3
  63.7 2.8 %prepare.1 = (bf16[2944,128]{1,0:T(8,128)(2,1)S(1)}, bf16[23,128,128]{2,1,0:T(8,128)(2,1)S(1)}) custom-call(bf16[1536,384]{1,0:T(8,128)(2,1)S(1)} %bitcast.11, bf16[1408,256]{1,0:T(8,128)(2,1)S(1)} %copy-done.3), custom_call_target="tpu_custom_call" | custom-call | tf_op jit(solution)/shard_map/prepare/pallas_call | solution.py:91
  66.5 6.3 %attend_first.1.refs_0_ = bf16[64,12,8,128]{3,2,1,0:T(8,128)(2,1)} custom-call(s32[12]{0:T(128)S(1)} %add_subtract_fusion.lengths, bf16[1536,384]{1,0:T(8,128)(2,1)S(1)} %bitcast.12, bf16[2944,128]{1,0:T(8,128)(2,1)S(1)} %get-tuple-element.7.key_ref, bf16[23,128,128]{2,1,0:T(8,128)(2,1)S(1)} %get-tuple-element.8.turned_hbm), custom_call_target="tpu_custom_call" | custom-call | tf_op jit(solution)/shard_map/attend_first/pallas_call | solution.py:238
  72.8 0.0 copy-start
  72.8 0.9 copy-done
  73.7 4.7 %all-to-all-done = bf16[8,192,384]{2,1,0:T(8,128)(2,1)S(1)} async-done(((bf16[8,192,384]{2,1,0:T(8,128)(2,1)}), bf16[8,192,384]{2,1,0:T(8,128)(2,1)S(1)}, u32[]{:S(2)}, u32[]{:S(2)}) %all-to-all-start) | async-done | bytes 1179680 | tf_op jit(solution)/shard_map/all_to_all | solution.py:323
  78.5 1.1 copy-done.1
  79.6 8.4 %attend_second.1 = bf16[64,12,8,128]{3,2,1,0:T(8,128)(2,1)} custom-call(s32[12]{0:T(128)S(1)} %add_subtract_fusion.lengths, bf16[1536,384]{1,0:T(8,128)(2,1)S(1)} %bitcast.16, bf16[2944,128]{1,0:T(8,128)(2,1)S(1)} %get-tuple-element.7.key_ref, bf16[23,128,128]{2,1,0:T(8,128)(2,1)S(1)} %copy-done.1, ...), custom_call_target="tpu_custom_call", output_to_operand_aliasing={{}: (4, {})} | custom-call | tf_op jit(solution)/shard_map/attend_second/pallas_call | solution.py:238
  88.1 13.1 %all-to-all-start.2 = ((bf16[64,12,8,128]{3,2,1,0:T(8,128)(2,1)}), bf16[64,12,8,128]{3,2,1,0:T(8,128)(2,1)S(1)}, u32[]{:S(2)}, u32[]{:S(2)}) async-start(bf16[64,12,8,128]{3,2,1,0:T(8,128)(2,1)} %attend_second.1), calls=%async_computation.2 | async-start | bytes 3145728 | tf_op jit(solution)/shard_map/all_to_all | solution.py:362
  101.2 0.2 select_reduce_fusion
  101.4 39.6 %all-to-all-done.2 = bf16[64,12,8,128]{3,2,1,0:T(8,128)(2,1)S(1)} async-done(((bf16[64,12,8,128]{3,2,1,0:T(8,128)(2,1)}), bf16[64,12,8,128]{3,2,1,0:T(8,128)(2,1)S(1)}, u32[]{:S(2)}, u32[]{:S(2)}) %all-to-all-start.2) | async-done | bytes 1572896 | tf_op jit(solution)/shard_map/all_to_all | solution.py:362
  141.0 1.6 route.1
  142.6 53.4 %all_to_all.20 = bf16[512,3,4,128]{3,2,1,0:T(4,128)(2,1)S(1)} all-to-all(bf16[512,3,4,128]{3,2,1,0:T(4,128)(2,1)S(1)} %bitcast.14), channel_id=1, replica_groups=mesh['ctx'=64,'head'=8] {'ctx','head'}, dimensions={0} | all-to-all | bytes 3145728 | tf_op jit(solution)/shard_map/all_to_all | solution.py:367
  196.0 1.8 settle.1
  (8 shorter events, 0.0 us)
Async XLA Ops:
  2.2 42.9 %all-to-all-start.1 = ((bf16[8,192,384]{2,1,0:T(8,128)(2,1)}), bf16[8,192,384]{2,1,0:T(8,128)(2,1)S(1)}, u32[]{:S(2)}, u32[]{:S(2)}) async-start(bf16[8,192,384]{2,1,0:T(8,128)(2,1)} %pack.3), calls=%async_computation.1 | async-start | bytes 2359296 | tf_op jit(solution)/shard_map/all_to_all | solution.py:323
  15.3 37.9 %copy-start.4 = (s32[256]{0:T(256)S(1)}, s32[256]{0:T(256)}, u32[]{:S(2)}) copy-start(s32[256]{0:T(256)} %param.10) | copy-start | bytes 3076
  15.3 37.9 %copy-start.5 = (s32[256]{0:T(256)S(1)}, s32[256]{0:T(256)}, u32[]{:S(2)}) copy-start(s32[256]{0:T(256)} %param.11) | copy-start | bytes 3076
  15.3 37.9 %copy-start.6 = (s32[256]{0:T(256)S(1)}, s32[256]{0:T(256)}, u32[]{:S(2)}) copy-start(s32[256]{0:T(256)} %param.13) | copy-start | bytes 3076
  15.3 37.9 %copy-start.7 = (s32[256]{0:T(256)S(1)}, s32[256]{0:T(256)}, u32[]{:S(2)}) copy-start(s32[256]{0:T(256)} %param.12) | copy-start | bytes 3076
  45.1 33.3 %all-to-all-start = ((bf16[8,192,384]{2,1,0:T(8,128)(2,1)}), bf16[8,192,384]{2,1,0:T(8,128)(2,1)S(1)}, u32[]{:S(2)}, u32[]{:S(2)}) async-start(bf16[8,192,384]{2,1,0:T(8,128)(2,1)} %pack.2), calls=%async_computation | async-start | bytes 2359296 | tf_op jit(solution)/shard_map/all_to_all | solution.py:323
  49.6 12.1 %collective-permute-start = (bf16[1408,256]{1,0:T(8,128)(2,1)}, bf16[1408,256]{1,0:T(8,128)(2,1)S(1)}, u32[]{:S(2)}, u32[]{:S(2)}) collective-permute-start(bf16[1408,256]{1,0:T(8,128)(2,1)} %slice.4), channel_id=1, source_target_pairs={{0,8},{8,16},{16,24},{24,32},{32,40},{40,48},{48,56},{56,64},{64,7... | collective-permute-start | bytes 2162696 | tf_op jit(solution)/shard_map/ppermute | solution.py:335
  61.7 0.9 copy-start.2
  62.6 1.1 copy-start.3
  72.8 0.9 copy-start
  78.5 1.1 copy-start.1
  88.1 52.9 %all-to-all-start.2 = ((bf16[64,12,8,128]{3,2,1,0:T(8,128)(2,1)}), bf16[64,12,8,128]{3,2,1,0:T(8,128)(2,1)S(1)}, u32[]{:S(2)}, u32[]{:S(2)}) async-start(bf16[64,12,8,128]{3,2,1,0:T(8,128)(2,1)} %attend_second.1), calls=%async_computation.2 | async-start | bytes 3145728 | tf_op jit(solution)/shard_map/all_to_all | solution.py:362
